TPU v7x, 32 devices: a whole 2x2x4 slice. The times are simulated.
32 devices in a mesh: dp: 8 (over y, x, core), ctx: 4 (over z).
Axes of the slice: x: 2, y: 2, z: 4, core: 2. Of those that a mesh axis runs over, the one named last changes fastest.
Arguments:
- tokens: bfloat16 [16, 256, 1024], P('dp', 'ctx'), may hold values from -6 to 6
- out_grad: bfloat16 [16, 256, 1024], P('dp', 'ctx'), may hold values from -6 to 6
- lengths: int32 [16], P('dp'), may hold values from 64 to 256, as said below
- w_qkv: bfloat16 [1024, 3072], replicated, may hold values from -0.1875 to 0.1875
- w_out: bfloat16 [1024, 1024], replicated, may hold values from -3 to 3
- w_in: bfloat16 [1024, 4096], replicated, may hold values from -0.1875 to 0.1875
- w_fc2: bfloat16 [4096, 1024], replicated, may hold values from -0.09375 to 0.09375
- vectors: float32 [12, 1024], replicated, may hold values from -0.15 to 1.3
- moment_one: float32 [32, 393600], P(('dp', 'ctx')), may hold values from -6 to 6
- moment_two: float32 [32, 393600], P(('dp', 'ctx')), may hold values from 1 to 100
Outputs:
- out: bfloat16 [16, 256, 1024], P('dp', 'ctx')
- tokens_grad: bfloat16 [16, 256, 1024], P('dp', 'ctx')
- grad_rows: float32 [32, 393600], P(('dp', 'ctx'))
- new_params: float32 [32, 393600], P(('dp', 'ctx'))
- new_one: float32 [32, 393600], P(('dp', 'ctx'))
- new_two: float32 [32, 393600], P(('dp', 'ctx'))
Inputs may be any that keep to these rules, and one draw needn't show every extreme that they name: `lengths`: each slot holds one sequence starting at its first position; in every draw one slot is full and one holds 64 positions.
All inputs are finite; a program needn't handle non-finite values.
Results may differ from a plain program's by a relative error of at most 0.015.
Values may be sent and summed in bfloat16 or wider, within the bound.
A program may use at most 320 MiB of HBM per device.

v0:
```python
from functools import partial

import jax
import jax.numpy as jnp
from jax import lax
from jax.sharding import PartitionSpec as P

D = 1024
H = 16
HD = 64
FF = 4096


EPSILON = 1e-05
learn_rate = 0.01
beta_one = 0.9
beta_two = 0.999
adam_eps = 1e-08
decay_rate = 0.01
step_count = 10.0


def layer_norm(values, gain, shift):
    center = values - jnp.mean(values, axis=-1, keepdims=True)
    spread = jnp.mean(center * center, axis=-1, keepdims=True)
    return center * lax.rsqrt(spread + EPSILON) * gain + shift


def split_vectors(vectors):
    ratio = FF // D
    return (
        vectors[0],
        vectors[1],
        vectors[2],
        vectors[3 : 3 + ratio].reshape(FF),
        vectors[3 + ratio],
        vectors[4 + ratio],
        vectors[5 + ratio],
        vectors[6 + ratio],
        vectors[7 + ratio],
    )


def inner(left, right):
    return lax.dot_general(
        left, right, (((0,), (0,)), ((), ())), preferred_element_type=jnp.float32
    )


def through(left, weight):
    return lax.dot_general(
        left, weight, (((1,), (1,)), ((), ())), preferred_element_type=jnp.float32
    )


def run_slots(function, items):
    return lax.map(lambda item: function(*item), items)


def heads_block():
    return 4


def split_heads(matrix):
    count = matrix.shape[0]
    group = heads_block()
    return jnp.moveaxis(matrix.reshape(count, H // group, group, HD), 1, 0)


def join_heads(blocked):
    return jnp.moveaxis(blocked, 0, 1).reshape(blocked.shape[1], H * HD)


def split_stats(stats):
    group = heads_block()
    return stats.reshape(H // group, group, stats.shape[-1])


def shard_piece(left, right, number, shard_count):
    weight_rows = left.shape[1]
    columns = right.shape[1]
    per_shard = weight_rows * columns // shard_count
    block = inner(left, right).reshape(-1)
    return block.reshape(number, per_shard)


def project(flat_tokens, w_qkv, vectors):
    joined = jnp.dot(flat_tokens, w_qkv, preferred_element_type=jnp.float32)
    queries = ((joined[:, :D] + vectors[0]) * 0.125).astype(jnp.bfloat16)
    keys = joined[:, D : 2 * D].astype(jnp.bfloat16)
    values = (joined[:, 2 * D :] + vectors[1]).astype(jnp.bfloat16)
    return (queries, keys, values)


def attend_slot(queries, keys, values, live):
    rows = queries.shape[0]

    def attend_one_block(item):
        query_heads, key_heads, value_heads = item
        scores = jnp.einsum(
            "qhd,khd->hqk", query_heads, key_heads, preferred_element_type=jnp.float32
        )
        scores = jnp.where(live[None, None, :], scores, -1e30)
        maximum = jnp.max(scores, axis=-1, keepdims=True)
        expo = jnp.exp(scores - maximum)
        total = jnp.sum(expo, axis=-1, keepdims=True)
        probs_low = (expo / total).astype(jnp.bfloat16)
        mixed = jnp.einsum(
            "hqk,khd->qhd", probs_low, value_heads, preferred_element_type=jnp.float32
        )
        return (mixed, (maximum + jnp.log(total))[..., 0])

    mixed, log_total = lax.map(
        attend_one_block, (split_heads(queries), split_heads(keys), split_heads(values))
    )
    return (join_heads(mixed), log_total.reshape(H, rows))


def query_back(queries, keys, values, live, log_total, grad_mixed, with_keys):
    rows = queries.shape[0]

    def query_one_block(item):
        query_heads, key_heads, value_heads, grad_heads, block_log = item
        scores = jnp.einsum(
            "qhd,khd->hqk", query_heads, key_heads, preferred_element_type=jnp.float32
        )
        scores = jnp.where(live[None, None, :], scores, -1e30)
        probs = jnp.exp(scores - block_log[:, :, None])
        grad_probs = jnp.einsum(
            "qhd,khd->hqk", grad_heads, value_heads, preferred_element_type=jnp.float32
        )
        row_sums = jnp.sum(probs * grad_probs, axis=-1)
        grad_scores = (probs * (grad_probs - row_sums[:, :, None])).astype(jnp.bfloat16)
        grad_query = jnp.einsum(
            "hqk,khd->qhd", grad_scores, key_heads, preferred_element_type=jnp.float32
        )
        grad_key = jnp.einsum(
            "hqk,qhd->khd", grad_scores, query_heads, preferred_element_type=jnp.float32
        )
        grad_value = jnp.einsum(
            "hqk,qhd->khd",
            probs.astype(jnp.bfloat16),
            grad_heads,
            preferred_element_type=jnp.float32,
        )
        return (grad_query, row_sums, grad_key, grad_value)

    items = (
        split_heads(queries),
        split_heads(keys),
        split_heads(values),
        split_heads(grad_mixed),
        split_stats(log_total),
    )
    results = lax.map(query_one_block, items)
    grad_query, row_sums, grad_key, grad_value = results
    return (
        join_heads(grad_query),
        row_sums.reshape(H, rows),
        join_heads(grad_key),
        join_heads(grad_value),
    )


def tail(flat_tokens, mixed, w_out, w_in, w_fc2, vectors):
    bias_q, bias_v, bias_o, bias_in, bias_fc2, gain_one, shift_one, gain_two, shift_two = (
        split_vectors(vectors)
    )
    mixed_low = mixed.astype(jnp.bfloat16)
    summed_one = (
        flat_tokens.astype(jnp.float32)
        + jnp.dot(mixed_low, w_out, preferred_element_type=jnp.float32)
        + bias_o
    )
    normed = layer_norm(summed_one, gain_one, shift_one)
    normed_low = normed.astype(jnp.bfloat16)
    hidden_pre = jnp.dot(normed_low, w_in, preferred_element_type=jnp.float32) + bias_in
    hidden_low = jax.nn.gelu(hidden_pre, approximate=False).astype(jnp.bfloat16)
    summed_two = normed + jnp.dot(hidden_low, w_fc2, preferred_element_type=jnp.float32) + bias_fc2
    result = layer_norm(summed_two, gain_two, shift_two)
    return (mixed_low, summed_one, normed_low, hidden_pre, hidden_low, summed_two, result)


def body(tokens, out_grad, lengths, w_qkv, w_out, w_in, w_fc2, vectors, moment_one, moment_two):
    slots, piece, width = tokens.shape
    length = piece * lax.axis_size("ctx")
    local_pos = lax.axis_index("ctx") * piece + jnp.arange(piece, dtype=jnp.int32)
    own_live = local_pos[None, :] < lengths[:, None]
    valid = own_live.astype(jnp.float32)
    key_live = jnp.arange(length, dtype=jnp.int32)[None, :] < lengths[:, None]
    bias_q, bias_v, bias_o, bias_in, bias_fc2, gain_one, shift_one, gain_two, shift_two = (
        split_vectors(vectors)
    )
    flat_tokens = tokens.reshape(slots * piece, width)
    queries, keys, values = project(flat_tokens, w_qkv, vectors)
    keys_all, values_all = (
        lax.all_gather(keys.reshape(slots, piece, width), "ctx", axis=1, tiled=True),
        lax.all_gather(values.reshape(slots, piece, width), "ctx", axis=1, tiled=True),
    )
    mixed, log_total = run_slots(
        attend_slot, (queries.reshape(slots, piece, width), keys_all, values_all, key_live)
    )
    saved = tail(flat_tokens, mixed.reshape(slots * piece, width), w_out, w_in, w_fc2, vectors)
    out = (saved[6].reshape(slots, piece, width) * valid[..., None]).astype(jnp.bfloat16)
    again = lax.optimization_barrier(flat_tokens)
    queries, keys, values = project(again, w_qkv, vectors)
    keys_all, values_all = (
        lax.all_gather(keys.reshape(slots, piece, width), "ctx", axis=1, tiled=True),
        lax.all_gather(values.reshape(slots, piece, width), "ctx", axis=1, tiled=True),
    )
    mixed, log_total = run_slots(
        attend_slot, (queries.reshape(slots, piece, width), keys_all, values_all, key_live)
    )
    saved = tail(again, mixed.reshape(slots * piece, width), w_out, w_in, w_fc2, vectors)
    mixed_low, summed_one, normed_low, hidden_pre, hidden_low, summed_two, result = saved
    cotangent = (out_grad.astype(jnp.float32) * valid[..., None]).reshape(slots * piece, width)
    unused_two, norm_two_back = jax.vjp(layer_norm, summed_two, gain_two, shift_two)
    grad_two, grad_gain_two, grad_shift_two = norm_two_back(cotangent)
    grad_fc2_low = grad_two.astype(jnp.bfloat16)
    bias_fc2_grad = jnp.sum(grad_fc2_low.astype(jnp.float32), axis=0)
    grad_hidden = through(grad_fc2_low, w_fc2)
    unused_gelu, gelu_back = jax.vjp(partial(jax.nn.gelu, approximate=False), hidden_pre)
    grad_pre_low = gelu_back(grad_hidden)[0].astype(jnp.bfloat16)
    bias_in_grad = jnp.sum(grad_pre_low.astype(jnp.float32), axis=0)
    grad_normed = grad_two + through(grad_pre_low, w_in)
    unused_one, norm_one_back = jax.vjp(layer_norm, summed_one, gain_one, shift_one)
    grad_one, grad_gain_one, grad_shift_one = norm_one_back(grad_normed)
    grad_branch_low = grad_one.astype(jnp.bfloat16)
    bias_out_grad = jnp.sum(grad_branch_low.astype(jnp.float32), axis=0)
    grad_mixed_low = (
        through(grad_branch_low, w_out).astype(jnp.bfloat16).reshape(slots, piece, width)
    )
    queries_slots = queries.reshape(slots, piece, width)
    grad_query, row_sums, grad_key, grad_value = run_slots(
        partial(query_back, with_keys=True),
        (queries_slots, keys_all, values_all, key_live, log_total, grad_mixed_low),
    )
    grad_key, grad_value = (
        lax.psum_scatter(
            grad_key.astype(jnp.bfloat16), "ctx", scatter_dimension=1, tiled=True
        ).astype(jnp.float32),
        lax.psum_scatter(
            grad_value.astype(jnp.bfloat16), "ctx", scatter_dimension=1, tiled=True
        ).astype(jnp.float32),
    )
    rows = slots * piece
    grad_query_low = grad_query.reshape(rows, width).astype(jnp.bfloat16) * jnp.bfloat16(0.125)
    grad_key_low = grad_key.reshape(rows, width).astype(jnp.bfloat16)
    grad_value_low = grad_value.reshape(rows, width).astype(jnp.bfloat16)
    grad_joined = jnp.concatenate([grad_query_low, grad_key_low, grad_value_low], axis=1)
    bias_q_grad = jnp.sum(grad_query_low.astype(jnp.float32), axis=0)
    bias_v_grad = jnp.sum(grad_value_low.astype(jnp.float32), axis=0)
    tokens_grad = (
        (grad_one + through(grad_joined, w_qkv)).reshape(slots, piece, width).astype(jnp.bfloat16)
    )
    vector_grad = jnp.concatenate(
        [
            bias_q_grad[None],
            bias_v_grad[None],
            bias_out_grad[None],
            bias_in_grad.reshape(FF // D, D),
            bias_fc2_grad[None],
            grad_gain_one[None],
            grad_shift_one[None],
            grad_gain_two[None],
            grad_shift_two[None],
        ],
        axis=0,
    )
    count = lax.axis_size(("dp", "ctx"))
    vector_rows = vector_grad.reshape(count, -1)
    pairs = (
        (flat_tokens, grad_joined),
        (mixed_low, grad_branch_low),
        (normed_low, grad_pre_low),
        (hidden_low, grad_fc2_low),
    )
    blocks = [
        shard_piece(left, right, 1 * lax.axis_size(("dp", "ctx")), count) for left, right in pairs
    ]
    blocks.append(vector_rows)
    grad_rows = lax.psum_scatter(
        jnp.concatenate(blocks, axis=1), ("dp", "ctx"), scatter_dimension=0, tiled=True
    )
    index = lax.axis_index(("dp", "ctx"))
    params = jnp.concatenate(
        [
            lax.dynamic_slice_in_dim(weight.reshape(count, -1), index, 1, 0).astype(jnp.float32)
            for weight in (w_qkv, w_out, w_in, w_fc2, vectors)
        ],
        axis=1,
    )
    new_one = beta_one * moment_one + (1.0 - beta_one) * grad_rows
    new_two = beta_two * moment_two + (1.0 - beta_two) * grad_rows * grad_rows
    fix_one = 1.0 - beta_one**step_count
    fix_two = 1.0 - beta_two**step_count
    update = new_one / fix_one / (jnp.sqrt(new_two / fix_two) + adam_eps)
    new_params = params - learn_rate * (update + decay_rate * params)
    return (out, tokens_grad, grad_rows, new_params, new_one, new_two)


def solution(mesh):
    placed = (
        P("dp", "ctx", None),
        P("dp", "ctx", None),
        P("dp"),
        P(),
        P(),
        P(),
        P(),
        P(),
        P(("dp", "ctx"), None),
        P(("dp", "ctx"), None),
    )
    return jax.shard_map(
        body,
        mesh=mesh,
        in_specs=placed,
        out_specs=(
            P("dp", "ctx", None),
            P("dp", "ctx", None),
            P(("dp", "ctx"), None),
            P(("dp", "ctx"), None),
            P(("dp", "ctx"), None),
            P(("dp", "ctx"), None),
        ),
        check_vma=False,
    )
```

profile of v0, /device:TPU:0, one launch (start us, length us, event | category | flops | bytes accessed | tf_op | source)
XLA Modules:
  0.0 1130.9 jit_solution(5506732546149771107)
XLA Ops:
  30.1 16.7 %all-gather.7.cloned.1.call-done = bf16[2,256,1024]{2,0,1:T(2,128)(2,1)} async-done(((bf16[2,64,1024]{2,0,1:T(2,128)(2,1)}), bf16[2,256,1024]{2,0,1:T(2,128)(2,1)}) %all-gather.7.cloned.1.call-update) | async-done | bytes 1048592 | tf_op jit(solution)/shard_map/all_gather | solution.py:198
  50.4 25.3 %all-gather.5.cloned.1.call-done = bf16[2,256,1024]{2,0,1:T(2,128)(2,1)} async-done(((bf16[2,64,1024]{2,0,1:T(2,128)(2,1)}), bf16[2,256,1024]{2,0,1:T(2,128)(2,1)}) %all-gather.5.cloned.1.call-update) | async-done | bytes 1048592 | tf_op jit(solution)/shard_map/all_gather | solution.py:197
  80.1 31.1 %while.73 = (s32[]{:T(128)}, bf16[2,64,1024]{2,1,0:T(8,128)(2,1)}, bf16[2,64,1024]{2,1,0:T(8,128)(2,1)}, bf16[2,256,1024]{1,2,0:T(8,128)(2,1)}, bf16[2,256,1024]...) while((s32[]{:T(128)}, bf16[2,64,1024]{2,1,0:T(8,128)(2,1)}, ...), condition=%wide.region_5.6_spmd, body=%wide.region_0.5_spmd.sunk | while | flops 25625344 | bytes 4659458 | solution.py:57
  83.5 10.5 while.78
  98.9 10.5 while.78
  115.3 12.0 %fusion.167 = (f32[128]{0:T(128)S(1)}, f32[128,1024]{1,0:T(8,128)}) fusion(f32[1024]{0:T(1024)S(1)} %bitcast.355, bf16[4096,1024]{1,0:T(8,128)(2,1)} %param.28, bf16[1024,4096]{1,0:T(8,128)(2,1)} %param.27, f32[4096]{0:T(1024)S(1)} %bitcast.353, f32[128,1024]{1,0:T(8,128)S(1)} %get-tuple-element.479, f32[1024]{0:T(1024)S(1)} %bitcast.334, ...), kind=kOutput, calls=%fused_computation.286 | convolution fusion | flops 2183659520 | bytes 17856000 | tf_op jit(solution)/shard_map/dot_general | solution.py:179
  136.7 27.3 %while.75 = (s32[]{:T(128)}, bf16[2,64,1024]{2,1,0:T(8,128)(2,1)}, f32[2,16,64]{2,1,0:T(8,128)}, bf16[2,64,1024]{2,1,0:T(8,128)(2,1)}, bf16[2,256,1024]{1,2,0:T(...) while((s32[]{:T(128)}, bf16[2,64,1024]{2,1,0:T(8,128)(2,1)}, ...), condition=%wide.region_15.16_spmd, body=%wide.region_10.15_spmd.sunk | while | flops 17235712 | bytes 4483354 | solution.py:57
  138.8 9.3 while.79
  152.4 9.3 while.79
  166.7 9.8 multiply_convert_fusion.1
  195.2 52.0 %while.77 = (s32[]{:T(128)}, bf16[2,64,1024]{2,1,0:T(8,128)(2,1)}, bf16[2,256,1024]{2,1,0:T(8,128)(2,1)}, bf16[2,256,1024]{2,1,0:T(8,128)(2,1)}, bf16[2,64,1024]...) while((s32[]{:T(128)}, bf16[2,64,1024]{2,1,0:T(8,128)(2,1)}, ...), condition=%wide.region_28.29_spmd, body=%wide.region_24.28_spmd.sunk | while | flops 42467072 | bytes 21775396 | solution.py:57
  198.9 16.9 %while.80 = (s32[]{:T(128)}, bf16[4,64,4,64]{1,3,2,0:T(8,128)(2,1)}, bf16[4,256,4,64]{1,3,2,0:T(8,128)(2,1)}, bf16[4,256,4,64]{1,3,2,0:T(8,128)(2,1)}, bf16[4,25...) while((s32[]{:T(128)}, ...), condition=%wide.region_27.27_spmd, body=%wide.region_25.26_spmd.sunk | while | flops 42467072 | bytes 11804405 | solution.py:155
  225.0 16.9 %while.80 = (s32[]{:T(128)}, bf16[4,64,4,64]{1,3,2,0:T(8,128)(2,1)}, bf16[4,256,4,64]{1,3,2,0:T(8,128)(2,1)}, bf16[4,256,4,64]{1,3,2,0:T(8,128)(2,1)}, bf16[4,25...) while((s32[]{:T(128)}, ...), condition=%wide.region_27.27_spmd, body=%wide.region_25.26_spmd.sunk | while | flops 42467072 | bytes 11804405 | solution.py:155
  254.5 9.4 reshape.372
  263.8 8.9 reshape.373
  280.6 8.2 fusion.152
  288.8 12.3 %reshape_reshape.14 = f32[32,131072]{1,0:T(8,128)} reshape(f32[1024,4096]{1,0:T(8,128)} %fusion.152) | data formatting | bytes 33554432 | tf_op jit(solution)/shard_map/reshape;reshape | solution.py:84
  309.2 12.2 %reshape_reshape.15 = f32[32,131072]{1,0:T(8,128)} reshape(f32[4096,1024]{1,0:T(8,128)} %fusion.173) | data formatting | bytes 33554432 | tf_op jit(solution)/shard_map/reshape;reshape | solution.py:84
  329.0 12.6 %copy.59 = f32[1024,3072]{1,0:T(8,128)} copy(f32[1024,3072]{0,1:T(8,128)} %convolution_bitcast_fusion.5) | data formatting | bytes 25165824 | tf_op jit(solution)/shard_map/dot_general | solution.py:45
  341.6 10.0 reshape_reshape.12
  351.7 10.0 constant_dynamic-update-slice_fusion.9
  366.6 13.2 %constant_dynamic-update-slice_fusion.7 = f32[32,393600]{1,0:T(8,128)} fusion(f32[32,393600]{1,0:T(8,128)} %constant_dynamic-update-slice_fusion.8, f32[32,131072]{1,0:T(8,128)} %reshape_reshape.14), kind=kLoop, calls=%fused_computation.221 | loop fusion | bytes 33554432
  399.9 710.0 %all-reduce.3.cloned.1.call-done = f32[32,393600]{1,0:T(8,128)} async-done(((f32[32,393600]{1,0:T(8,128)}), f32[32,393600]{1,0:T(8,128)}) %all-reduce.3.cloned.1.call-update) | async-done | bytes 50380816
  1109.9 14.0 %multiply_subtract_fusion = (f32[1,393600]{1,0:T(1,128)}, f32[1,393600]{1,0:T(1,128)}, f32[1,393600]{1,0:T(1,128)}, f32[1,393600]{1,0:T(1,128)}) fusion(f32[1,393600]{1,0:T(1,128)S(1)} %constant_dynamic-update-slice_fusion.10, f32[1,393600]{1,0:T(1,128)} %param.30, f32[1,393600]{1,0:T(1,128)} %param.31, f32[32,393600]{1,0:T(8,128)} %all-reduce.3.cloned.1.call-done, ...), kind=kLoop, calls=%fused_computation.126 | loop fusion | flops 5904000 | bytes 12595204 | tf_op jit(solution)/shard_map/sub | solution.py:298
  (463 shorter events, 230.2 us)
Async XLA Ops:
  7.2 39.6 %all-gather.7.cloned.1.call-start = ((), (), s32[]{:S(2)}) async-start(), calls=%async_computation.3 | async-start | bytes 1310720 | tf_op jit(solution)/shard_map/all_gather | solution.py:198
  15.9 59.8 %all-gather.5.cloned.1.call-start = ((), (), s32[]{:S(2)}) async-start(), calls=%async_computation.2 | async-start | bytes 1310720 | tf_op jit(solution)/shard_map/all_gather | solution.py:197
  17.0 95.9 %all-gather.11.cloned.1.call-start = ((), (), s32[]{:S(2)}) async-start(), calls=%async_computation.5 | async-start | bytes 1310720 | tf_op jit(solution)/shard_map/all_gather | solution.py:209
  19.0 114.6 %all-gather.9.cloned.1.call-start = ((), (), s32[]{:S(2)}) async-start(), calls=%async_computation.4 | async-start | bytes 1310720 | tf_op jit(solution)/shard_map/all_gather | solution.py:208
  20.1 301.6 %reduce-scatter.3.cloned.1.call-start = ((), (), s32[]{:S(2)}) async-start(), calls=%async_computation.6 | async-start | bytes 1310720 | tf_op jit(solution)/shard_map/reduce_scatter | solution.py:239
  28.6 50.8 %copy-start.41 = (f32[2,64]{1,0:T(2,128)}, f32[2,64]{1,0:T(2,128)S(1)}, u32[]{:S(2)}) copy-start(f32[2,64]{1,0:T(2,128)S(1)} %compare_convert_fusion) | copy-start | bytes 1540
  80.1 31.1 %copy-start.1 = (bf16[1024,1024]{1,0:T(8,128)(2,1)S(1)}, bf16[1024,1024]{1,0:T(8,128)(2,1)}, u32[]{:S(2)}) copy-start(bf16[1024,1024]{1,0:T(8,128)(2,1)} %param.26) | copy-start | bytes 6291460
  164.1 12.5 %slice-start.4 = ((s8[8388608]{0:T(1024)(128)(4,1)}), s8[4194304]{0:T(1024)(128)(4,1)S(1)}, s32[]{:S(2)}) async-start(s8[8388608]{0:T(1024)(128)(4,1)} %bitcast.291), calls=%async_computation.13 | async-start | bytes 8388608
  166.4 24.7 %copy-start.3 = (f32[128,1024]{1,0:T(8,128)}, f32[128,1024]{1,0:T(8,128)S(1)}, u32[]{:S(2)}) copy-start(f32[128,1024]{1,0:T(8,128)S(1)} %get-tuple-element.474) | copy-start | bytes 1572868
  166.7 24.5 %copy-start.39 = (f32[128]{0:T(128)}, f32[128]{0:T(128)S(1)}, u32[]{:S(2)}) copy-start(f32[128]{0:T(128)S(1)} %fusion.118) | copy-start | bytes 1540
  247.2 74.4 %reduce-scatter.5.cloned.1.call-start = ((), (), s32[]{:S(2)}) async-start(), calls=%async_computation.7 | async-start | bytes 1310720 | tf_op jit(solution)/shard_map/reduce_scatter | solution.py:242
  253.2 856.6 %all-reduce.3.cloned.1.call-start = ((), (), s32[]{:S(2)}) async-start(), calls=%async_computation.8 | async-start | bytes 100761600
  288.8 12.3 %copy-start.12 = (bf16[128,4096]{1,0:T(8,128)(2,1)S(1)}, bf16[128,4096]{1,0:T(8,128)(2,1)}, u32[]{:S(2)}) copy-start(bf16[128,4096]{1,0:T(8,128)(2,1)} %copy-done.11) | copy-start | bytes 3145732
  288.8 12.3 %copy-start.25 = (bf16[128,1024]{1,0:T(8,128)(2,1)S(1)}, bf16[128,1024]{1,0:T(8,128)(2,1)}, u32[]{:S(2)}) copy-start(bf16[128,1024]{1,0:T(8,128)(2,1)} %copy-done.24) | copy-start | bytes 786436
  309.2 12.3 %copy-start.38 = (f32[4096]{0:T(1024)S(1)}, f32[4096]{0:T(1024)}, u32[]{:S(2)}) copy-start(f32[4096]{0:T(1024)} %get-tuple-element.432) | copy-start | bytes 49156
  309.2 12.3 %copy-start.28 = (bf16[2,64,1024]{2,1,0:T(8,128)(2,1)S(1)}, bf16[2,64,1024]{2,1,0:T(8,128)(2,1)}, u32[]{:S(2)}) copy-start(bf16[2,64,1024]{2,1,0:T(8,128)(2,1)} %get-tuple-element.257) | copy-start | bytes 786436
  309.2 12.4 %copy-start.10 = (bf16[2,64,1024]{2,1,0:T(8,128)(2,1)S(1)}, bf16[2,64,1024]{2,1,0:T(8,128)(2,1)}, u32[]{:S(2)}) copy-start(bf16[2,64,1024]{2,1,0:T(8,128)(2,1)} %param.22) | copy-start | bytes 786436
  351.6 10.1 copy-start.32
  351.6 10.1 copy-start.33
  351.6 10.1 copy-start.34
  361.9 17.9 %slice-start = ((s8[16777216]{0:T(1024)(128)(4,1)}), s8[4194304]{0:T(1024)(128)(4,1)S(1)}, s32[]{:S(2)}) async-start(s8[16777216]{0:T(1024)(128)(4,1)} %bitcast.287), calls=%async_computation.9 | async-start | bytes 8388608
  366.6 13.2 %slice-start.1 = ((s8[16777216]{0:T(1024)(128)(4,1)}), s8[4194304]{0:T(1024)(128)(4,1)S(1)}, s32[]{:S(2)}) async-start(s8[16777216]{0:T(1024)(128)(4,1)} %bitcast.287), calls=%async_computation.10 | async-start | bytes 8388608
  366.6 14.0 %slice-start.2 = ((s8[16777216]{0:T(1024)(128)(4,1)}), s8[4194304]{0:T(1024)(128)(4,1)S(1)}, s32[]{:S(2)}) async-start(s8[16777216]{0:T(1024)(128)(4,1)} %bitcast.287), calls=%async_computation.11 | async-start | bytes 8388608
  366.6 15.3 %slice-start.3 = ((s8[16777216]{0:T(1024)(128)(4,1)}), s8[4194304]{0:T(1024)(128)(4,1)S(1)}, s32[]{:S(2)}) async-start(s8[16777216]{0:T(1024)(128)(4,1)} %bitcast.287), calls=%async_computation.12 | async-start | bytes 8388608
  (67 other events, 232.5 us)
Sparse Core Ops, SparseCore 0:
  16.0 30.6 all-gather.6
  48.3 27.3 all-gather.4
  77.3 27.4 all-gather.10
  106.2 27.3 all-gather.8
  247.4 26.6 reduce-scatter.2
  276.8 25.7 reduce-scatter.4
  388.7 721.0 all-reduce.2
where the time goes:
time: 1140 us; the launch traced here: 1130 us
  waiting for transfers between devices  758 us (66%)
  local copies, waits for them, and re-layouts  197 us (17%)
  matrix products  127 us (11%)
  other arithmetic  31.5 us (3%)
  between operations  14.9 us (1%)
    unnamed x8, waiting for transfers between devices  710 us
    another operation x4, local copies, waits for them, and re-layouts, shard_piece(): return block.reshape(number, per_shard)  39.6 us
    unnamed x102, local copies, waits for them, and re-layouts  38.4 us
    all_gather x2, waiting for transfers between devices, body(): lax.all_gather(keys.reshape(slots, piece, width), 'ctx', axis=1, tiled=True)  31.6 us
    dot_general x16, matrix products, attend_one_block(): jnp.einsum('hqk,khd->qhd', probs_low, value_heads, preferred_element_type...  31.1 us
    reshape x5, local copies, waits for them, and re-layouts, body(): weight.reshape(count, -1)  29.9 us
    dot_general x4, matrix products, inner(): lax.dot_general(left, right, (((0,), (0,)), ((), ())), preferred_element_...  26.3 us
  transfers between devices with their start and end apart: 7, of which 4 were waited for; matrix products, arithmetic and copies ran while one was open for 14% of the time, Pallas kernels for 0%

commit v1 on v0

--- a/solution.py
+++ b/solution.py
@@ -3,6 +3,8 @@
 import jax
 import jax.numpy as jnp
 from jax import lax
+from jax.experimental import pallas as pl
+from jax.experimental.pallas import tpu as pltpu
 from jax.sharding import PartitionSpec as P
 
 D = 1024
@@ -299,6 +301,719 @@
     return (out, tokens_grad, grad_rows, new_params, new_one, new_two)
 
 
+BF16 = jnp.bfloat16
+F32 = jnp.float32
+
+
+def layer_norm_stats(values):
+    center = values - jnp.mean(values, axis=-1, keepdims=True)
+    spread = jnp.mean(center * center, axis=-1, keepdims=True)
+    return center, lax.rsqrt(spread + EPSILON)
+
+
+def layer_norm_back(center, scale, gain, cotangent):
+    scaled = cotangent * gain
+    mean_scaled = jnp.mean(scaled, axis=-1, keepdims=True)
+    mean_cross = jnp.mean(scaled * center, axis=-1, keepdims=True)
+    return scale * (scaled - mean_scaled - center * (scale * scale) * mean_cross)
+
+
+def normal_cdf(values):
+    return 0.5 * (1.0 + lax.erf(values * 0.7071067811865476))
+
+
+def dot(left, right):
+    return jnp.dot(left, right, preferred_element_type=F32)
+
+
+def positions(axis, shape, slot, piece):
+    place = lax.broadcasted_iota(jnp.int32, shape, axis)
+    block = lax.div(place, piece)
+    half = lax.div(block, 2)
+    step = lax.rem(block, 2)
+    return (2 * half + lax.rem(slot + step, 2)) * piece + lax.rem(place, piece)
+
+
+def head_probs(queries, keys, live):
+    scores = through(queries, keys)
+    scores = jnp.where(live, scores, -1e30)
+    expo = jnp.exp(scores - jnp.max(scores, axis=-1, keepdims=True))
+    return expo / jnp.sum(expo, axis=-1, keepdims=True)
+
+
+def full(shape):
+    return pl.BlockSpec(shape, lambda i, *s: (0,) * len(shape))
+
+
+def call(kernel, scalars, grid, ins, outs, scratch=(), flops=0, moved=0, name=None):
+    arrays, in_specs = zip(*ins)
+    shapes, out_specs = zip(*outs)
+    return pl.pallas_call(
+        kernel,
+        out_shape=shapes,
+        grid_spec=pltpu.PrefetchScalarGridSpec(
+            num_scalar_prefetch=1,
+            grid=(grid,),
+            in_specs=list(in_specs),
+            out_specs=list(out_specs),
+            scratch_shapes=list(scratch),
+        ),
+        compiler_params=pltpu.CompilerParams(
+            dimension_semantics=("arbitrary",), vmem_limit_bytes=60 * 1024 * 1024
+        ),
+        cost_estimate=pl.CostEstimate(flops=flops, bytes_accessed=moved, transcendentals=0),
+        name=name,
+    )(scalars, *arrays)
+
+
+def attention_kernel(piece, sc, own, other, wq, wk, wv, wo, vec, rows_out, saved_out, part_out):
+    core, slot, length = sc[0], sc[1], sc[2]
+    half = own.shape[0]
+
+    @pl.when(pl.program_id(0) == 0)
+    def _():
+        rows_out[pl.ds(pl.multiple_of(core * half, half), half), :] = own[...]
+        rows_out[pl.ds(pl.multiple_of((1 - core) * half, half), half), :] = other[...]
+        part_out[...] = jnp.zeros_like(part_out)
+
+    rows = rows_out[...]
+    queries = ((dot(rows, wq[...]) + vec[0:1, :]) * 0.125).astype(BF16)
+    keys = dot(rows, wk[...]).astype(BF16)
+    values = (dot(rows, wv[...]) + vec[1:2, :]).astype(BF16)
+    width = queries.shape[1]
+    live = positions(1, (1, 2 * half), slot, piece) < length
+    lane = lax.broadcasted_iota(jnp.int32, (1, width), 1)
+    mixed = jnp.zeros(queries.shape, F32)
+    for head in range(width // HD):
+        mine = lax.div(lane, HD) == head
+        probs = head_probs(jnp.where(mine, queries, jnp.zeros_like(queries)), keys, live)
+        mixed = jnp.where(mine, dot(probs.astype(BF16), values), mixed)
+    mixed_low = mixed.astype(BF16)
+    saved_out[0, :, 0:width] = queries
+    saved_out[0, :, width : 2 * width] = keys
+    saved_out[0, :, 2 * width : 3 * width] = values
+    saved_out[0, :, 3 * width : 4 * width] = mixed_low
+    part_out[...] += dot(mixed_low, wo[...])
+
+
+def feed_kernel(sc, rows, part, peer, vec, bias, w_up, w_down, sum_out, low_out, own_out, pre_out, part_out):
+    core = sc[0]
+    length, half = rows.shape[0], own_out.shape[0]
+
+    @pl.when(pl.program_id(0) == 0)
+    def _():
+        @pl.loop(0, length // 32)
+        def _(chunk):
+            at = pl.ds(pl.multiple_of(chunk * 32, 32), 32)
+            summed = rows[at, :].astype(F32) + (part[at, :] + peer[at, :]) + vec[2:3, :]
+            center, scale = layer_norm_stats(summed)
+            sum_out[at, :] = summed
+            low_out[at, :] = (center * scale * vec[8:9, :] + vec[9:10, :]).astype(BF16)
+
+        own_out[...] = low_out[pl.ds(pl.multiple_of(core * half, half), half), :]
+        part_out[...] = jnp.zeros_like(part_out)
+
+    pre = dot(low_out[...], w_up[...]) + bias[...]
+    pre_out[...] = pre
+    part_out[...] += dot((pre * normal_cdf(pre)).astype(BF16), w_down[...])
+
+
+def feed_back_kernel(
+    piece, sc, summed, part, peer, grad_own, grad_other, vec, pre, w_up, w_down,
+    result_out, low_out, own_out, grad_out, vec_out, part_out, cot,
+):
+    core, slot, length = sc[0], sc[1], sc[2]
+    rows, half = summed.shape[0], grad_own.shape[0]
+
+    @pl.when(pl.program_id(0) == 0)
+    def _():
+        cot[pl.ds(pl.multiple_of(core * half, half), half), :] = grad_own[...]
+        cot[pl.ds(pl.multiple_of((1 - core) * half, half), half), :] = grad_other[...]
+        vec_out[...] = jnp.zeros_like(vec_out)
+
+        @pl.loop(0, rows // 32)
+        def _(chunk):
+            start = pl.multiple_of(chunk * 32, 32)
+            at = pl.ds(start, 32)
+            center, scale = layer_norm_stats(summed[at, :])
+            normed = center * scale * vec[8:9, :] + vec[9:10, :]
+            center, scale = layer_norm_stats(normed + (part[at, :] + peer[at, :]) + vec[7:8, :])
+            place = start + lax.broadcasted_iota(jnp.int32, (32, 1), 0)
+            block = lax.div(place, piece)
+            spot = 2 * lax.div(block, 2) + lax.rem(slot + lax.rem(block, 2), 2)
+            valid = (spot * piece + lax.rem(place, piece) < length).astype(F32)
+            unit = center * scale
+            low_out[at, :] = (valid * (unit * vec[10:11, :] + vec[11:12, :])).astype(BF16)
+            error = cot[at, :].astype(F32) * valid
+            grad = layer_norm_back(center, scale, vec[10:11, :], error)
+            grad_out[at, :] = grad
+            grad_low = grad.astype(BF16).astype(F32)
+            vec_out[0:1, :] += jnp.sum(grad_low, axis=0, keepdims=True)
+            vec_out[1:2, :] += jnp.sum(error * unit, axis=0, keepdims=True)
+            vec_out[2:3, :] += jnp.sum(error, axis=0, keepdims=True)
+
+        result_out[...] = low_out[pl.ds(pl.multiple_of(core * half, half), half), :]
+        low_out[...] = grad_out[...].astype(BF16)
+        own_out[...] = low_out[pl.ds(pl.multiple_of(core * half, half), half), :]
+        part_out[...] = jnp.zeros_like(part_out)
+
+    value = pre[...]
+    slope = normal_cdf(value) + value * (jnp.exp(-0.5 * value * value) * 0.3989422804014327)
+    grad_pre = (through(low_out[...], w_down[...]) * slope).astype(BF16)
+    part_out[...] += through(grad_pre, w_up[...])
+
+
+def attention_back_kernel(
+    piece, parts, sc, summed, grad_two, part, peer, vec, wo, saved, wq, wk, wv, *rest
+):
+    outs, (low_out, own_out, vec_out, side_out, keep_out, send_out, acc) = (
+        rest[:parts],
+        rest[parts:],
+    )
+    core, slot, length = sc[0], sc[1], sc[2]
+    step = pl.program_id(0)
+    rows, half = summed.shape[0], own_out.shape[0]
+    mine_at = pl.ds(pl.multiple_of(core * half, half), half)
+    other_at = pl.ds(pl.multiple_of((1 - core) * half, half), half)
+
+    @pl.when(step == 0)
+    def _():
+        vec_out[...] = jnp.zeros_like(vec_out)
+
+        @pl.loop(0, rows // 32)
+        def _(chunk):
+            at = pl.ds(pl.multiple_of(chunk * 32, 32), 32)
+            center, scale = layer_norm_stats(summed[at, :])
+            error = grad_two[at, :] + (part[at, :] + peer[at, :])
+            grad = layer_norm_back(center, scale, vec[8:9, :], error)
+            acc[at, :] = grad
+            low = grad.astype(BF16)
+            low_out[at, :] = low
+            vec_out[0:1, :] += jnp.sum(low.astype(F32), axis=0, keepdims=True)
+            vec_out[1:2, :] += jnp.sum(error * (center * scale), axis=0, keepdims=True)
+            vec_out[2:3, :] += jnp.sum(error, axis=0, keepdims=True)
+
+        own_out[...] = low_out[mine_at, :]
+        acc[other_at, :] = jnp.zeros((half, acc.shape[1]), F32)
+
+    width = wo.shape[0]
+    grad_mixed = through(low_out[...], wo[...]).astype(BF16)
+    queries = saved[0, :, 0:width]
+    keys = saved[0, :, width : 2 * width]
+    values = saved[0, :, 2 * width : 3 * width]
+    live = positions(1, (1, rows), slot, piece) < length
+    lane = lax.broadcasted_iota(jnp.int32, (1, width), 1)
+    grad_q = jnp.zeros((rows, width), F32)
+    grad_k = grad_q
+    grad_v = grad_q
+    for head in range(width // HD):
+        mine = lax.div(lane, HD) == head
+        probs = head_probs(jnp.where(mine, queries, jnp.zeros_like(queries)), keys, live)
+        grad_probs = through(jnp.where(mine, grad_mixed, jnp.zeros_like(grad_mixed)), values)
+        dsum = jnp.sum(probs * grad_probs, axis=-1, keepdims=True)
+        grad_scores = (probs * (grad_probs - dsum)).astype(BF16)
+        grad_q = jnp.where(mine, dot(grad_scores, keys), grad_q)
+        grad_k = jnp.where(mine, inner(grad_scores, queries), grad_k)
+        grad_v = jnp.where(mine, inner(probs.astype(BF16), grad_mixed), grad_v)
+    grad_q = grad_q.astype(BF16) * jnp.bfloat16(0.125)
+    grad_k = grad_k.astype(BF16)
+    grad_v = grad_v.astype(BF16)
+    side_out[0, 0:1, :] = jnp.sum(grad_q.astype(F32), axis=0, keepdims=True)
+    side_out[0, 1:2, :] = jnp.sum(grad_v.astype(F32), axis=0, keepdims=True)
+    for number in range(parts):
+
+        @pl.when(step == number)
+        def _(out=outs[number]):
+            out[:, 0:width] = grad_q
+            out[:, width : 2 * width] = grad_k
+            out[:, 2 * width : 3 * width] = grad_v
+            out[:, 3 * width : 4 * width] = saved[0, :, 3 * width : 4 * width]
+
+    acc[...] += through(grad_q, wq[...]) + through(grad_k, wk[...]) + through(grad_v, wv[...])
+
+    @pl.when(step == parts - 1)
+    def _():
+        keep_out[...] = acc[mine_at, :]
+        send_out[...] = acc[other_at, :]
+
+
+def gather_rows(sc, dest, own, mine, theirs):
+    core = sc[0]
+    length = own.shape[0]
+    half = length // 2
+    dest[0:length, :] = own[...]
+    for number, (one, two) in enumerate(zip(mine, theirs)):
+        base = (number + 1) * length
+        dest[pl.ds(pl.multiple_of(base + core * half, half), half), :] = one[...]
+        dest[pl.ds(pl.multiple_of(base + (1 - core) * half, half), half), :] = two[...]
+
+
+def feed_grad_kernel(others, lines, sc, *refs):
+    size = 1 + 2 * others
+    left = refs[:size]
+    right = refs[size : 2 * size]
+    w_up, w_down, bias, out, bias_out, lefts, rights, hidden, grads = refs[2 * size :]
+    gather_rows(sc, lefts, left[0], left[1 : 1 + others], left[1 + others :])
+    gather_rows(sc, rights, right[0], right[1 : 1 + others], right[1 + others :])
+    total = lefts.shape[0]
+    bias_out[...] = jnp.zeros_like(bias_out)
+
+    @pl.loop(0, total // 256)
+    def _(chunk):
+        at = pl.ds(pl.multiple_of(chunk * 256, 256), 256)
+        pre = dot(lefts[at, :], w_up[...]) + bias[...]
+        cdf = normal_cdf(pre)
+        slope = cdf + pre * (jnp.exp(-0.5 * pre * pre) * 0.3989422804014327)
+        hidden[at, :] = (pre * cdf).astype(BF16)
+        low = (through(rights[at, :], w_down[...]) * slope).astype(BF16)
+        grads[at, :] = low
+        bias_out[...] += jnp.sum(low.astype(F32), axis=0, keepdims=True)
+
+    count = out.shape[0]
+    chunk_down = out.shape[1] // 2
+    down = inner(hidden[...], rights[...]).astype(BF16)
+    for number in range(count):
+        out[number, 0:chunk_down, :] = down[number * chunk_down : (number + 1) * chunk_down, :]
+    columns = grads.shape[1]
+    packs = out.shape[2] // columns
+    groups = lefts.shape[1] // (lines * count)
+    per_pack = groups // packs
+    for group in range(groups):
+        start = group * lines * count
+        up = inner(lefts[:, start : start + lines * count], grads[...]).astype(BF16)
+        row = chunk_down + (group % per_pack) * lines
+        col = (group // per_pack) * columns
+        for number in range(count):
+            out[number, row : row + lines, col : col + columns] = up[
+                number * lines : (number + 1) * lines, :
+            ]
+
+
+def input_grad_kernel(others, lines, sc, *refs):
+    size = 1 + 2 * others
+    left = refs[:size]
+    right = refs[size : 2 * size]
+    joined = refs[2 * size : 2 * size + 1 + others]
+    out, lefts, rights, joint = refs[2 * size + 1 + others :]
+    gather_rows(sc, lefts, left[0], left[1 : 1 + others], left[1 + others :])
+    gather_rows(sc, rights, right[0], right[1 : 1 + others], right[1 + others :])
+    length = joined[0].shape[0]
+    for number, block in enumerate(joined):
+        joint[number * length : (number + 1) * length, :] = block[...]
+    columns = joint.shape[1] // 4
+    count = out.shape[0]
+    groups = lefts.shape[1] // (lines * count)
+    across = inner(joint[:, 3 * columns : 4 * columns], rights[...]).astype(BF16)
+    for group in range(groups):
+        start = group * lines * count
+        block = inner(lefts[:, start : start + lines * count], joint[:, 0 : 3 * columns])
+        block = block.astype(BF16)
+        row = group * lines
+        for number in range(count):
+            at = slice(number * lines, (number + 1) * lines)
+            out[number, row : row + lines, 0 : 3 * columns] = block[at, :]
+            out[number, row : row + lines, 3 * columns : 4 * columns] = across[
+                at, group * columns : (group + 1) * columns
+            ]
+
+
+def swap(value, mask):
+    size = lax.axis_size("dp")
+    return lax.ppermute(value, "dp", [(i, i ^ mask) for i in range(size)])
+
+
+def spread_rows(pieces):
+    devices, depth = lax.axis_size("dp"), lax.axis_size("ctx")
+    place = lax.axis_index("ctx")
+    got = []
+    for step in range(2):
+        pairs = []
+        for dp in range(devices):
+            for z in range(depth):
+                target = (dp - dp % 2 + z // 2) * depth + 2 * (dp % 2) + (z + step) % 2
+                pairs.append((dp * depth + z, target))
+        picked = jnp.where((place + step) % 2 == 0, pieces[0], pieces[1])
+        got.append(lax.ppermute(picked, ("dp", "ctx"), pairs))
+    return got
+
+
+def return_rows(half):
+    devices, depth = lax.axis_size("dp"), lax.axis_size("ctx")
+    place = lax.axis_index("ctx")
+    piece = half.shape[0] // 2
+    got = []
+    for step in range(2):
+        pairs = []
+        for dp in range(devices):
+            for z in range(depth):
+                target = (dp - dp % 2 + z // 2) * depth + 2 * (dp % 2) + (z + step) % 2
+                pairs.append((target, dp * depth + z))
+        got.append(
+            lax.ppermute(half[step * piece : (step + 1) * piece], ("dp", "ctx"), pairs)
+        )
+    even = place % 2 == 0
+    return jnp.stack([jnp.where(even, got[0], got[1]), jnp.where(even, got[1], got[0])])
+
+
+def gather_plane(own):
+    chips = lax.axis_size("dp") // 2
+    mine = [swap(own, 2 * mask) for mask in range(1, chips)]
+    return mine + [swap(value, 1) for value in mine]
+
+
+def scatter_line(chunks):
+    depth = chunks.shape[0]
+    place = lax.axis_index("ctx")
+
+    def take(number):
+        number = jnp.clip(number, 0, depth - 1)
+        return lax.dynamic_index_in_dim(chunks, number, 0, keepdims=False)
+
+    right, left = None, None
+    for step in range(1, depth):
+        out_right = take(depth - step + place)
+        out_left = take(place - (depth - step))
+        if right is not None:
+            out_right = (out_right.astype(F32) + right.astype(F32)).astype(BF16)
+            out_left = (out_left.astype(F32) + left.astype(F32)).astype(BF16)
+        right = lax.ppermute(out_right, "ctx", [(z, z + 1) for z in range(step)])
+        left = lax.ppermute(
+            out_left, "ctx", [(z, z - 1) for z in range(depth - 1, depth - 1 - step, -1)]
+        )
+    return take(place).astype(F32) + right.astype(F32) + left.astype(F32)
+
+
+def trade_columns(blocks):
+    size = blocks.shape[0]
+    rows = blocks.shape[1]
+    me = lax.axis_index("dp")
+    held = blocks
+    bit = 1
+    while bit < size:
+        pair = held.reshape(held.shape[0] // 2, 2, rows, held.shape[2])
+        mine = (me // bit) % 2
+        keep = lax.dynamic_index_in_dim(pair, mine, 1, keepdims=False)
+        send = lax.dynamic_index_in_dim(pair, 1 - mine, 1, keepdims=False)
+        got = swap(send.astype(BF16), bit).astype(F32)
+        low = mine == 0
+        held = jnp.concatenate([jnp.where(low, keep, got), jnp.where(low, got, keep)], axis=2)
+        bit *= 2
+    return held[0]
+
+
+def total_over_devices(value):
+    bit = 1
+    while bit < lax.axis_size("dp"):
+        value = value + swap(value, bit)
+        bit *= 2
+    depth = lax.axis_size("ctx")
+    bit = 1
+    while bit < depth:
+        value = value + lax.ppermute(value, "ctx", [(z, z ^ bit) for z in range(depth)])
+        bit *= 2
+    return value
+
+
+def slot_body(tokens, out_grad, lengths, w_qkv, w_out, w_in, w_fc2, vectors, moment_one, moment_two):
+    slots, piece, width = tokens.shape
+    devices, depth = lax.axis_size("dp"), lax.axis_size("ctx")
+    chips = devices // 2
+    count = devices * depth
+    me, slot = lax.axis_index("dp"), lax.axis_index("ctx")
+    core, chip = me % 2, me // 2
+    half = 2 * piece
+    rows = 2 * half
+    block = D // devices
+    features = w_in.shape[1]
+    lines = D // count
+
+    first = spread_rows(tokens)
+    own = jnp.concatenate(first, axis=0)
+    other = swap(own, 1)
+    peer_lengths = swap(lengths, 1)
+    owner = slot // 2
+    length = jnp.where(owner == core, lengths, peer_lengths)
+    length = jnp.where(slot % 2 == 0, length[0], length[1])
+    scalars = jnp.stack([core, slot, length, chip, me]).astype(jnp.int32)
+    grad_pieces = spread_rows(out_grad)
+    grad_own = jnp.concatenate(grad_pieces, axis=0)
+    grad_other = swap(grad_own, 1)
+    ratio = features // D
+    bias_in = vectors[3 : 3 + ratio].reshape(1, features)
+
+    def head_block(i, s):
+        return 2 * jnp.bitwise_xor(i, s[3]) + s[0]
+
+    token_rows, saved, part = call(
+        partial(attention_kernel, piece),
+        scalars,
+        chips,
+        [
+            (own, full((half, D))),
+            (other, full((half, D))),
+            (w_qkv, pl.BlockSpec((D, block), lambda i, s: (0, head_block(i, s)))),
+            (w_qkv, pl.BlockSpec((D, block), lambda i, s: (0, devices + head_block(i, s)))),
+            (w_qkv, pl.BlockSpec((D, block), lambda i, s: (0, 2 * devices + head_block(i, s)))),
+            (w_out, pl.BlockSpec((block, D), lambda i, s: (head_block(i, s), 0))),
+            (vectors, pl.BlockSpec((vectors.shape[0], block), lambda i, s: (0, head_block(i, s)))),
+        ],
+        [
+            (jax.ShapeDtypeStruct((rows, D), BF16), full((rows, D))),
+            (
+                jax.ShapeDtypeStruct((chips, rows, 4 * block), BF16),
+                pl.BlockSpec((1, rows, 4 * block), lambda i, s: (i, 0, 0)),
+            ),
+            (jax.ShapeDtypeStruct((rows, D), F32), full((rows, D))),
+        ],
+        flops=2 * rows * D * 4 * D // 2,
+        moved=6 * 1024 * 1024,
+        name="attention",
+    )
+    peer = swap(part, 1)
+    token_plane = gather_plane(own)
+
+    wide = 512
+    steps = features // 2 // wide
+    vec_spec = full(vectors.shape)
+    up_spec = pl.BlockSpec((D, wide), lambda i, s: (0, s[0] * steps + i))
+    down_spec = pl.BlockSpec((wide, D), lambda i, s: (s[0] * steps + i, 0))
+    row_f32 = (jax.ShapeDtypeStruct((rows, D), F32), full((rows, D)))
+    row_low = (jax.ShapeDtypeStruct((rows, D), BF16), full((rows, D)))
+    half_low = (jax.ShapeDtypeStruct((half, D), BF16), full((half, D)))
+    half_f32 = (jax.ShapeDtypeStruct((half, D), F32), full((half, D)))
+    summed, normed_low, normed_own, hidden_pre, part = call(
+        feed_kernel,
+        scalars,
+        steps,
+        [
+            (token_rows, full((rows, D))),
+            (part, full((rows, D))),
+            (peer, full((rows, D))),
+            (vectors, vec_spec),
+            (bias_in, pl.BlockSpec((1, wide), lambda i, s: (0, s[0] * steps + i))),
+            (w_in, up_spec),
+            (w_fc2, down_spec),
+        ],
+        [
+            row_f32,
+            row_low,
+            half_low,
+            (
+                jax.ShapeDtypeStruct((rows, features // 2), F32),
+                pl.BlockSpec((rows, wide), lambda i, s: (0, i)),
+            ),
+            row_f32,
+        ],
+        flops=2 * rows * D * features,
+        moved=14 * 1024 * 1024,
+        name="feed",
+    )
+    peer = swap(part, 1)
+    normed_plane = gather_plane(normed_own)
+
+    result, grad_low, grad_low_own, grad_two, vec_two, part = call(
+        partial(feed_back_kernel, piece),
+        scalars,
+        steps,
+        [
+            (summed, full((rows, D))),
+            (part, full((rows, D))),
+            (peer, full((rows, D))),
+            (grad_own, full((half, D))),
+            (grad_other, full((half, D))),
+            (vectors, vec_spec),
+            (hidden_pre, pl.BlockSpec((rows, wide), lambda i, s: (0, i))),
+            (w_in, up_spec),
+            (w_fc2, down_spec),
+        ],
+        [
+            half_low,
+            row_low,
+            half_low,
+            row_f32,
+            (jax.ShapeDtypeStruct((8, D), F32), full((8, D))),
+            row_f32,
+        ],
+        scratch=[pltpu.VMEM((rows, D), BF16)],
+        flops=2 * rows * D * features,
+        moved=16 * 1024 * 1024,
+        name="feed_back",
+    )
+    peer = swap(part, 1)
+    grad_plane = gather_plane(grad_low_own)
+    out = return_rows(result)
+
+    *joined, branch_low, branch_own, vec_one, side, keep, send = call(
+        partial(attention_back_kernel, piece, chips),
+        scalars,
+        chips,
+        [
+            (summed, full((rows, D))),
+            (grad_two, full((rows, D))),
+            (part, full((rows, D))),
+            (peer, full((rows, D))),
+            (vectors, vec_spec),
+            (w_out, pl.BlockSpec((block, D), lambda i, s: (head_block(i, s), 0))),
+            (saved, pl.BlockSpec((1, rows, 4 * block), lambda i, s: (i, 0, 0))),
+            (w_qkv, pl.BlockSpec((D, block), lambda i, s: (0, head_block(i, s)))),
+            (w_qkv, pl.BlockSpec((D, block), lambda i, s: (0, devices + head_block(i, s)))),
+            (w_qkv, pl.BlockSpec((D, block), lambda i, s: (0, 2 * devices + head_block(i, s)))),
+        ],
+        [(jax.ShapeDtypeStruct((rows, 4 * block), BF16), full((rows, 4 * block)))] * chips
+        + [
+            row_low,
+            half_low,
+            (jax.ShapeDtypeStruct((8, D), F32), full((8, D))),
+            (
+                jax.ShapeDtypeStruct((chips, 8, block), F32),
+                pl.BlockSpec((1, 8, block), lambda i, s: (jnp.bitwise_xor(i, s[3]), 0, 0)),
+            ),
+            half_f32,
+            half_f32,
+        ],
+        scratch=[pltpu.VMEM((rows, D), F32)],
+        flops=2 * rows * D * 4 * D // 2 * 2,
+        moved=8 * 1024 * 1024,
+        name="attention_back",
+    )
+    tokens_half = (keep + swap(send, 1)).astype(BF16)
+    tokens_grad = return_rows(tokens_half)
+    branch_plane = gather_plane(branch_own)
+    joined_plane = [joined[0]] + [swap(joined[mask], 2 * mask) for mask in range(1, chips)]
+
+    others = chips - 1
+    total = rows * chips
+    part_f = features // devices
+    half_spec = full((half, D))
+    plane_specs = [full((rows, D))] + [half_spec] * (2 * others)
+    packed, bias_rows = call(
+        partial(feed_grad_kernel, others, lines),
+        scalars,
+        1,
+        list(zip([normed_low] + normed_plane, plane_specs))
+        + list(zip([grad_low] + grad_plane, plane_specs))
+        + [
+            (w_in, pl.BlockSpec((D, part_f), lambda i, s: (0, s[4]))),
+            (w_fc2, pl.BlockSpec((part_f, D), lambda i, s: (s[4], 0))),
+            (bias_in, pl.BlockSpec((1, part_f), lambda i, s: (0, s[4]))),
+        ],
+        [
+            (
+                jax.ShapeDtypeStruct((depth, 2 * part_f // depth, D), BF16),
+                full((depth, 2 * part_f // depth, D)),
+            ),
+            (jax.ShapeDtypeStruct((1, part_f), F32), full((1, part_f))),
+        ],
+        scratch=[
+            pltpu.VMEM((total, D), BF16),
+            pltpu.VMEM((total, D), BF16),
+            pltpu.VMEM((total, part_f), BF16),
+            pltpu.VMEM((total, part_f), BF16),
+        ],
+        flops=2 * total * D * part_f * 4,
+        moved=10 * 1024 * 1024,
+        name="feed_grad",
+    )
+    feed_sum = scatter_line(packed)
+    (packed_two,) = call(
+        partial(input_grad_kernel, others, lines),
+        scalars,
+        1,
+        list(zip([token_rows] + token_plane, plane_specs))
+        + list(zip([branch_low] + branch_plane, plane_specs))
+        + [(value, full((rows, 4 * block))) for value in joined_plane],
+        [
+            (
+                jax.ShapeDtypeStruct((depth, devices * lines, 4 * block), BF16),
+                full((depth, devices * lines, 4 * block)),
+            ),
+        ],
+        scratch=[
+            pltpu.VMEM((total, D), BF16),
+            pltpu.VMEM((total, D), BF16),
+            pltpu.VMEM((total, 4 * block), BF16),
+        ],
+        flops=2 * total * D * 4 * block,
+        moved=8 * 1024 * 1024,
+        name="input_grad",
+    )
+    input_sum = scatter_line(packed_two)
+
+    down_rows = part_f // depth
+    grad_fc2 = feed_sum[:down_rows]
+    packs = D // part_f
+    in_blocks = (
+        feed_sum[down_rows:]
+        .reshape(devices // packs, lines, packs, part_f)
+        .transpose(2, 0, 1, 3)
+        .reshape(devices, lines, part_f)
+    )
+    grad_in = trade_columns(in_blocks)
+    by_owner = input_sum.reshape(devices, lines, 4 * block)
+    grad_joint = trade_columns(by_owner[:, :, : 3 * block])
+    grad_qkv = (
+        grad_joint.reshape(lines, devices, 3, block).transpose(0, 2, 1, 3).reshape(lines, 3 * D)
+    )
+    grad_out_w = by_owner[:, :, 3 * block :].transpose(1, 0, 2).reshape(lines, D)
+
+    once = (core == 0).astype(F32)
+    side_rows = side[:, :2].transpose(1, 0, 2)
+    spot = jnp.arange(2, dtype=jnp.int32)[None, None, :, None] == core
+    side_rows = jnp.where(spot, side_rows[:, :, None, :], 0.0).reshape(2, D)
+    bias_grad = lax.dynamic_update_slice_in_dim(
+        jnp.zeros((1, features), F32), bias_rows, me * part_f, 1
+    ).reshape(ratio, D)
+    vector_grad = jnp.concatenate(
+        [
+            side_rows,
+            vec_one[0:1] * once,
+            bias_grad,
+            vec_two[0:1] * once,
+            vec_one[1:3] * once,
+            vec_two[1:3] * once,
+        ],
+        axis=0,
+    )
+    vector_grad = total_over_devices(vector_grad).reshape(count, -1)
+    index = me * depth + slot
+    own_vectors = lax.dynamic_slice_in_dim(vector_grad, index, 1, 0)
+    grad_rows = jnp.concatenate(
+        [value.reshape(1, -1) for value in (grad_qkv, grad_out_w, grad_in, grad_fc2, own_vectors)],
+        axis=1,
+    )
+    return (out, tokens_grad) + update(
+        grad_rows, index, count, (w_qkv, w_out, w_in, w_fc2, vectors), moment_one, moment_two
+    )
+
+
+def update(grad_rows, index, count, weights, moment_one, moment_two):
+    pieces = []
+    for weight in weights:
+        if weight.shape[0] % count == 0:
+            lines = weight.shape[0] // count
+            piece = lax.dynamic_slice_in_dim(weight, index * lines, lines, 0)
+        else:
+            piece = lax.dynamic_slice_in_dim(weight.reshape(count, -1), index, 1, 0)
+        pieces.append(piece.reshape(1, -1).astype(F32))
+    params = jnp.concatenate(pieces, axis=1)
+    new_one = beta_one * moment_one + (1.0 - beta_one) * grad_rows
+    new_two = beta_two * moment_two + (1.0 - beta_two) * grad_rows * grad_rows
+    fix_one = 1.0 - beta_one**step_count
+    fix_two = 1.0 - beta_two**step_count
+    change = new_one / fix_one / (jnp.sqrt(new_two / fix_two) + adam_eps)
+    new_params = params - learn_rate * (change + decay_rate * params)
+    return (grad_rows, new_params, new_one, new_two)
+
+
+def layer(tokens, *rest):
+    slots, piece, width = tokens.shape
+    devices, depth = lax.axis_size("dp"), lax.axis_size("ctx")
+    fits = slots == 2 and depth == 2 * slots and devices % 2 == 0
+    if fits and (H * HD // devices) % 128 == 0 and (FF // devices) % 128 == 0:
+        return slot_body(tokens, *rest)
+    return body(tokens, *rest)
+
+
 def solution(mesh):
     placed = (
         P("dp", "ctx", None),
@@ -313,7 +1028,7 @@
         P(("dp", "ctx"), None),
     )
     return jax.shard_map(
-        body,
+        layer,
         mesh=mesh,
         in_specs=placed,
         out_specs=(

time: 1140 us -> 293 us (0.26)
  waiting for transfers between devices: 758 us -> 80 us
  local copies, waits for them, and re-layouts: 197 us -> 23.6 us
  matrix products: 127 us -> 0 us
  starting transfers between devices: 0.46 us -> 89.3 us
  Pallas kernels: 0 us -> 65.2 us
  between operations: 14.9 us -> 2.99 us
    unnamed x8 -> x0, waiting for transfers between devices: 710 us -> none
    dot_general x87 -> x0, matrix products: 124 us -> none  [the longest x16 31.1 us: attend_one_block(): jnp.einsum('hqk,khd->qhd', probs_low, value_heads, preferred_element_type...]
    ppermute x0 -> x65, starting transfers between devices: none -> 89.3 us  [the longest x43 41.8 us: swap(): return lax.ppermute(value, 'dp', [(i, i ^ mask) for i in range(size)])]
    ppermute x0 -> x65, waiting for transfers between devices: none -> 80 us  [the longest x43 48 us: swap(): return lax.ppermute(value, 'dp', [(i, i ^ mask) for i in range(size)])]
    pallas_call x0 -> x6, Pallas kernels: none -> 65.2 us  [call(): pl.pallas_call(kernel, out_shape=shapes, grid_spec=pltpu.PrefetchScalarGr...]
    all_gather x4 -> x0, waiting for transfers between devices: 48.3 us -> none  [the longest x2 31.6 us: body(): lax.all_gather(keys.reshape(slots, piece, width), 'ctx', axis=1, tiled=True)]
    another operation x7 -> x2, local copies, waits for them, and re-layouts: 41.8 us -> 0.89 us  [the longest x1 0.61 us: slot_body(): scalars = jnp.stack([core, slot, length, chip, me]).astype(jnp.int32)]
    reshape x19 -> x5, local copies, waits for them, and re-layouts: 37.6 us -> 1.21 us  [the longest x1 0.63 us: slot_body(): vector_grad = total_over_devices(vector_grad).reshape(count, -1)]
  transfers between devices with their start and end apart: 7 -> 65, of which waited for: 4 -> 21; matrix products, arithmetic and copies ran while one was open for 14% -> 11% of each run, Pallas kernels for 0% -> 10%
where the time goes in v1:
time: 293 us; the launch traced here: 291 us
  starting transfers between devices  89.3 us (30%)
  waiting for transfers between devices  80 us (27%)
  Pallas kernels  65.2 us (22%)
  other arithmetic  30.4 us (10%)
  local copies, waits for them, and re-layouts  23.6 us (8%)
  between operations  2.99 us (1%)
    pallas_call x6, Pallas kernels, call(): pl.pallas_call(kernel, out_shape=shapes, grid_spec=pltpu.PrefetchScalarGr...  65.2 us
    ppermute x43, waiting for transfers between devices, swap(): return lax.ppermute(value, 'dp', [(i, i ^ mask) for i in range(size)])  48 us
    ppermute x43, starting transfers between devices, swap(): return lax.ppermute(value, 'dp', [(i, i ^ mask) for i in range(size)])  41.8 us
    ppermute x6, starting transfers between devices, scatter_line(): right = lax.ppermute(out_right, 'ctx', [(z, z + 1) for z in range(step)])  31.1 us
    unnamed x83, local copies, waits for them, and re-layouts  13.2 us
    sub x1, other arithmetic, update(): new_params = params - learn_rate * (change + decay_rate * params)  12.2 us
    ppermute x6, waiting for transfers between devices, scatter_line(): lax.ppermute(out_left, 'ctx', [(z, z - 1) for z in range(depth - 1, depth...  11.8 us
    ppermute x4, waiting for transfers between devices, return_rows(): lax.ppermute(half[step * piece:(step + 1) * piece], ('dp', 'ctx'), pairs)  10 us
  transfers between devices with their start and end apart: 65, of which 21 were waited for; matrix products, arithmetic and copies ran while one was open for 11% of the time, Pallas kernels for 10%

profile of v1, /device:TPU:0, one launch (start us, length us, event | category | flops | bytes accessed | tf_op | source)
XLA Modules:
  0.0 291.5 jit_solution(494095571849849209)
XLA Ops:
  8.9 5.3 %collective-permute-start.3 = (bf16[128,1024]{1,0:T(8,128)(2,1)S(1)}, bf16[128,1024]{1,0:T(8,128)(2,1)S(1)}, u32[]{:S(2)}, u32[]{:S(2)}) collective-permute-start(bf16[128,1024]{1,0:T(8,128)(2,1)S(1)} %constant_dynamic-update-slice_fusion.own), channel_id=1, source_target_pairs={{0,4},{4,0},{8,12},{12,8},{16,20},{20,16},{24,28},{28,24},{1,5},{5... | collective-permute-start | bytes 786440 | tf_op jit(solution)/shard_map/ppermute | solution.py:622
  18.1 8.7 %attention.1 = (bf16[256,1024]{1,0:T(8,128)(2,1)}, bf16[4,256,512]{2,1,0:T(8,128)(2,1)}, f32[256,1024]{1,0:T(8,128)}) custom-call(s32[5]{0:T(128)} %stack.41.sc, bf16[128,1024]{1,0:T(8,128)(2,1)} %copy-done.9, bf16[128,1024]{1,0:T(8,128)(2,1)} %copy-done.15, bf16[1024,3072]{1,0:T(8,128)(2,1)} %wv.3, bf16[1024,3072]{1,0:T(8,128)(2,1)} %wv.3, ...), custom_call_target="tpu_custom_call" | custom-call | flops 1073741824 | bytes 6291456 | tf_op jit(solution)/shard_map/attention/pallas_call | solution.py:351
  30.6 11.0 %feed.1 = (f32[256,1024]{1,0:T(8,128)}, bf16[256,1024]{1,0:T(8,128)(2,1)}, bf16[128,1024]{1,0:T(8,128)(2,1)}, f32[256,2048]{1,0:T(8,128)}, f32[256,1024]{1,0:T(8,128)}) custom-call(s32[5]{0:T(128)} %stack.41.sc, bf16[256,1024]{1,0:T(8,128)(2,1)} %get-tuple-element.32.rows.refs_0_, f32[256,1024]{1,0:T(8,128)} %get-tuple-element.33.part, ...), custom_call_target="tpu_custom_call" | custom-call | flops 2147483648 | bytes 14680064 | tf_op jit(solution)/shard_map/feed/pallas_call | solution.py:351
  44.0 3.8 %collective-permute-done.7 = bf16[64,1024]{1,0:T(8,128)(2,1)S(1)} collective-permute-done((bf16[64,1024]{1,0:T(8,128)(2,1)S(1)}, bf16[64,1024]{1,0:T(8,128)(2,1)S(1)}, u32[]{:S(2)}, u32[]{:S(2)}) %collective-permute-start.7) | collective-permute-done | bytes 131104 | tf_op jit(solution)/shard_map/ppermute | solution.py:636
  47.8 6.1 %collective-permute-start.8 = (bf16[128,1024]{1,0:T(8,128)(2,1)S(1)}, bf16[128,1024]{1,0:T(8,128)(2,1)S(1)}, u32[]{:S(2)}, u32[]{:S(2)}) collective-permute-start(bf16[128,1024]{1,0:T(8,128)(2,1)S(1)} %constant_dynamic-update-slice_fusion.2.grad_own), channel_id=1, source_target_pairs={{0,4},{4,0},{8,12},{12,8},{16,20},{20,16},{24,28},{28,24},{1,5},{5... | collective-permute-start | bytes 786440 | tf_op jit(solution)/shard_map/ppermute | solution.py:622
  58.8 4.5 %collective-permute-done.39.refs_1_ = bf16[128,1024]{1,0:T(8,128)(2,1)S(1)} collective-permute-done((bf16[128,1024]{1,0:T(8,128)(2,1)}, bf16[128,1024]{1,0:T(8,128)(2,1)S(1)}, u32[]{:S(2)}, u32[]{:S(2)}) %collective-permute-start.39) | collective-permute-done | bytes 262176 | tf_op jit(solution)/shard_map/ppermute | solution.py:622
  63.3 5.9 %collective-permute-done.40.refs_2_ = bf16[128,1024]{1,0:T(8,128)(2,1)S(1)} collective-permute-done((bf16[128,1024]{1,0:T(8,128)(2,1)}, bf16[128,1024]{1,0:T(8,128)(2,1)S(1)}, u32[]{:S(2)}, u32[]{:S(2)}) %collective-permute-start.40) | collective-permute-done | bytes 262176 | tf_op jit(solution)/shard_map/ppermute | solution.py:622
  70.3 13.3 %feed_back.1 = (bf16[128,1024]{1,0:T(8,128)(2,1)}, bf16[256,1024]{1,0:T(8,128)(2,1)}, bf16[128,1024]{1,0:T(8,128)(2,1)}, f32[256,1024]{1,0:T(8,128)}, f32[8,1024]{1,0:T(8,128)}, /*index=5*/f32[256,1024]{1,0:T(8,128)}) custom-call(s32[5]{0:T(128)} %stack.41.sc, f32[256,1024]{1,0:T(8,128)} %get-tuple-element.34.summed, f32[256,1024]{1,0:T(8,128)} %get-tuple-element.35.part, ...), custom_call_target="tpu_custom_call" | custom-call | flops 2147483648 | bytes 16777216 | tf_op jit(solution)/shard_map/feed_back/pallas_call | solution.py:351
  88.7 4.4 %collective-permute-done.45.refs_8_ = bf16[128,1024]{1,0:T(8,128)(2,1)S(1)} collective-permute-done((bf16[128,1024]{1,0:T(8,128)(2,1)}, bf16[128,1024]{1,0:T(8,128)(2,1)S(1)}, u32[]{:S(2)}, u32[]{:S(2)}) %collective-permute-start.45) | collective-permute-done | bytes 262176 | tf_op jit(solution)/shard_map/ppermute | solution.py:622
  93.1 4.6 %collective-permute-done.46.refs_9_ = bf16[128,1024]{1,0:T(8,128)(2,1)S(1)} collective-permute-done((bf16[128,1024]{1,0:T(8,128)(2,1)}, bf16[128,1024]{1,0:T(8,128)(2,1)S(1)}, u32[]{:S(2)}, u32[]{:S(2)}) %collective-permute-start.46) | collective-permute-done | bytes 262176 | tf_op jit(solution)/shard_map/ppermute | solution.py:622
  101.8 10.3 %feed_grad.1 = (bf16[4,256,1024]{2,1,0:T(8,128)(2,1)}, f32[1,512]{1,0:T(1,128)}) custom-call(s32[5]{0:T(128)} %stack.41.sc, bf16[256,1024]{1,0:T(8,128)(2,1)} %get-tuple-element.49.refs_0_, bf16[128,1024]{1,0:T(8,128)(2,1)} %copy-done.20, bf16[128,1024]{1,0:T(8,128)(2,1)} %copy-done.21, bf16[128,1024]{1,0:T(8,128)(2,1)} %copy-done.22, ...), custom_call_target="tpu_custom_call" | custom-call | flops 4294967296 | bytes 10485760 | tf_op jit(solution)/shard_map/feed_grad/pallas_call | solution.py:351
  115.1 16.0 %attention_back.1 = (bf16[256,512]{1,0:T(8,128)(2,1)}, bf16[256,512]{1,0:T(8,128)(2,1)}, bf16[256,512]{1,0:T(8,128)(2,1)}, bf16[256,512]{1,0:T(8,128)(2,1)}, bf1...) custom-call(s32[5]{0:T(128)} %stack.41.sc, ...), custom_call_target="tpu_custom_call" | custom-call | flops 2147483648 | bytes 8388608 | tf_op jit(solution)/shard_map/attention_back/pallas_call | solution.py:351
  146.0 6.1 %collective-permute-done.16.refs_2_ = bf16[128,1024]{1,0:T(8,128)(2,1)} collective-permute-done((bf16[128,1024]{1,0:T(8,128)(2,1)S(1)}, bf16[128,1024]{1,0:T(8,128)(2,1)}, u32[]{:S(2)}, u32[]{:S(2)}) %collective-permute-start.16) | collective-permute-done | bytes 262176 | tf_op jit(solution)/shard_map/ppermute | solution.py:622
  165.0 4.8 %collective-permute-done.51 = bf16[256,1024]{1,0:T(8,128)(2,1)S(1)} collective-permute-done((bf16[256,1024]{1,0:T(8,128)(2,1)}, bf16[256,1024]{1,0:T(8,128)(2,1)S(1)}, u32[]{:S(2)}, u32[]{:S(2)}) %collective-permute-start.51) | collective-permute-done | bytes 524320 | tf_op jit(solution)/shard_map/ppermute | solution.py:679
  174.1 5.3 %collective-permute-done.22.refs_9_ = bf16[128,1024]{1,0:T(8,128)(2,1)S(1)} collective-permute-done((bf16[128,1024]{1,0:T(8,128)(2,1)}, bf16[128,1024]{1,0:T(8,128)(2,1)S(1)}, u32[]{:S(2)}, u32[]{:S(2)}) %collective-permute-start.22) | collective-permute-done | bytes 262176 | tf_op jit(solution)/shard_map/ppermute | solution.py:622
  190.8 5.9 %input_grad.1 = bf16[4,256,512]{2,1,0:T(8,128)(2,1)} custom-call(s32[5]{0:T(128)} %stack.41.sc, bf16[256,1024]{1,0:T(8,128)(2,1)} %get-tuple-element.32.rows.refs_0_, bf16[128,1024]{1,0:T(8,128)(2,1)} %copy-done.16, bf16[128,1024]{1,0:T(8,128)(2,1)} %collective-permute-done.16.refs_2_, bf16[128,1024]{1,0:T(8,128)(2,1)} %collective-permute-done.17.refs_3_, ...), custom_call_target="tpu_custom_call" | custom-call | flops 1073741824 | bytes 8388608 | tf_op jit(solution)/shard_map/input_grad/pallas_call | solution.py:351
  198.6 3.6 %collective-permute-start.30 = (bf16[256,512]{1,0:T(8,128)(2,1)S(1)}, bf16[256,512]{1,0:T(8,128)(2,1)S(1)}, u32[]{:S(2)}, u32[]{:S(2)}) collective-permute-start(bf16[256,512]{1,0:T(8,128)(2,1)S(1)} %get-tuple-element.69), channel_id=1, source_target_pairs={{0,1},{4,5},{8,9},{12,13},{16,17},{20,21},{24,25},{28,29}} | collective-permute-start | bytes 786440 | tf_op jit(solution)/shard_map/ppermute | solution.py:679
  206.5 4.1 %collective-permute-start.31 = (bf16[256,512]{1,0:T(8,128)(2,1)S(1)}, bf16[256,512]{1,0:T(8,128)(2,1)S(1)}, u32[]{:S(2)}, u32[]{:S(2)}) collective-permute-start(bf16[256,512]{1,0:T(8,128)(2,1)S(1)} %fusion.8), channel_id=1, source_target_pairs={{0,1},{1,2},{4,5},{5,6},{8,9},{9,10},{12,13},{13,14},{16,17},{17,1... | collective-permute-start | bytes 786440 | tf_op jit(solution)/shard_map/ppermute | solution.py:679
  210.6 12.7 %collective-permute-start.53 = (bf16[256,1024]{1,0:T(8,128)(2,1)S(1)}, bf16[256,1024]{1,0:T(8,128)(2,1)S(1)}, u32[]{:S(2)}, u32[]{:S(2)}) collective-permute-start(bf16[256,1024]{1,0:T(8,128)(2,1)S(1)} %get-tuple-element.61), channel_id=1, source_target_pairs={{0,1},{1,2},{2,3},{4,5},{5,6},{6,7},{8,9},{9,10},{10,11},{12,13},{... | collective-permute-start | bytes 1572872 | tf_op jit(solution)/shard_map/ppermute | solution.py:679
  228.4 10.0 %collective-permute-done.14 = bf16[64,1024]{1,0:T(8,128)(2,1)S(1)} collective-permute-done((bf16[64,1024]{1,0:T(8,128)(2,1)S(1)}, bf16[64,1024]{1,0:T(8,128)(2,1)S(1)}, u32[]{:S(2)}, u32[]{:S(2)}) %collective-permute-start.14) | collective-permute-done | bytes 131104 | tf_op jit(solution)/shard_map/ppermute | solution.py:652
  239.9 4.4 %collective-permute-start.32 = (bf16[256,512]{1,0:T(8,128)(2,1)}, bf16[256,512]{1,0:T(8,128)(2,1)S(1)}, u32[]{:S(2)}, u32[]{:S(2)}) collective-permute-start(bf16[256,512]{1,0:T(8,128)(2,1)} %get-tuple-element.67), channel_id=1, source_target_pairs={{0,1},{1,2},{2,3},{4,5},{5,6},{6,7},{8,9},{9,10},{10,11},{12,13},{... | collective-permute-start | bytes 786440 | tf_op jit(solution)/shard_map/ppermute | solution.py:679
  249.6 11.7 %collective-permute-done.35 = bf16[256,512]{1,0:T(8,128)(2,1)} collective-permute-done((bf16[256,512]{1,0:T(8,128)(2,1)}, bf16[256,512]{1,0:T(8,128)(2,1)}, u32[]{:S(2)}, u32[]{:S(2)}) %collective-permute-start.35) | collective-permute-done | bytes 262176 | tf_op jit(solution)/shard_map/ppermute | solution.py:680
  266.3 3.4 %collective-permute-done.37 = bf16[2,32,768]{2,1,0:T(8,128)(2,1)S(1)} collective-permute-done((bf16[2,32,768]{2,1,0:T(8,128)(2,1)S(1)}, bf16[2,32,768]{2,1,0:T(8,128)(2,1)S(1)}, u32[]{:S(2)}, u32[]{:S(2)}) %collective-permute-start.37) | collective-permute-done | bytes 98336 | tf_op jit(solution)/shard_map/ppermute | solution.py:622
  279.2 12.2 %multiply_subtract_fusion = (f32[1,393600]{1,0:T(1,128)}, f32[1,393600]{1,0:T(1,128)}, f32[1,393600]{1,0:T(1,128)}) fusion(f32[1,393600]{1,0:T(1,128)} %constant_dynamic-update-slice_fusion.9, f32[1,393600]{1,0:T(1,128)S(1)} %constant_dynamic-update-slice_fusion.4, f32[1,393600]{1,0:T(1,128)S(1)} %copy-done.4, f32[1,393600]{1,0:T(1,128)S(1)} %copy-done.5), kind=kLoop, calls=%fused_computation.2 | loop fusion | flops 5904000 | bytes 11020800 | tf_op jit(solution)/shard_map/sub | solution.py:1004
  (273 shorter events, 110.2 us)
Async XLA Ops:
  41.6 27.6 %collective-permute-start.5 = (f32[256,1024]{1,0:T(8,128)}, f32[256,1024]{1,0:T(8,128)S(1)}, u32[]{:S(2)}, u32[]{:S(2)}) collective-permute-start(f32[256,1024]{1,0:T(8,128)} %get-tuple-element.35.part), channel_id=1, source_target_pairs={{0,4},{4,0},{8,12},{12,8},{16,20},{20,16},{24,28},{28,24},{1,5},{5... | collective-permute-start | bytes 3145736 | tf_op jit(solution)/shard_map/ppermute | solution.py:622
  47.8 21.5 %collective-permute-start.8 = (bf16[128,1024]{1,0:T(8,128)(2,1)S(1)}, bf16[128,1024]{1,0:T(8,128)(2,1)S(1)}, u32[]{:S(2)}, u32[]{:S(2)}) collective-permute-start(bf16[128,1024]{1,0:T(8,128)(2,1)S(1)} %constant_dynamic-update-slice_fusion.2.grad_own), channel_id=1, source_target_pairs={{0,4},{4,0},{8,12},{12,8},{16,20},{20,16},{24,28},{28,24},{1,5},{5... | collective-permute-start | bytes 786440 | tf_op jit(solution)/shard_map/ppermute | solution.py:622
  56.9 28.9 %collective-permute-start.41 = (bf16[128,1024]{1,0:T(8,128)(2,1)}, bf16[128,1024]{1,0:T(8,128)(2,1)S(1)}, u32[]{:S(2)}, u32[]{:S(2)}) collective-permute-start(bf16[128,1024]{1,0:T(8,128)(2,1)} %get-tuple-element.50), channel_id=1, source_target_pairs={{0,24},{4,28},{8,16},{12,20},{16,8},{20,12},{24,0},{28,4},{1,25},{... | collective-permute-start | bytes 786440 | tf_op jit(solution)/shard_map/ppermute | solution.py:622
  63.3 24.7 %collective-permute-start.42 = (bf16[128,1024]{1,0:T(8,128)(2,1)S(1)}, bf16[128,1024]{1,0:T(8,128)(2,1)S(1)}, u32[]{:S(2)}, u32[]{:S(2)}) collective-permute-start(bf16[128,1024]{1,0:T(8,128)(2,1)S(1)} %collective-permute-done.39.refs_1_), channel_id=1, source_target_pairs={{0,4},{4,0},{8,12},{12,8},{16,20},{20,16},{24,28},{28,24},{1,5},{5... | collective-permute-start | bytes 786440 | tf_op jit(solution)/shard_map/ppermute | solution.py:622
  69.2 18.9 %collective-permute-start.43 = (bf16[128,1024]{1,0:T(8,128)(2,1)S(1)}, bf16[128,1024]{1,0:T(8,128)(2,1)S(1)}, u32[]{:S(2)}, u32[]{:S(2)}) collective-permute-start(bf16[128,1024]{1,0:T(8,128)(2,1)S(1)} %collective-permute-done.40.refs_2_), channel_id=1, source_target_pairs={{0,4},{4,0},{8,12},{12,8},{16,20},{20,16},{24,28},{28,24},{1,5},{5... | collective-permute-start | bytes 786440 | tf_op jit(solution)/shard_map/ppermute | solution.py:622
  88.0 26.1 %collective-permute-start.11 = (f32[256,1024]{1,0:T(8,128)}, f32[256,1024]{1,0:T(8,128)S(1)}, u32[]{:S(2)}, u32[]{:S(2)}) collective-permute-start(f32[256,1024]{1,0:T(8,128)} %get-tuple-element.39.part), channel_id=1, source_target_pairs={{0,4},{4,0},{8,12},{12,8},{16,20},{20,16},{24,28},{28,24},{1,5},{5... | collective-permute-start | bytes 3145736 | tf_op jit(solution)/shard_map/ppermute | solution.py:622
  137.9 14.2 %collective-permute-start.16 = (bf16[128,1024]{1,0:T(8,128)(2,1)S(1)}, bf16[128,1024]{1,0:T(8,128)(2,1)}, u32[]{:S(2)}, u32[]{:S(2)}) collective-permute-start(bf16[128,1024]{1,0:T(8,128)(2,1)S(1)} %copy-done.10), channel_id=1, source_target_pairs={{0,16},{4,20},{8,24},{12,28},{16,0},{20,4},{24,8},{28,12},{1,17},{... | collective-permute-start | bytes 786440 | tf_op jit(solution)/shard_map/ppermute | solution.py:622
  154.7 15.1 %collective-permute-start.51 = (bf16[256,1024]{1,0:T(8,128)(2,1)}, bf16[256,1024]{1,0:T(8,128)(2,1)S(1)}, u32[]{:S(2)}, u32[]{:S(2)}) collective-permute-start(bf16[256,1024]{1,0:T(8,128)(2,1)} %get-tuple-element.63), channel_id=1, source_target_pairs={{0,1},{4,5},{8,9},{12,13},{16,17},{20,21},{24,25},{28,29}} | collective-permute-start | bytes 1572872 | tf_op jit(solution)/shard_map/ppermute | solution.py:679
  157.8 14.7 %collective-permute-start.21 = (bf16[128,1024]{1,0:T(8,128)(2,1)}, bf16[128,1024]{1,0:T(8,128)(2,1)}, u32[]{:S(2)}, u32[]{:S(2)}) collective-permute-start(bf16[128,1024]{1,0:T(8,128)(2,1)} %get-tuple-element.44), channel_id=1, source_target_pairs={{0,8},{4,12},{8,0},{12,4},{16,24},{20,28},{24,16},{28,20},{1,9},{5... | collective-permute-start | bytes 786440 | tf_op jit(solution)/shard_map/ppermute | solution.py:622
  162.6 16.8 %collective-permute-start.22 = (bf16[128,1024]{1,0:T(8,128)(2,1)}, bf16[128,1024]{1,0:T(8,128)(2,1)S(1)}, u32[]{:S(2)}, u32[]{:S(2)}) collective-permute-start(bf16[128,1024]{1,0:T(8,128)(2,1)} %get-tuple-element.44), channel_id=1, source_target_pairs={{0,16},{4,20},{8,24},{12,28},{16,0},{20,4},{24,8},{28,12},{1,17},{... | collective-permute-start | bytes 786440 | tf_op jit(solution)/shard_map/ppermute | solution.py:622
  164.2 16.2 %collective-permute-start.23 = (bf16[128,1024]{1,0:T(8,128)(2,1)}, bf16[128,1024]{1,0:T(8,128)(2,1)}, u32[]{:S(2)}, u32[]{:S(2)}) collective-permute-start(bf16[128,1024]{1,0:T(8,128)(2,1)} %get-tuple-element.44), channel_id=1, source_target_pairs={{0,24},{4,28},{8,16},{12,20},{16,8},{20,12},{24,0},{28,4},{1,25},{... | collective-permute-start | bytes 786440 | tf_op jit(solution)/shard_map/ppermute | solution.py:622
  171.0 15.3 %collective-permute-start.28 = (bf16[256,512]{1,0:T(8,128)(2,1)}, bf16[256,512]{1,0:T(8,128)(2,1)}, u32[]{:S(2)}, u32[]{:S(2)}) collective-permute-start(bf16[256,512]{1,0:T(8,128)(2,1)} %get-tuple-element.47), channel_id=1, source_target_pairs={{0,16},{4,20},{8,24},{12,28},{16,0},{20,4},{24,8},{28,12},{1,17},{... | collective-permute-start | bytes 786440 | tf_op jit(solution)/shard_map/ppermute | solution.py:622
  180.4 17.4 %collective-permute-start.54 = (bf16[256,1024]{1,0:T(8,128)(2,1)}, bf16[256,1024]{1,0:T(8,128)(2,1)S(1)}, u32[]{:S(2)}, u32[]{:S(2)}) collective-permute-start(bf16[256,1024]{1,0:T(8,128)(2,1)} %get-tuple-element.64), channel_id=1, source_target_pairs={{3,2},{7,6},{11,10},{15,14},{19,18},{23,22},{27,26},{31,30}} | collective-permute-start | bytes 1572872 | tf_op jit(solution)/shard_map/ppermute | solution.py:680
  181.1 21.2 %collective-permute-start.52 = (bf16[256,1024]{1,0:T(8,128)(2,1)}, bf16[256,1024]{1,0:T(8,128)(2,1)}, u32[]{:S(2)}, u32[]{:S(2)}) collective-permute-start(bf16[256,1024]{1,0:T(8,128)(2,1)} %fusion.3), channel_id=1, source_target_pairs={{0,1},{1,2},{4,5},{5,6},{8,9},{9,10},{12,13},{13,14},{16,17},{17,1... | collective-permute-start | bytes 1572872 | tf_op jit(solution)/shard_map/ppermute | solution.py:679
  187.4 17.2 %collective-permute-start.12 = (f32[128,1024]{1,0:T(8,128)}, f32[128,1024]{1,0:T(8,128)}, u32[]{:S(2)}, u32[]{:S(2)}) collective-permute-start(f32[128,1024]{1,0:T(8,128)} %get-tuple-element.42), channel_id=1, source_target_pairs={{0,4},{4,0},{8,12},{12,8},{16,20},{20,16},{24,28},{28,24},{1,5},{5... | collective-permute-start | bytes 1572872 | tf_op jit(solution)/shard_map/ppermute | solution.py:622
  189.7 36.7 %collective-permute-start.10 = (bf16[64,1024]{1,0:T(8,128)(2,1)}, bf16[64,1024]{1,0:T(8,128)(2,1)S(1)}, u32[]{:S(2)}, u32[]{:S(2)}) collective-permute-start(bf16[64,1024]{1,0:T(8,128)(2,1)} %get-tuple-element.90), channel_id=1, source_target_pairs={{1,0},{0,1},{5,2},{4,3},{3,4},{2,5},{7,6},{6,7},{9,8},{8,9},{13,10... | collective-permute-start | bytes 393224 | tf_op jit(solution)/shard_map/ppermute | solution.py:652
  190.1 37.6 %collective-permute-start.9 = (bf16[64,1024]{1,0:T(8,128)(2,1)S(1)}, bf16[64,1024]{1,0:T(8,128)(2,1)S(1)}, u32[]{:S(2)}, u32[]{:S(2)}) collective-permute-start(bf16[64,1024]{1,0:T(8,128)(2,1)S(1)} %get-tuple-element.89), channel_id=1, source_target_pairs={{0,0},{1,1},{4,2},{5,3},{2,4},{3,5},{6,6},{7,7},{8,8},{9,9},{12,10... | collective-permute-start | bytes 393224 | tf_op jit(solution)/shard_map/ppermute | solution.py:652
  205.7 17.8 %collective-permute-start.33 = (bf16[256,512]{1,0:T(8,128)(2,1)S(1)}, bf16[256,512]{1,0:T(8,128)(2,1)S(1)}, u32[]{:S(2)}, u32[]{:S(2)}) collective-permute-start(bf16[256,512]{1,0:T(8,128)(2,1)S(1)} %get-tuple-element.70), channel_id=1, source_target_pairs={{3,2},{7,6},{11,10},{15,14},{19,18},{23,22},{27,26},{31,30}} | collective-permute-start | bytes 786440 | tf_op jit(solution)/shard_map/ppermute | solution.py:680
  206.5 17.7 %collective-permute-start.31 = (bf16[256,512]{1,0:T(8,128)(2,1)S(1)}, bf16[256,512]{1,0:T(8,128)(2,1)S(1)}, u32[]{:S(2)}, u32[]{:S(2)}) collective-permute-start(bf16[256,512]{1,0:T(8,128)(2,1)S(1)} %fusion.8), channel_id=1, source_target_pairs={{0,1},{1,2},{4,5},{5,6},{8,9},{9,10},{12,13},{13,14},{16,17},{17,1... | collective-permute-start | bytes 786440 | tf_op jit(solution)/shard_map/ppermute | solution.py:679
  210.6 35.7 %collective-permute-start.53 = (bf16[256,1024]{1,0:T(8,128)(2,1)S(1)}, bf16[256,1024]{1,0:T(8,128)(2,1)S(1)}, u32[]{:S(2)}, u32[]{:S(2)}) collective-permute-start(bf16[256,1024]{1,0:T(8,128)(2,1)S(1)} %get-tuple-element.61), channel_id=1, source_target_pairs={{0,1},{1,2},{2,3},{4,5},{5,6},{6,7},{8,9},{9,10},{10,11},{12,13},{... | collective-permute-start | bytes 1572872 | tf_op jit(solution)/shard_map/ppermute | solution.py:679
  226.4 20.0 %collective-permute-start.56 = (bf16[256,1024]{1,0:T(8,128)(2,1)S(1)}, bf16[256,1024]{1,0:T(8,128)(2,1)S(1)}, u32[]{:S(2)}, u32[]{:S(2)}) collective-permute-start(bf16[256,1024]{1,0:T(8,128)(2,1)S(1)} %fusion.2), channel_id=1, source_target_pairs={{3,2},{2,1},{1,0},{7,6},{6,5},{5,4},{11,10},{10,9},{9,8},{15,14},{... | collective-permute-start | bytes 1572872 | tf_op jit(solution)/shard_map/ppermute | solution.py:680
  227.7 16.6 %collective-permute-start.34 = (bf16[256,512]{1,0:T(8,128)(2,1)S(1)}, bf16[256,512]{1,0:T(8,128)(2,1)S(1)}, u32[]{:S(2)}, u32[]{:S(2)}) collective-permute-start(bf16[256,512]{1,0:T(8,128)(2,1)S(1)} %get-tuple-element.68), channel_id=1, source_target_pairs={{3,2},{2,1},{7,6},{6,5},{11,10},{10,9},{15,14},{14,13},{19,18},{18... | collective-permute-start | bytes 786440 | tf_op jit(solution)/shard_map/ppermute | solution.py:680
  245.0 16.3 %collective-permute-start.35 = (bf16[256,512]{1,0:T(8,128)(2,1)}, bf16[256,512]{1,0:T(8,128)(2,1)}, u32[]{:S(2)}, u32[]{:S(2)}) collective-permute-start(bf16[256,512]{1,0:T(8,128)(2,1)} %fusion.7), channel_id=1, source_target_pairs={{3,2},{2,1},{1,0},{7,6},{6,5},{5,4},{11,10},{10,9},{9,8},{15,14},{... | collective-permute-start | bytes 786440 | tf_op jit(solution)/shard_map/ppermute | solution.py:680
  247.3 16.9 %collective-permute-start.57 = (bf16[4,32,512]{2,1,0:T(8,128)(2,1)S(1)}, bf16[4,32,512]{2,1,0:T(8,128)(2,1)S(1)}, u32[]{:S(2)}, u32[]{:S(2)}) collective-permute-start(bf16[4,32,512]{2,1,0:T(8,128)(2,1)S(1)} %fusion.17), channel_id=1, source_target_pairs={{0,4},{4,0},{8,12},{12,8},{16,20},{20,16},{24,28},{28,24},{1,5},{5... | collective-permute-start | bytes 393224 | tf_op jit(solution)/shard_map/ppermute | solution.py:622
  (73 other events, 603.1 us)

commit v2 on v0

--- a/solution.py
+++ b/solution.py
@@ -3,6 +3,8 @@
 import jax
 import jax.numpy as jnp
 from jax import lax
+from jax.experimental import pallas as pl
+from jax.experimental.pallas import tpu as pltpu
 from jax.sharding import PartitionSpec as P
 
 D = 1024
@@ -299,6 +301,770 @@
     return (out, tokens_grad, grad_rows, new_params, new_one, new_two)
 
 
+BF16 = jnp.bfloat16
+F32 = jnp.float32
+
+
+def layer_norm_stats(values):
+    center = values - jnp.mean(values, axis=-1, keepdims=True)
+    spread = jnp.mean(center * center, axis=-1, keepdims=True)
+    return center, lax.rsqrt(spread + EPSILON)
+
+
+def layer_norm_back(center, scale, gain, cotangent):
+    scaled = cotangent * gain
+    mean_scaled = jnp.mean(scaled, axis=-1, keepdims=True)
+    mean_cross = jnp.mean(scaled * center, axis=-1, keepdims=True)
+    return scale * (scaled - mean_scaled - center * (scale * scale) * mean_cross)
+
+
+def normal_cdf(values):
+    return 0.5 * (1.0 + lax.erf(values * 0.7071067811865476))
+
+
+def dot(left, right):
+    return jnp.dot(left, right, preferred_element_type=F32)
+
+
+def positions(axis, shape, slot, piece):
+    place = lax.broadcasted_iota(jnp.int32, shape, axis)
+    block = lax.div(place, piece)
+    half = lax.div(block, 2)
+    step = lax.rem(block, 2)
+    return (2 * half + lax.rem(slot + step, 2)) * piece + lax.rem(place, piece)
+
+
+def head_probs(queries, keys, live):
+    scores = through(queries, keys)
+    scores = jnp.where(live, scores, -1e30)
+    expo = jnp.exp(scores - jnp.max(scores, axis=-1, keepdims=True))
+    return expo / jnp.sum(expo, axis=-1, keepdims=True)
+
+
+MESH = pl.DeviceIdType.MESH
+
+
+class Links:
+    def __init__(self, sends, recvs):
+        self.sends, self.recvs = sends, recvs
+        self.used = 0
+        self.open = []
+
+    def copy(self, source, target, device):
+        self.used += 1
+        return self.again(source, target, device)
+
+    def again(self, source, target, device):
+        number = self.used - 1
+        return pltpu.make_async_remote_copy(
+            src_ref=source,
+            dst_ref=target,
+            send_sem=self.sends.at[number],
+            recv_sem=self.recvs.at[number],
+            device_id=device,
+            device_id_type=MESH,
+        )
+
+    def send(self, source, target, device):
+        made = self.copy(source, target, device)
+        made.start()
+        self.open.append((made, None))
+        return made
+
+    def send_if(self, condition, source, target, device):
+        made = self.copy(source, target, device)
+        pl.when(condition)(made.start)
+        self.open.append((made, condition))
+        return made
+
+    def send_or_keep(self, here, source, target, device):
+        number = self.used
+        made = self.copy(source, target, device)
+        local = pltpu.make_async_copy(source, target, self.recvs.at[number])
+        pl.when(here)(local.start)
+        away = jnp.logical_not(here)
+        pl.when(away)(made.start)
+        self.open.append((made, away))
+
+        def wait():
+            pl.when(here)(local.wait)
+            pl.when(away)(made.wait_recv)
+
+        return wait
+
+    def close(self):
+        for made, condition in self.open:
+            if condition is None:
+                made.wait_send()
+            else:
+                pl.when(condition)(made.wait_send)
+
+
+def flip(value, mask):
+    result = value
+    bit = 1
+    while bit <= mask:
+        if mask & bit:
+            result = result + bit * (1 - 2 * lax.rem(lax.div(value, bit), 2))
+        bit *= 2
+    return result
+
+
+def flip_traced(value, mask, size):
+    result = value
+    bit = 1
+    while bit < size:
+        set_bit = lax.rem(lax.div(mask, bit), 2)
+        result = result + bit * set_bit * (1 - 2 * lax.rem(lax.div(value, bit), 2))
+        bit *= 2
+    return result
+
+
+def at_rows(start, size):
+    return pl.ds(pl.multiple_of(start, 64), size)
+
+
+def slot_kernel(devices, depth, features, *refs):
+    (
+        tokens, out_grad, lens, vec, w_qkv, w_out, w_in, w_fc2,
+        out_ref, tgrad_ref, g_qkv, g_out, g_in, g_fc2, g_vec,
+        wqkv, wo, w_up, w_down,
+        x_all, n_all, g_all, b_all, j_all, j_send, g_rows, lens_peer,
+        qkv, mixed, part, part_a, part_b, part_c, part_d, summed, grad_two, grad_one,
+        pre_s, hid, hid_all, gp_all, packed, right, left, packed_two, right_two, left_two,
+        trade_in, got_in, trade_qkv, got_qkv, vec_s, vec_got, dqkv, out_half, out_got, tg_half, tg_got,
+        local_sems, sends, recvs,
+    ) = refs
+    chips = devices // 2
+    me, slot = lax.axis_index("dp"), lax.axis_index("ctx")
+    core, chip = lax.rem(me, 2), lax.div(me, 2)
+    base = me - core
+    peer = (base + 1 - core, slot)
+    piece = tokens.shape[1]
+    half = 2 * piece
+    rows = 2 * half
+    block = D // devices
+    wide = features // devices
+    lines = D // (devices * depth)
+    net = Links(sends, recvs)
+    mine_at = at_rows(core * half, half)
+    other_at = at_rows((1 - core) * half, half)
+    chunk = 32
+
+    loads = []
+
+    def load(source, target):
+        made = pltpu.make_async_copy(source, target, local_sems.at[len(loads)])
+        made.start()
+        loads.append(made)
+
+    where = [2 * flip(chip, mask) + core for mask in range(chips)]
+    for mask in range(chips):
+        for kind in range(3):
+            start = pl.multiple_of(kind * D + where[mask] * block, block)
+            load(
+                w_qkv.at[:, pl.ds(start, block)],
+                wqkv.at[:, (3 * mask + kind) * block : (3 * mask + kind + 1) * block],
+            )
+    n_qkv = len(loads)
+    for mask in range(chips):
+        start = pl.multiple_of(where[mask] * block, block)
+        load(w_out.at[pl.ds(start, block), :], wo.at[mask * block : (mask + 1) * block, :])
+    n_out = len(loads)
+    for mask in range(chips):
+        start = pl.multiple_of(where[mask] * wide, wide)
+        load(w_in.at[:, pl.ds(start, wide)], w_up.at[:, mask * wide : (mask + 1) * wide])
+    n_up = len(loads)
+    for mask in range(chips):
+        start = pl.multiple_of(where[mask] * wide, wide)
+        load(w_fc2.at[pl.ds(start, wide), :], w_down.at[mask * wide : (mask + 1) * wide, :])
+
+    barrier = pltpu.get_barrier_semaphore()
+    friends = [(flip(me, mask), slot) for mask in range(1, devices)]
+    for shift in range(1, depth):
+        far = lax.rem(slot + shift, depth)
+        friends += [(me, far), (flip(me, 1), far)]
+    for friend in friends:
+        pl.semaphore_signal(barrier, inc=1, device_id=friend, device_id_type=MESH)
+    pl.semaphore_wait(barrier, len(friends))
+
+    def spread(source, target):
+        waits = []
+        for step in range(2):
+            pick = lax.rem(slot + step, 2)
+            upper = lax.div(slot, 2)
+            place = 2 * core + pick
+            here = jnp.logical_and(upper == core, place == slot)
+            waits.append(
+                net.send_or_keep(
+                    here,
+                    source.at[pick],
+                    target.at[at_rows((2 * upper + step) * piece, piece)],
+                    (base + upper, place),
+                )
+            )
+        return waits
+
+    def pass_on(waits, target):
+        made = []
+        for step, wait in enumerate(waits):
+            wait()
+            spot = target.at[at_rows((2 * core + step) * piece, piece)]
+            made.append(net.send(spot, spot, peer))
+        return made
+
+    token_waits = spread(tokens, x_all)
+    grad_waits = spread(out_grad, g_rows)
+    lens_copy = net.send(lens, lens_peer, peer)
+    vec_s[...] = jnp.zeros_like(vec_s)
+    token_passes = pass_on(token_waits, x_all)
+
+    def plane_start(target):
+        source = target.at[mine_at]
+        return [
+            net.send(
+                source, target.at[at_rows(mask * rows + core * half, half)], (flip(me, 2 * mask), slot)
+            )
+            for mask in range(1, chips)
+        ]
+
+    def plane_pass(copies, target):
+        made = []
+        for mask, copy in enumerate(copies, 1):
+            copy.wait_recv()
+            spot = target.at[at_rows(mask * rows + core * half, half)]
+            made.append(net.send(spot, spot, peer))
+        return made
+
+    x_plane = plane_start(x_all)
+    for made in loads[:n_qkv]:
+        made.wait()
+    lens_copy.wait_recv()
+    for made in token_passes:
+        made.wait_recv()
+    owned = jnp.where(lax.div(slot, 2) == core, lens[...], lens_peer[...])
+    length = jnp.where(lax.rem(slot, 2) == 0, owned[0:1, 0:1], owned[1:2, 0:1])
+    live = positions(1, (1, rows), slot, piece) < length
+    lane = lax.broadcasted_iota(jnp.int32, (1, block), 1)
+
+    @pl.loop(0, chips)
+    def _(mask):
+        spot = 2 * flip_traced(chip, mask, chips) + core
+        lanes = pl.ds(pl.multiple_of(spot * block, block), block)
+        joined = dot(x_all[0:rows, :], wqkv[:, pl.ds(pl.multiple_of(mask * 3 * block, block), 3 * block)])
+        queries = ((joined[:, 0:block] + vec[0:1, lanes]) * 0.125).astype(BF16)
+        keys = joined[:, block : 2 * block].astype(BF16)
+        values = (joined[:, 2 * block :] + vec[1:2, lanes]).astype(BF16)
+        total = jnp.zeros((rows, block), F32)
+        for head in range(block // HD):
+            mine = lax.div(lane, HD) == head
+            probs = head_probs(jnp.where(mine, queries, jnp.zeros_like(queries)), keys, live)
+            total = jnp.where(mine, dot(probs.astype(BF16), values), total)
+        start = pl.multiple_of(mask * 3 * block, block)
+        qkv[:, pl.ds(start, block)] = queries
+        qkv[:, pl.ds(pl.multiple_of(start + block, block), block)] = keys
+        qkv[:, pl.ds(pl.multiple_of(start + 2 * block, block), block)] = values
+        mixed[:, pl.ds(pl.multiple_of(mask * block, block), block)] = total.astype(BF16)
+
+    for made in loads[n_qkv:n_out]:
+        made.wait()
+
+    def exchange(compute, target, before):
+        made = []
+        for number, at in enumerate((other_at, mine_at)):
+            if before is not None:
+                before[number].wait_send()
+            part[at, :] = compute(at)
+            made.append(net.copy(part.at[at], target.at[at], peer))
+            made[-1].start()
+        return made
+
+    first = exchange(lambda at: dot(mixed[at, :], wo[...]), part_a, None)
+    grad_passes = pass_on(grad_waits, g_rows)
+
+    def norm_one(start):
+        @pl.loop(0, half // chunk)
+        def _(step):
+            at = pl.ds(pl.multiple_of(start + step * chunk, chunk), chunk)
+            total = x_all[at, :].astype(F32) + (part[at, :] + part_a[at, :]) + vec[2:3, :]
+            center, scale = layer_norm_stats(total)
+            summed[at, :] = total
+            n_all[at, :] = (center * scale * vec[8:9, :] + vec[9:10, :]).astype(BF16)
+
+    first[0].wait_recv()
+    norm_one(core * half)
+    n_plane = plane_start(n_all)
+    first[1].wait_recv()
+    norm_one((1 - core) * half)
+    for made in loads[n_out:]:
+        made.wait()
+
+    def bias_of(mask):
+        spot = flip_traced(chip, mask, chips)
+        lanes = pl.ds(pl.multiple_of(core * wide, wide), wide)
+        result = vec[3:4, lanes]
+        for row in range(1, chips):
+            result = jnp.where(spot == row, vec[3 + row : 4 + row, lanes], result)
+        return result
+
+    @pl.loop(0, chips)
+    def _(mask):
+        at = pl.ds(pl.multiple_of(mask * wide, wide), wide)
+        value = dot(n_all[0:rows, :], w_up[:, at]) + bias_of(mask)
+        pre_s[:, at] = value
+        hid[:, at] = (value * normal_cdf(value)).astype(BF16)
+
+    second = exchange(lambda at: dot(hid[at, :], w_down[...]), part_b, first)
+    for made in grad_passes:
+        made.wait_recv()
+
+    def norm_two(start, own):
+        @pl.loop(0, half // chunk)
+        def _(step):
+            begin = pl.multiple_of(start + step * chunk, chunk)
+            at = pl.ds(begin, chunk)
+            center, scale = layer_norm_stats(summed[at, :])
+            normed = center * scale * vec[8:9, :] + vec[9:10, :]
+            center, scale = layer_norm_stats(normed + (part[at, :] + part_b[at, :]) + vec[7:8, :])
+            place = begin + lax.broadcasted_iota(jnp.int32, (chunk, 1), 0)
+            piece_of = lax.div(place, piece)
+            spot = 2 * lax.div(piece_of, 2) + lax.rem(slot + lax.rem(piece_of, 2), 2)
+            valid = (spot * piece + lax.rem(place, piece) < length).astype(F32)
+            unit = center * scale
+            error = g_rows[at, :].astype(F32) * valid
+            grad = layer_norm_back(center, scale, vec[10:11, :], error)
+            grad_two[at, :] = grad
+            low = grad.astype(BF16)
+            g_all[at, :] = low
+            if own:
+                out_half[pl.ds(pl.multiple_of(step * chunk, chunk), chunk), :] = (
+                    valid * (unit * vec[10:11, :] + vec[11:12, :])
+                ).astype(BF16)
+                vec_s[7:8, :] += jnp.sum(low.astype(F32), axis=0, keepdims=True)
+                vec_s[10:11, :] += jnp.sum(error * unit, axis=0, keepdims=True)
+                vec_s[11:12, :] += jnp.sum(error, axis=0, keepdims=True)
+
+    def go_back(source, target):
+        waits = []
+        for step in range(2):
+            place = 2 * core + lax.rem(slot + step, 2)
+            upper = lax.div(slot, 2)
+            here = jnp.logical_and(upper == core, place == slot)
+            waits.append(
+                net.send_or_keep(
+                    here,
+                    source.at[step * piece : (step + 1) * piece],
+                    target.at[lax.rem(slot, 2)],
+                    (base + upper, place),
+                )
+            )
+        return waits
+
+    second[0].wait_recv()
+    norm_two(core * half, True)
+    g_plane = plane_start(g_all)
+    second[1].wait_recv()
+    norm_two((1 - core) * half, False)
+    out_waits = go_back(out_half, out_got)
+    n_pass = plane_pass(n_plane, n_all)
+    x_pass = plane_pass(x_plane, x_all)
+
+    def slope_of(value, cdf):
+        return cdf + value * (jnp.exp(-0.5 * value * value) * 0.3989422804014327)
+
+    @pl.loop(0, chips)
+    def _(mask):
+        at = pl.ds(pl.multiple_of(mask * wide, wide), wide)
+        value = pre_s[:, at]
+        grad = through(g_all[0:rows, :], w_down[at, :])
+        hid[:, at] = (grad * slope_of(value, normal_cdf(value))).astype(BF16)
+
+    third = exchange(lambda at: through(hid[at, :], w_up[...]), part_c, second)
+
+    def norm_one_back(start, own):
+        @pl.loop(0, half // chunk)
+        def _(step):
+            at = pl.ds(pl.multiple_of(start + step * chunk, chunk), chunk)
+            center, scale = layer_norm_stats(summed[at, :])
+            error = grad_two[at, :] + (part[at, :] + part_c[at, :])
+            grad = layer_norm_back(center, scale, vec[8:9, :], error)
+            low = grad.astype(BF16)
+            b_all[at, :] = low
+            grad_one[at, :] = grad
+            if own:
+                vec_s[2:3, :] += jnp.sum(low.astype(F32), axis=0, keepdims=True)
+                vec_s[8:9, :] += jnp.sum(error * (center * scale), axis=0, keepdims=True)
+                vec_s[9:10, :] += jnp.sum(error, axis=0, keepdims=True)
+
+    third[0].wait_recv()
+    norm_one_back(core * half, True)
+    b_plane = plane_start(b_all)
+    third[1].wait_recv()
+    norm_one_back((1 - core) * half, False)
+    g_pass = plane_pass(g_plane, g_all)
+
+    bias_mine = bias_of(0)
+
+    def feed_rows(mask):
+        at = slice(mask * rows, (mask + 1) * rows)
+        value = dot(n_all[at, :], w_up[:, 0:wide]) + bias_mine
+        cdf = normal_cdf(value)
+        hid_all[at, :] = (value * cdf).astype(BF16)
+        low = (through(g_all[at, :], w_down[0:wide, :]) * slope_of(value, cdf)).astype(BF16)
+        gp_all[at, :] = low
+        return jnp.sum(low.astype(F32), axis=0, keepdims=True)
+
+    bias_sum = feed_rows(0)
+    for mask in range(1, chips):
+        n_pass[mask - 1].wait_recv()
+        g_pass[mask - 1].wait_recv()
+        bias_sum = bias_sum + feed_rows(mask)
+    lanes = pl.ds(pl.multiple_of(core * wide, wide), wide)
+    for row in range(chips):
+        vec_s[3 + row : 4 + row, lanes] = jnp.where(chip == row, bias_sum, jnp.zeros_like(bias_sum))
+    down_rows = wide // depth
+    packs = D // wide
+    per_pack = devices // packs
+    span = lines * depth
+    down = inner(hid_all[...], g_all[...]).astype(BF16)
+    for number in range(depth):
+        packed[number, 0:down_rows, :] = down[number * down_rows : (number + 1) * down_rows, :]
+    for group in range(devices):
+        up = inner(n_all[:, group * span : (group + 1) * span], gp_all[...]).astype(BF16)
+        row = down_rows + (group % per_pack) * lines
+        col = (group // per_pack) * wide
+        for number in range(depth):
+            packed[number, row : row + lines, col : col + wide] = up[
+                number * lines : (number + 1) * lines, :
+            ]
+
+    class Line:
+        def __init__(self, chunks, from_left, from_right):
+            self.chunks, self.from_left, self.from_right = chunks, from_left, from_right
+            self.up, self.down, self.first_up, self.first_down = [], [], [], []
+            after = (me, lax.rem(slot + 1, depth))
+            before = (me, lax.rem(slot + depth - 1, depth))
+            for order in range(depth - 1):
+                top, low = depth - 1 - order, order
+                spot = from_left.at[order]
+                self.up.append(net.copy(spot, spot, after))
+                self.first_up.append(net.again(chunks.at[top], spot, after))
+                net.open.append((self.up[-1], slot < top))
+                spot = from_right.at[order]
+                self.down.append(net.copy(spot, spot, before))
+                self.first_down.append(net.again(chunks.at[low], spot, before))
+                net.open.append((self.down[-1], slot > low))
+
+        def first(self):
+            for order in range(depth - 1):
+                pl.when(slot == 0)(self.first_up[order].start)
+                pl.when(slot == depth - 1)(self.first_down[order].start)
+
+        def stage(self, order):
+            top, low = depth - 1 - order, order
+
+            @pl.when(jnp.logical_and(slot >= 1, slot <= top))
+            def _():
+                self.up[order].wait_recv()
+
+            @pl.when(jnp.logical_and(slot >= 1, slot < top))
+            def _():
+                self.from_left[order] = (
+                    self.from_left[order].astype(F32) + self.chunks[top].astype(F32)
+                ).astype(BF16)
+                self.up[order].start()
+
+            @pl.when(jnp.logical_and(slot <= depth - 2, slot >= low))
+            def _():
+                self.down[order].wait_recv()
+
+            @pl.when(jnp.logical_and(slot <= depth - 2, slot > low))
+            def _():
+                self.from_right[order] = (
+                    self.from_right[order].astype(F32) + self.chunks[low].astype(F32)
+                ).astype(BF16)
+                self.down[order].start()
+
+    feed_line = Line(packed, right, left)
+    feed_line.first()
+
+    grad_parts = range(1, chips)
+
+    def attention_back(mask):
+        start = mask * 3 * block
+        queries = qkv[:, start : start + block]
+        keys = qkv[:, start + block : start + 2 * block]
+        values = qkv[:, start + 2 * block : start + 3 * block]
+        grad_mixed = through(b_all[0:rows, :], wo[mask * block : (mask + 1) * block, :]).astype(BF16)
+        grad_q = jnp.zeros((rows, block), F32)
+        grad_k = grad_q
+        grad_v = grad_q
+        for head in range(block // HD):
+            mine = lax.div(lane, HD) == head
+            probs = head_probs(jnp.where(mine, queries, jnp.zeros_like(queries)), keys, live)
+            grad_probs = through(jnp.where(mine, grad_mixed, jnp.zeros_like(grad_mixed)), values)
+            dsum = jnp.sum(probs * grad_probs, axis=-1, keepdims=True)
+            grad_scores = (probs * (grad_probs - dsum)).astype(BF16)
+            grad_q = jnp.where(mine, dot(grad_scores, keys), grad_q)
+            grad_k = jnp.where(mine, inner(grad_scores, queries), grad_k)
+            grad_v = jnp.where(mine, inner(probs.astype(BF16), grad_mixed), grad_v)
+        grad_q = grad_q.astype(BF16) * jnp.bfloat16(0.125)
+        grad_k = grad_k.astype(BF16)
+        grad_v = grad_v.astype(BF16)
+        spot = pl.ds(pl.multiple_of(where[mask] * block, block), block)
+        vec_s[0:1, spot] = jnp.sum(grad_q.astype(F32), axis=0, keepdims=True)
+        vec_s[1:2, spot] = jnp.sum(grad_v.astype(F32), axis=0, keepdims=True)
+        dqkv[:, start : start + block] = grad_q
+        dqkv[:, start + block : start + 2 * block] = grad_k
+        dqkv[:, start + 2 * block : start + 3 * block] = grad_v
+        if mask:
+            joint = j_send.at[mask - 1]
+        else:
+            joint = j_all.at[0:rows]
+        joint[:, 0:block] = grad_q
+        joint[:, block : 2 * block] = grad_k
+        joint[:, 2 * block : 3 * block] = grad_v
+        joint[:, 3 * block : 4 * block] = mixed[:, mask * block : (mask + 1) * block]
+        if mask:
+            return net.send(
+                joint, j_all.at[mask * rows : (mask + 1) * rows], (flip(me, 2 * mask), slot)
+            )
+        return None
+
+    j_copies = [attention_back(mask) for mask in grad_parts]
+    attention_back(0)
+    feed_line.stage(0)
+    b_pass = plane_pass(b_plane, b_all)
+    for made in third:
+        made.wait_send()
+    part[0:half, :] = through(dqkv[other_at, :], wqkv[...])
+    tg_copy = net.copy(part.at[0:half], part_d, peer)
+    tg_copy.start()
+    part[half:rows, :] = grad_one[mine_at, :] + through(dqkv[mine_at, :], wqkv[...])
+    tg_copy.wait_recv()
+    tg_half[...] = (part[half:rows, :] + part_d[...]).astype(BF16)
+    tg_waits = go_back(tg_half, tg_got)
+
+    for made in b_pass + x_pass + j_copies:
+        made.wait_recv()
+    across = inner(j_all[:, 3 * block : 4 * block], b_all[...]).astype(BF16)
+    for group in range(devices):
+        both = inner(x_all[:, group * span : (group + 1) * span], j_all[:, 0 : 3 * block]).astype(BF16)
+        row = group * lines
+        for number in range(depth):
+            at = slice(number * lines, (number + 1) * lines)
+            packed_two[number, row : row + lines, 0 : 3 * block] = both[at, :]
+            packed_two[number, row : row + lines, 3 * block : 4 * block] = across[
+                at, group * block : (group + 1) * block
+            ]
+    input_line = Line(packed_two, right_two, left_two)
+    input_line.first()
+
+    hops = []
+    bit = 1
+    while bit < devices:
+        hops.append((flip(me, bit), slot))
+        bit *= 2
+    bit = 1
+    while bit < depth:
+        hops.append((me, flip(slot, bit)))
+        bit *= 2
+
+    def vector_hop(number):
+        made = net.copy(vec_s, vec_got.at[number], hops[number])
+        made.start()
+        made.wait()
+        vec_s[...] += vec_got[number]
+
+    def finish(line, target, rows_at):
+        target[...] = line.chunks[slot, rows_at, :].astype(F32)
+
+        @pl.when(slot >= 1)
+        def _():
+            target[...] += line.from_left[depth - 1 - slot, rows_at, :].astype(F32)
+
+        @pl.when(slot <= depth - 2)
+        def _():
+            target[...] += line.from_right[slot, rows_at, :].astype(F32)
+
+    vector_hop(0)
+    feed_line.stage(1)
+    vector_hop(1)
+    vector_hop(2)
+    feed_line.stage(2)
+    finish(feed_line, g_fc2, slice(0, down_rows))
+    low_part = part_d.at[0:down_rows]
+    finish(feed_line, low_part, slice(down_rows, 2 * down_rows))
+    for group in range(devices):
+        row = (group % per_pack) * lines
+        col = (group // per_pack) * wide
+        trade_in[group] = low_part[row : row + lines, col : col + wide].astype(BF16)
+
+    def trade(source, target):
+        return [
+            net.send(source.at[flip(me, mask)], target.at[me], (flip(me, mask), slot))
+            for mask in range(1, devices)
+        ]
+
+    in_copies = trade(trade_in, got_in)
+    input_line.stage(0)
+    vector_hop(3)
+    input_line.stage(1)
+    vector_hop(4)
+    for made in in_copies:
+        made.wait_recv()
+    got_in[me] = trade_in[me]
+    for group in range(devices):
+        g_in[:, group * wide : (group + 1) * wide] = got_in[group].astype(F32)
+    g_vec[...] = vec_s[0 : g_vec.shape[0], :]
+    for wait in out_waits + tg_waits:
+        wait()
+    out_ref[...] = out_got[...]
+    tgrad_ref[...] = tg_got[...]
+    input_line.stage(2)
+    tg_copy.wait_send()
+    total = part.at[0 : 2 * half, 0 : 4 * block]
+    finish(input_line, total, slice(0, rows))
+    for group in range(devices):
+        trade_qkv[group] = total[group * lines : (group + 1) * lines, 0 : 3 * block].astype(BF16)
+        g_out[:, group * block : (group + 1) * block] = total[
+            group * lines : (group + 1) * lines, 3 * block : 4 * block
+        ]
+    for made in trade(trade_qkv, got_qkv):
+        made.wait_recv()
+    got_qkv[me] = trade_qkv[me]
+    for group in range(devices):
+        for kind in range(3):
+            g_qkv[:, kind * D + group * block : kind * D + (group + 1) * block] = got_qkv[
+                group, :, kind * block : (kind + 1) * block
+            ].astype(F32)
+    net.close()
+
+
+def slot_body(tokens, out_grad, lengths, w_qkv, w_out, w_in, w_fc2, vectors, moment_one, moment_two):
+    slots, piece, width = tokens.shape
+    devices, depth = lax.axis_size("dp"), lax.axis_size("ctx")
+    chips = devices // 2
+    count = devices * depth
+    features = w_in.shape[1]
+    half = 2 * piece
+    rows = 2 * half
+    block = D // devices
+    wide = features // devices
+    lines = D // count
+    total = rows * chips
+    hops = (devices.bit_length() - 1) + (depth.bit_length() - 1)
+    lens = jnp.broadcast_to(lengths[:, None], (slots, 128))
+    low = lambda *shape: pltpu.VMEM(shape, BF16)
+    wide_f32 = lambda *shape: pltpu.VMEM(shape, F32)
+    anywhere = pl.BlockSpec(memory_space=pl.ANY)
+    inside = pl.BlockSpec(memory_space=pltpu.VMEM)
+    copies = 96
+    out, tokens_grad, grad_qkv, grad_out_w, grad_in, grad_fc2, vector_grad = pl.pallas_call(
+        partial(slot_kernel, devices, depth, features),
+        out_shape=(
+            jax.ShapeDtypeStruct(tokens.shape, BF16),
+            jax.ShapeDtypeStruct(tokens.shape, BF16),
+            jax.ShapeDtypeStruct((lines, 3 * D), F32),
+            jax.ShapeDtypeStruct((lines, D), F32),
+            jax.ShapeDtypeStruct((lines, features), F32),
+            jax.ShapeDtypeStruct((features // count, D), F32),
+            jax.ShapeDtypeStruct(vectors.shape, F32),
+        ),
+        in_specs=[anywhere, anywhere, inside, inside] + [anywhere] * 4,
+        out_specs=(inside,) * 7,
+        scratch_shapes=[
+            low(D, 3 * D // 2),
+            low(D // 2, D),
+            low(D, features // 2),
+            low(features // 2, D),
+            low(total, D),
+            low(total, D),
+            low(total, D),
+            low(total, D),
+            low(total, 4 * block),
+            low(chips - 1, rows, 4 * block),
+            low(rows, D),
+            pltpu.VMEM((slots, 128), jnp.int32),
+            low(rows, 3 * D // 2),
+            low(rows, D // 2),
+            wide_f32(rows, D),
+            wide_f32(rows, D),
+            wide_f32(rows, D),
+            wide_f32(rows, D),
+            wide_f32(half, D),
+            wide_f32(rows, D),
+            wide_f32(rows, D),
+            wide_f32(rows, D),
+            wide_f32(rows, features // 2),
+            low(rows, features // 2),
+            low(total, wide),
+            low(total, wide),
+            low(depth, 2 * wide // depth, D),
+            low(depth - 1, 2 * wide // depth, D),
+            low(depth - 1, 2 * wide // depth, D),
+            low(depth, devices * lines, 4 * block),
+            low(depth - 1, devices * lines, 4 * block),
+            low(depth - 1, devices * lines, 4 * block),
+            low(devices, lines, wide),
+            low(devices, lines, wide),
+            low(devices, lines, 3 * block),
+            low(devices, lines, 3 * block),
+            wide_f32(16, D),
+            wide_f32(hops, 16, D),
+            low(rows, 3 * D // 2),
+            low(half, D),
+            low(*tokens.shape),
+            low(half, D),
+            low(*tokens.shape),
+            pltpu.SemaphoreType.DMA((6 * chips,)),
+            pltpu.SemaphoreType.DMA((copies,)),
+            pltpu.SemaphoreType.DMA((copies,)),
+        ],
+        compiler_params=pltpu.CompilerParams(
+            collective_id=0, has_side_effects=True, vmem_limit_bytes=64 * 1024 * 1024 - 64 * 1024
+        ),
+        name="slot",
+    )(tokens, out_grad, lens, vectors, w_qkv, w_out, w_in, w_fc2)
+    index = lax.axis_index("dp") * depth + lax.axis_index("ctx")
+    own_vectors = lax.dynamic_slice_in_dim(vector_grad.reshape(count, -1), index, 1, 0)
+    grad_rows = jnp.concatenate(
+        [value.reshape(1, -1) for value in (grad_qkv, grad_out_w, grad_in, grad_fc2, own_vectors)],
+        axis=1,
+    )
+    return (out, tokens_grad) + update(
+        grad_rows, index, count, (w_qkv, w_out, w_in, w_fc2, vectors), moment_one, moment_two
+    )
+
+
+def update(grad_rows, index, count, weights, moment_one, moment_two):
+    pieces = []
+    for weight in weights:
+        if weight.shape[0] % count == 0:
+            lines = weight.shape[0] // count
+            piece = lax.dynamic_slice_in_dim(weight, index * lines, lines, 0)
+        else:
+            piece = lax.dynamic_slice_in_dim(weight.reshape(count, -1), index, 1, 0)
+        pieces.append(piece.reshape(1, -1).astype(F32))
+    params = jnp.concatenate(pieces, axis=1)
+    new_one = beta_one * moment_one + (1.0 - beta_one) * grad_rows
+    new_two = beta_two * moment_two + (1.0 - beta_two) * grad_rows * grad_rows
+    fix_one = 1.0 - beta_one**step_count
+    fix_two = 1.0 - beta_two**step_count
+    change = new_one / fix_one / (jnp.sqrt(new_two / fix_two) + adam_eps)
+    new_params = params - learn_rate * (change + decay_rate * params)
+    return (grad_rows, new_params, new_one, new_two)
+
+
+def layer(tokens, *rest):
+    slots, piece, width = tokens.shape
+    devices, depth = lax.axis_size("dp"), lax.axis_size("ctx")
+    fits = slots == 2 and depth == 2 * slots and devices % 2 == 0
+    if fits and (H * HD // devices) % 128 == 0 and (FF // devices) % 128 == 0:
+        return slot_body(tokens, *rest)
+    return body(tokens, *rest)
+
+
 def solution(mesh):
     placed = (
         P("dp", "ctx", None),
@@ -313,7 +1079,7 @@
         P(("dp", "ctx"), None),
     )
     return jax.shard_map(
-        body,
+        layer,
         mesh=mesh,
         in_specs=placed,
         out_specs=(

time: 1140 us -> 209 us (0.18)
  waiting for transfers between devices: 758 us -> 0 us
  local copies, waits for them, and re-layouts: 197 us -> 16.2 us
  Pallas kernels: 0 us -> 176 us
  matrix products: 127 us -> 0 us
  other arithmetic: 31.5 us -> 16.1 us
  between operations: 14.9 us -> 0.79 us
    unnamed x8 -> x0, waiting for transfers between devices: 710 us -> none
    pallas_call x0 -> x1, Pallas kernels: none -> 176 us  [slot_body(): pl.pallas_call(partial(slot_kernel, devices, depth, features), out_shape=...]
    dot_general x87 -> x0, matrix products: 124 us -> none  [the longest x16 31.1 us: attend_one_block(): jnp.einsum('hqk,khd->qhd', probs_low, value_heads, preferred_element_type...]
    all_gather x4 -> x0, waiting for transfers between devices: 48.3 us -> none  [the longest x2 31.6 us: body(): lax.all_gather(keys.reshape(slots, piece, width), 'ctx', axis=1, tiled=True)]
    another operation x7 -> x0, local copies, waits for them, and re-layouts: 41.8 us -> none  [the longest x4 39.6 us: shard_piece(): return block.reshape(number, per_shard)]
    reshape x19 -> x2, local copies, waits for them, and re-layouts: 37.6 us -> 2.38 us  [the longest x1 1.47 us: update(): piece = lax.dynamic_slice_in_dim(weight.reshape(count, -1), index, 1, 0)]
    unnamed x102 -> x30, local copies, waits for them, and re-layouts: 38.4 us -> 11.1 us
    while x76 -> x0, local copies, waits for them, and re-layouts: 24.3 us -> none
  transfers between devices with their start and end apart: 7 -> 0, of which waited for: 4 -> 0; matrix products, arithmetic and copies ran while one was open for 14% -> 0% of each run, Pallas kernels for 0% -> 0%
where the time goes in v2:
time: 209 us
  Pallas kernels  176 us (84%)
  local copies, waits for them, and re-layouts  16.2 us (8%)
  other arithmetic  16.1 us (8%)
    pallas_call x1, Pallas kernels, slot_body(): pl.pallas_call(partial(slot_kernel, devices, depth, features), out_shape=...  176 us
    sub x1, other arithmetic, update(): new_params = params - learn_rate * (change + decay_rate * params)  12.3 us
    unnamed x30, local copies, waits for them, and re-layouts  11.1 us

profile of v2, /device:TPU:0, one launch (start us, length us, event | category | flops | bytes accessed | tf_op | source)
XLA Modules:
  0.0 208.8 jit_solution(9266323353663545974)
XLA Ops:
  0.6 1.3 broadcast_in_dim.2.refs_2_
  1.9 1.5 reshape.424
  3.4 0.8 convert_bitcast_fusion.3
  4.4 1.0 convert_bitcast_fusion.2
  5.4 0.4 copy.20
  5.8 1.0 convert_bitcast_fusion.1
  6.8 0.5 copy.22
  7.3 1.0 convert_bitcast_fusion
  8.3 0.5 copy.23
  8.9 0.8 constant_dynamic-update-slice_fusion.9
  9.6 0.7 constant_dynamic-update-slice_fusion.8
  10.3 0.8 constant_dynamic-update-slice_fusion.7
  11.1 0.8 constant_dynamic-update-slice_fusion.6
  12.0 175.7 %slot.1 = (bf16[2,64,1024]{2,1,0:T(8,128)(2,1)}, bf16[2,64,1024]{2,1,0:T(8,128)(2,1)}, f32[32,3072]{1,0:T(8,128)}, f32[32,1024]{1,0:T(8,128)}, f32[32,4096]{1,0:...) custom-call(bf16[2,64,1024]{2,1,0:T(8,128)(2,1)} %refs_0_.1, bf16[2,64,1024]{2,1,0:T(8,128)(2,1)} %refs_1_.1, ...), custom_call_target="tpu_custom_call" | custom-call | tf_op jit(solution)/shard_map/slot/pallas_call | solution.py:963
  187.6 0.9 reshape.423
  188.6 1.0 copy.17
  189.6 1.4 copy.16
  191.0 1.6 copy.18
  192.6 0.5 copy.19
  193.4 1.4 constant_dynamic-update-slice_fusion
  194.8 0.2 copy-done.2
  195.1 12.3 %multiply_subtract_fusion = (f32[1,393600]{1,0:T(1,128)}, f32[1,393600]{1,0:T(1,128)}, f32[1,393600]{1,0:T(1,128)}) fusion(f32[1,393600]{1,0:T(1,128)} %get-tuple-element.24, f32[1,393600]{1,0:T(1,128)S(1)} %get-tuple-element.33, f32[1,393600]{1,0:T(1,128)S(1)} %copy-done.1, f32[1,393600]{1,0:T(1,128)S(1)} %copy-done.2), kind=kLoop, calls=%fused_computation.2 | loop fusion | flops 5904000 | bytes 11020800 | tf_op jit(solution)/shard_map/sub | solution.py:1055
  207.4 0.7 copy.34
  208.1 0.7 copy.35
  (16 shorter events, 0.3 us)
Async XLA Ops:
  187.6 5.0 %copy-start.3 = (f32[128,1024]{1,0:T(8,128)S(1)}, f32[128,1024]{1,0:T(8,128)}, u32[]{:S(2)}) copy-start(f32[128,1024]{1,0:T(8,128)} %get-tuple-element.18) | copy-start | bytes 1572868
  193.1 1.7 copy-start.1
  193.2 1.9 copy-start.2
  194.8 12.6 %copy-start = (f32[1,393600]{1,0:T(1,128)}, f32[1,393600]{1,0:T(1,128)S(1)}, u32[]{:S(2)}) copy-start(f32[1,393600]{1,0:T(1,128)S(1)} %get-tuple-element.33) | copy-start | bytes 4723204
  195.1 12.3 %copy-start.5 = (bf16[2,64,1024]{2,1,0:T(8,128)(2,1)S(1)}, bf16[2,64,1024]{2,1,0:T(8,128)(2,1)}, u32[]{:S(2)}) copy-start(bf16[2,64,1024]{2,1,0:T(8,128)(2,1)} %get-tuple-element.31) | copy-start | bytes 786436
  195.1 13.0 %copy-start.4 = (bf16[2,64,1024]{2,1,0:T(8,128)(2,1)S(1)}, bf16[2,64,1024]{2,1,0:T(8,128)(2,1)}, u32[]{:S(2)}) copy-start(bf16[2,64,1024]{2,1,0:T(8,128)(2,1)} %get-tuple-element.32) | copy-start | bytes 786436

commit v3 on v2

--- a/solution.py
+++ b/solution.py
@@ -426,13 +426,13 @@
 
 def slot_kernel(devices, depth, features, *refs):
     (
-        tokens, out_grad, lens, vec, w_qkv, w_out, w_in, w_fc2,
+        tokens, out_grad, lengths, vec, w_qkv, w_out, w_in, w_fc2,
         out_ref, tgrad_ref, g_qkv, g_out, g_in, g_fc2, g_vec,
         wqkv, wo, w_up, w_down,
         x_all, n_all, g_all, b_all, j_all, j_send, g_rows, lens_peer,
         qkv, mixed, part, part_a, part_b, part_c, part_d, summed, grad_two, grad_one,
         pre_s, hid, hid_all, gp_all, packed, right, left, packed_two, right_two, left_two,
-        trade_in, got_in, trade_qkv, got_qkv, vec_s, vec_got, dqkv, out_half, out_got, tg_half, tg_got,
+        trade_in, got_in, trade_qkv, got_qkv, vec_s, vec_by, sums, dqkv, out_half, out_got, tg_half, tg_got, lens,
         local_sems, sends, recvs,
     ) = refs
     chips = devices // 2
@@ -451,6 +451,9 @@
     other_at = at_rows((1 - core) * half, half)
     chunk = 32
 
+    row_of = lax.broadcasted_iota(jnp.int32, lens.shape, 0)
+    lens[...] = jnp.where(row_of == 0, lengths[0], lengths[1])
+    vec_s[...] = jnp.zeros_like(vec_s)
     loads = []
 
     def load(source, target):
@@ -516,7 +519,6 @@
     token_waits = spread(tokens, x_all)
     grad_waits = spread(out_grad, g_rows)
     lens_copy = net.send(lens, lens_peer, peer)
-    vec_s[...] = jnp.zeros_like(vec_s)
     token_passes = pass_on(token_waits, x_all)
 
     def plane_start(target):
@@ -760,30 +762,27 @@
                 pl.when(slot == 0)(self.first_up[order].start)
                 pl.when(slot == depth - 1)(self.first_down[order].start)
 
-        def stage(self, order):
-            top, low = depth - 1 - order, order
-
-            @pl.when(jnp.logical_and(slot >= 1, slot <= top))
-            def _():
-                self.up[order].wait_recv()
-
-            @pl.when(jnp.logical_and(slot >= 1, slot < top))
-            def _():
-                self.from_left[order] = (
-                    self.from_left[order].astype(F32) + self.chunks[top].astype(F32)
-                ).astype(BF16)
-                self.up[order].start()
-
-            @pl.when(jnp.logical_and(slot <= depth - 2, slot >= low))
-            def _():
-                self.down[order].wait_recv()
-
-            @pl.when(jnp.logical_and(slot <= depth - 2, slot > low))
-            def _():
-                self.from_right[order] = (
-                    self.from_right[order].astype(F32) + self.chunks[low].astype(F32)
-                ).astype(BF16)
-                self.down[order].start()
+        def stage(self, time):
+            for order in range(time):
+                top, low = depth - 1 - order, order
+
+                @pl.when(slot == time - order)
+                def _(order=order, top=top):
+                    self.up[order].wait_recv()
+                    if time < depth - 1:
+                        self.from_left[order] = (
+                            self.from_left[order].astype(F32) + self.chunks[top].astype(F32)
+                        ).astype(BF16)
+                        self.up[order].start()
+
+                @pl.when(depth - 1 - slot == time - order)
+                def _(order=order, low=low):
+                    self.down[order].wait_recv()
+                    if time < depth - 1:
+                        self.from_right[order] = (
+                            self.from_right[order].astype(F32) + self.chunks[low].astype(F32)
+                        ).astype(BF16)
+                        self.down[order].start()
 
     feed_line = Line(packed, right, left)
     feed_line.first()
@@ -833,7 +832,6 @@
 
     j_copies = [attention_back(mask) for mask in grad_parts]
     attention_back(0)
-    feed_line.stage(0)
     b_pass = plane_pass(b_plane, b_all)
     for made in third:
         made.wait_send()
@@ -843,7 +841,21 @@
     part[half:rows, :] = grad_one[mine_at, :] + through(dqkv[mine_at, :], wqkv[...])
     tg_copy.wait_recv()
     tg_half[...] = (part[half:rows, :] + part_d[...]).astype(BF16)
+    feed_line.stage(1)
     tg_waits = go_back(tg_half, tg_got)
+
+    tiles = vec.shape[0] * D // 128
+    share = tiles // (devices * depth)
+    vec_by[...] = jnp.zeros_like(vec_by)
+    for tile in range(tiles):
+        owner, lane_group = tile // share, tile % share
+        row, col = tile // (D // 128), (tile % (D // 128)) * 128
+        spot = (owner % depth) * 16 + owner // depth
+        vec_by[spot : spot + 1, lane_group * 128 : (lane_group + 1) * 128] = vec_s[
+            row : row + 1, col : col + 128
+        ]
+    for number in range(depth):
+        packed_two[number, rows : rows + 16, :] = vec_by[number * 16 : (number + 1) * 16, :].astype(BF16)
 
     for made in b_pass + x_pass + j_copies:
         made.wait_recv()
@@ -860,22 +872,6 @@
     input_line = Line(packed_two, right_two, left_two)
     input_line.first()
 
-    hops = []
-    bit = 1
-    while bit < devices:
-        hops.append((flip(me, bit), slot))
-        bit *= 2
-    bit = 1
-    while bit < depth:
-        hops.append((me, flip(slot, bit)))
-        bit *= 2
-
-    def vector_hop(number):
-        made = net.copy(vec_s, vec_got.at[number], hops[number])
-        made.start()
-        made.wait()
-        vec_s[...] += vec_got[number]
-
     def finish(line, target, rows_at):
         target[...] = line.chunks[slot, rows_at, :].astype(F32)
 
@@ -887,11 +883,8 @@
         def _():
             target[...] += line.from_right[slot, rows_at, :].astype(F32)
 
-    vector_hop(0)
-    feed_line.stage(1)
-    vector_hop(1)
-    vector_hop(2)
-    feed_line.stage(2)
+    for time in range(2, depth):
+        feed_line.stage(time)
     finish(feed_line, g_fc2, slice(0, down_rows))
     low_part = part_d.at[0:down_rows]
     finish(feed_line, low_part, slice(down_rows, 2 * down_rows))
@@ -907,38 +900,141 @@
         ]
 
     in_copies = trade(trade_in, got_in)
-    input_line.stage(0)
-    vector_hop(3)
     input_line.stage(1)
-    vector_hop(4)
     for made in in_copies:
         made.wait_recv()
     got_in[me] = trade_in[me]
     for group in range(devices):
         g_in[:, group * wide : (group + 1) * wide] = got_in[group].astype(F32)
-    g_vec[...] = vec_s[0 : g_vec.shape[0], :]
+    for time in range(2, depth):
+        input_line.stage(time)
+    tg_copy.wait_send()
+    finish(input_line, sums, slice(0, rows + 16))
+    first_row = lax.broadcasted_iota(jnp.int32, (16, 3 * block), 0) == 0
+    for group in range(devices):
+        trade_qkv[group, 0:lines, :] = sums[group * lines : (group + 1) * lines, 0 : 3 * block].astype(BF16)
+        trade_qkv[group, lines : lines + 16, :] = jnp.where(
+            first_row, sums[rows + group : rows + group + 1, 0 : 3 * block], 0.0
+        ).astype(BF16)
+        g_out[:, group * block : (group + 1) * block] = sums[
+            group * lines : (group + 1) * lines, 3 * block : 4 * block
+        ]
+    qkv_copies = trade(trade_qkv, got_qkv)
     for wait in out_waits + tg_waits:
         wait()
     out_ref[...] = out_got[...]
     tgrad_ref[...] = tg_got[...]
-    input_line.stage(2)
-    tg_copy.wait_send()
-    total = part.at[0 : 2 * half, 0 : 4 * block]
-    finish(input_line, total, slice(0, rows))
-    for group in range(devices):
-        trade_qkv[group] = total[group * lines : (group + 1) * lines, 0 : 3 * block].astype(BF16)
-        g_out[:, group * block : (group + 1) * block] = total[
-            group * lines : (group + 1) * lines, 3 * block : 4 * block
-        ]
-    for made in trade(trade_qkv, got_qkv):
+    for made in qkv_copies:
         made.wait_recv()
     got_qkv[me] = trade_qkv[me]
+    vec_sum = jnp.zeros((16, 3 * block), F32)
     for group in range(devices):
+        vec_sum = vec_sum + got_qkv[group, lines : lines + 16, :].astype(F32)
         for kind in range(3):
             g_qkv[:, kind * D + group * block : kind * D + (group + 1) * block] = got_qkv[
-                group, :, kind * block : (kind + 1) * block
+                group, 0:lines, kind * block : (kind + 1) * block
             ].astype(F32)
+    g_vec[...] = vec_sum[0:8, :]
     net.close()
+
+
+def adam_kernel(count, *refs):
+    (
+        g_qkv, g_out, g_in, g_fc2, g_vec, vec, out_in, tgrad_in, w_qkv, w_out, w_in, w_fc2, m_one, m_two,
+        out_ref, tgrad_ref, rows_out, params_out, one_out, two_out,
+        grads, params, one, two, b_qkv, b_out, b_in, b_fc2, vec_flat, in_sems, w_sems, out_sems,
+    ) = refs
+    index = lax.axis_index("dp") * lax.axis_size("ctx") + lax.axis_index("ctx")
+    size = m_one.shape[1] // 128
+    parts = in_sems.shape[1]
+    step = grads.shape[0] // parts
+    spans = [(number * step, min((number + 1) * step, size) - number * step) for number in range(parts)]
+    loads = []
+    for number, (start, length) in enumerate(spans):
+        pair = []
+        for kind, (source, target) in enumerate(((m_one, one), (m_two, two))):
+            pair.append(
+                pltpu.make_async_copy(
+                    source.reshape(size, 128).at[start : start + length],
+                    target.at[start : start + length],
+                    in_sems.at[kind, number],
+                )
+            )
+            pair[-1].start()
+        loads.append(pair)
+    weights = []
+    for number, (source, target) in enumerate(
+        ((w_qkv, b_qkv), (w_out, b_out), (w_in, b_in), (w_fc2, b_fc2))
+    ):
+        lines = target.shape[0]
+        start = pl.multiple_of(index * lines, lines)
+        weights.append(
+            pltpu.make_async_copy(source.at[pl.ds(start, lines), :], target, w_sems.at[number])
+        )
+        weights[-1].start()
+    out_ref[...] = out_in[...]
+    tgrad_ref[...] = tgrad_in[...]
+
+    def flatten(source, target, base):
+        lines, groups = source.shape[0], source.shape[1] // 128
+        for col in range(groups):
+            value = source[:, col * 128 : (col + 1) * 128].astype(F32)
+            for row in range(0, lines, 8):
+                target[pl.ds(base + row * groups + col, 8, stride=groups), :] = value[row : row + 8, :]
+
+    base = 0
+    for grad in (g_qkv, g_out, g_in, g_fc2):
+        flatten(grad, grads, base)
+        base += grad.shape[0] * grad.shape[1] // 128
+    share = g_vec.shape[1] // 128
+    groups = vec.shape[1] // 128
+    for col in range(groups):
+        lanes = slice(col * 128, (col + 1) * 128)
+        vec_flat[pl.ds(col, 8, stride=groups), :] = vec[0:8, lanes]
+        for row in range(8, vec.shape[0]):
+            vec_flat[row * groups + col : row * groups + col + 1, :] = vec[row : row + 1, lanes]
+    place = lax.broadcasted_iota(jnp.int32, vec_flat.shape, 0)
+    for number in range(share):
+        grads[base + number : base + number + 1, :] = g_vec[0:1, number * 128 : (number + 1) * 128]
+        params[base + number : base + number + 1, :] = jnp.sum(
+            jnp.where(place == index * share + number, vec_flat[...], 0.0), axis=0, keepdims=True
+        )
+    base = 0
+    for made, weight in zip(weights, (b_qkv, b_out, b_in, b_fc2)):
+        made.wait()
+        flatten(weight, params, base)
+        base += weight.shape[0] * weight.shape[1] // 128
+    fix_one = 1.0 / (1.0 - beta_one**step_count)
+    fix_two = 1.0 / (1.0 - beta_two**step_count)
+    copies = []
+    for number, (start, length) in enumerate(spans):
+        for made in loads[number]:
+            made.wait()
+
+        @pl.loop(0, step // 56)
+        def _(chunk, start=start):
+            at = pl.ds(pl.multiple_of(start + chunk * 56, 8), 56)
+            grad, param = grads[at, :], params[at, :]
+            new_one = beta_one * one[at, :] + (1.0 - beta_one) * grad
+            new_two = beta_two * two[at, :] + (1.0 - beta_two) * grad * grad
+            one[at, :] = new_one
+            two[at, :] = new_two
+            change = new_one * fix_one / (jnp.sqrt(new_two * fix_two) + adam_eps)
+            params[at, :] = param - learn_rate * (change + decay_rate * param)
+
+        for kind, (source, target) in enumerate(
+            ((grads, rows_out), (params, params_out), (one, one_out), (two, two_out))
+        ):
+            copies.append(
+                pltpu.make_async_copy(
+                    source.at[start : start + length],
+                    target.reshape(size, 128).at[start : start + length],
+                    out_sems.at[kind, number],
+                )
+            )
+            copies[-1].start()
+    for made in copies:
+        made.wait()
 
 
 def slot_body(tokens, out_grad, lengths, w_qkv, w_out, w_in, w_fc2, vectors, moment_one, moment_two):
@@ -953,8 +1049,6 @@
     wide = features // devices
     lines = D // count
     total = rows * chips
-    hops = (devices.bit_length() - 1) + (depth.bit_length() - 1)
-    lens = jnp.broadcast_to(lengths[:, None], (slots, 128))
     low = lambda *shape: pltpu.VMEM(shape, BF16)
     wide_f32 = lambda *shape: pltpu.VMEM(shape, F32)
     anywhere = pl.BlockSpec(memory_space=pl.ANY)
@@ -969,9 +1063,9 @@
             jax.ShapeDtypeStruct((lines, D), F32),
             jax.ShapeDtypeStruct((lines, features), F32),
             jax.ShapeDtypeStruct((features // count, D), F32),
-            jax.ShapeDtypeStruct(vectors.shape, F32),
+            jax.ShapeDtypeStruct((8, 3 * block), F32),
         ),
-        in_specs=[anywhere, anywhere, inside, inside] + [anywhere] * 4,
+        in_specs=[anywhere, anywhere, pl.BlockSpec(memory_space=pltpu.SMEM), inside] + [anywhere] * 4,
         out_specs=(inside,) * 7,
         scratch_shapes=[
             low(D, 3 * D // 2),
@@ -1003,20 +1097,22 @@
             low(depth, 2 * wide // depth, D),
             low(depth - 1, 2 * wide // depth, D),
             low(depth - 1, 2 * wide // depth, D),
-            low(depth, devices * lines, 4 * block),
-            low(depth - 1, devices * lines, 4 * block),
-            low(depth - 1, devices * lines, 4 * block),
+            low(depth, devices * lines + 16, 4 * block),
+            low(depth - 1, devices * lines + 16, 4 * block),
+            low(depth - 1, devices * lines + 16, 4 * block),
             low(devices, lines, wide),
             low(devices, lines, wide),
-            low(devices, lines, 3 * block),
-            low(devices, lines, 3 * block),
+            low(devices, lines + 16, 3 * block),
+            low(devices, lines + 16, 3 * block),
             wide_f32(16, D),
-            wide_f32(hops, 16, D),
+            wide_f32(16 * depth, 4 * block),
+            wide_f32(rows + 16, 4 * block),
             low(rows, 3 * D // 2),
             low(half, D),
             low(*tokens.shape),
             low(half, D),
             low(*tokens.shape),
+            pltpu.VMEM((slots, 128), jnp.int32),
             pltpu.SemaphoreType.DMA((6 * chips,)),
             pltpu.SemaphoreType.DMA((copies,)),
             pltpu.SemaphoreType.DMA((copies,)),
@@ -1025,35 +1121,39 @@
             collective_id=0, has_side_effects=True, vmem_limit_bytes=64 * 1024 * 1024 - 64 * 1024
         ),
         name="slot",
-    )(tokens, out_grad, lens, vectors, w_qkv, w_out, w_in, w_fc2)
-    index = lax.axis_index("dp") * depth + lax.axis_index("ctx")
-    own_vectors = lax.dynamic_slice_in_dim(vector_grad.reshape(count, -1), index, 1, 0)
-    grad_rows = jnp.concatenate(
-        [value.reshape(1, -1) for value in (grad_qkv, grad_out_w, grad_in, grad_fc2, own_vectors)],
-        axis=1,
-    )
-    return (out, tokens_grad) + update(
-        grad_rows, index, count, (w_qkv, w_out, w_in, w_fc2, vectors), moment_one, moment_two
-    )
-
-
-def update(grad_rows, index, count, weights, moment_one, moment_two):
-    pieces = []
-    for weight in weights:
-        if weight.shape[0] % count == 0:
-            lines = weight.shape[0] // count
-            piece = lax.dynamic_slice_in_dim(weight, index * lines, lines, 0)
-        else:
-            piece = lax.dynamic_slice_in_dim(weight.reshape(count, -1), index, 1, 0)
-        pieces.append(piece.reshape(1, -1).astype(F32))
-    params = jnp.concatenate(pieces, axis=1)
-    new_one = beta_one * moment_one + (1.0 - beta_one) * grad_rows
-    new_two = beta_two * moment_two + (1.0 - beta_two) * grad_rows * grad_rows
-    fix_one = 1.0 - beta_one**step_count
-    fix_two = 1.0 - beta_two**step_count
-    change = new_one / fix_one / (jnp.sqrt(new_two / fix_two) + adam_eps)
-    new_params = params - learn_rate * (change + decay_rate * params)
-    return (grad_rows, new_params, new_one, new_two)
+    )(tokens, out_grad, lengths, vectors, w_qkv, w_out, w_in, w_fc2)
+    size = moment_one.shape[1] // 128
+    padded = (size + 279) // 280 * 280
+    flat = jax.ShapeDtypeStruct(moment_one.shape, F32)
+    return pl.pallas_call(
+        partial(adam_kernel, count),
+        out_shape=(
+            jax.ShapeDtypeStruct(tokens.shape, BF16),
+            jax.ShapeDtypeStruct(tokens.shape, BF16),
+            flat,
+            flat,
+            flat,
+            flat,
+        ),
+        in_specs=[inside] * 8 + [anywhere] * 6,
+        out_specs=(inside, inside) + (anywhere,) * 4,
+        scratch_shapes=[wide_f32(padded, 128)] * 4
+        + [
+            low(lines, 3 * D),
+            low(lines, D),
+            low(lines, features),
+            low(features // count, D),
+            wide_f32(vectors.shape[0] * D // 128, 128),
+            pltpu.SemaphoreType.DMA((2, 5)),
+            pltpu.SemaphoreType.DMA((4,)),
+            pltpu.SemaphoreType.DMA((4, 5)),
+        ],
+        compiler_params=pltpu.CompilerParams(vmem_limit_bytes=32 * 1024 * 1024),
+        name="adam",
+    )(
+        grad_qkv, grad_out_w, grad_in, grad_fc2, vector_grad, vectors, out, tokens_grad,
+        w_qkv, w_out, w_in, w_fc2, moment_one, moment_two,
+    )
 
 
 def layer(tokens, *rest):

time: 209 us -> 148 us (0.71); the launches traced: 209 us -> 145 us
  Pallas kernels: 176 us -> 126 us
  other arithmetic: 16.1 us -> 0 us
    pallas_call x1, Pallas kernels: 176 us -> 119 us  [slot_body(): pl.pallas_call(partial(slot_kernel, devices, depth, features), out_shape=...]
    sub x1 -> x0, other arithmetic: 12.3 us -> none  [update(): new_params = params - learn_rate * (change + decay_rate * params)]
    unnamed x30 -> x26, local copies, waits for them, and re-layouts: 11.1 us -> 18 us
    pallas_call x0 -> x1, Pallas kernels: none -> 6.77 us  [slot_body(): pl.pallas_call(partial(adam_kernel, count), out_shape=(jax.ShapeDtypeStru...]
    unnamed x4 -> x0, other arithmetic: 3.8 us -> none
    reshape x2 -> x0, local copies, waits for them, and re-layouts: 2.38 us -> none  [the longest x1 1.47 us: update(): piece = lax.dynamic_slice_in_dim(weight.reshape(count, -1), index, 1, 0)]
where the time goes in v3:
time: 148 us; the launch traced here: 145 us
  Pallas kernels  126 us (85%)
  local copies, waits for them, and re-layouts  18 us (12%)
    pallas_call x1, Pallas kernels, slot_body(): pl.pallas_call(partial(slot_kernel, devices, depth, features), out_shape=...  119 us
    unnamed x26, local copies, waits for them, and re-layouts  18 us
    pallas_call x1, Pallas kernels, slot_body(): pl.pallas_call(partial(adam_kernel, count), out_shape=(jax.ShapeDtypeStru...  6.77 us

profile of v3, /device:TPU:0, one launch (start us, length us, event | category | flops | bytes accessed | tf_op | source)
XLA Modules:
  0.0 144.9 jit_solution(13213990792371720712)
XLA Ops:
  0.6 119.3 %slot.1 = (bf16[2,64,1024]{2,1,0:T(8,128)(2,1)}, bf16[2,64,1024]{2,1,0:T(8,128)(2,1)}, f32[32,3072]{1,0:T(8,128)}, f32[32,1024]{1,0:T(8,128)}, f32[32,4096]{1,0:...) custom-call(bf16[2,64,1024]{2,1,0:T(8,128)(2,1)} %refs_0_.1, bf16[2,64,1024]{2,1,0:T(8,128)(2,1)} %refs_1_.1, s32[2]{0:T(128)} %refs_2_.1, ...), custom_call_target="tpu_custom_call" | custom-call | tf_op jit(solution)/shard_map/slot/pallas_call | solution.py:1057
  120.0 0.0 copy-start
  120.0 3.4 %copy-done = bf16[1024,4096]{1,0:T(8,128)(2,1)S(1)} copy-done((bf16[1024,4096]{1,0:T(8,128)(2,1)S(1)}, bf16[1024,4096]{1,0:T(8,128)(2,1)}, u32[]{:S(2)}) %copy-start) | copy-done | bytes 8388632
  123.3 0.0 copy-start.1
  123.3 2.8 %copy-done.1 = bf16[1024,3072]{1,0:T(8,128)(2,1)S(1)} copy-done((bf16[1024,3072]{1,0:T(8,128)(2,1)S(1)}, bf16[1024,3072]{1,0:T(8,128)(2,1)}, u32[]{:S(2)}) %copy-start.1) | copy-done | bytes 6291480
  126.1 0.0 copy-start.2
  126.1 1.6 %copy-done.2 = bf16[1024,1024]{1,0:T(8,128)(2,1)S(1)} copy-done((bf16[1024,1024]{1,0:T(8,128)(2,1)S(1)}, bf16[1024,1024]{1,0:T(8,128)(2,1)}, u32[]{:S(2)}) %copy-start.2) | copy-done | bytes 2097176
  127.7 0.0 copy-start.3
  127.7 1.4 copy-done.3
  129.1 0.0 copy-start.4
  129.1 1.4 copy-done.4
  130.5 1.0 copy-done.5
  131.6 0.0 copy-start.6
  131.6 1.0 copy-done.6
  132.6 0.0 copy-start.7
  132.6 1.0 copy-done.7
  133.6 0.0 copy-start.8
  133.6 0.9 copy-done.8
  134.6 0.0 copy-start.9
  134.6 0.9 copy-done.9
  135.5 0.8 copy-done.10
  136.4 0.9 copy-done.11
  137.3 0.7 copy-done.12
  138.0 6.8 %adam.1 = (bf16[2,64,1024]{2,1,0:T(8,128)(2,1)}, bf16[2,64,1024]{2,1,0:T(8,128)(2,1)}, f32[1,393600]{1,0:T(1,128)}, f32[1,393600]{1,0:T(1,128)}, f32[1,393600]{1,0:T(1,128)}, /*index=5*/f32[1,393600]{1,0:T(1,128)}) custom-call(f32[32,3072]{1,0:T(8,128)S(1)} %copy-done.7, f32[32,1024]{1,0:T(8,128)S(1)} %copy-done.11, f32[32,4096]{1,0:T(8,128)S(1)} %copy-done.5, ...), custom_call_target="tpu_custom_call" | custom-call | tf_op jit(solution)/shard_map/adam/pallas_call | solution.py:1128
  (4 shorter events, 0.0 us)
Async XLA Ops:
  120.0 3.4 %copy-start = (bf16[1024,4096]{1,0:T(8,128)(2,1)S(1)}, bf16[1024,4096]{1,0:T(8,128)(2,1)}, u32[]{:S(2)}) copy-start(bf16[1024,4096]{1,0:T(8,128)(2,1)} %refs_10_.1) | copy-start | bytes 25165828
  123.3 2.8 %copy-start.1 = (bf16[1024,3072]{1,0:T(8,128)(2,1)S(1)}, bf16[1024,3072]{1,0:T(8,128)(2,1)}, u32[]{:S(2)}) copy-start(bf16[1024,3072]{1,0:T(8,128)(2,1)} %refs_8_.1) | copy-start | bytes 18874372
  126.1 1.6 %copy-start.2 = (bf16[1024,1024]{1,0:T(8,128)(2,1)S(1)}, bf16[1024,1024]{1,0:T(8,128)(2,1)}, u32[]{:S(2)}) copy-start(bf16[1024,1024]{1,0:T(8,128)(2,1)} %refs_9_.1) | copy-start | bytes 6291460
  127.7 1.4 copy-start.3
  129.1 1.4 copy-start.4
  130.5 1.0 copy-start.5
  131.6 1.0 copy-start.6
  132.6 1.0 copy-start.7
  133.6 0.9 copy-start.8
  134.6 0.9 copy-start.9
  135.5 0.8 copy-start.10
  136.4 0.9 copy-start.11
  137.3 0.7 copy-start.12

commit v4 on v3

--- a/solution.py
+++ b/solution.py
@@ -1148,7 +1148,7 @@
             pltpu.SemaphoreType.DMA((4,)),
             pltpu.SemaphoreType.DMA((4, 5)),
         ],
-        compiler_params=pltpu.CompilerParams(vmem_limit_bytes=32 * 1024 * 1024),
+        compiler_params=pltpu.CompilerParams(vmem_limit_bytes=64 * 1024 * 1024 - 64 * 1024),
         name="adam",
     )(
         grad_qkv, grad_out_w, grad_in, grad_fc2, vector_grad, vectors, out, tokens_grad,

time: 148 us -> 131 us (0.89)
  local copies, waits for them, and re-layouts: 18 us -> 0 us
  Pallas kernels: 126 us -> 128 us
    unnamed x26 -> x0, local copies, waits for them, and re-layouts: 18 us -> none
where the time goes in v4:
time: 131 us; the launch traced here: 128 us
  Pallas kernels  128 us (98%)
    pallas_call x1, Pallas kernels, slot_body(): pl.pallas_call(partial(slot_kernel, devices, depth, features), out_shape=...  119 us
    pallas_call x1, Pallas kernels, slot_body(): pl.pallas_call(partial(adam_kernel, count), out_shape=(jax.ShapeDtypeStru...  8.17 us

profile of v4, /device:TPU:0, one launch (start us, length us, event | category | flops | bytes accessed | tf_op | source)
XLA Modules:
  0.0 128.3 jit_solution(12861683704116247849)
XLA Ops:
  0.6 119.3 %slot.1 = (bf16[2,64,1024]{2,1,0:T(8,128)(2,1)}, bf16[2,64,1024]{2,1,0:T(8,128)(2,1)}, f32[32,3072]{1,0:T(8,128)}, f32[32,1024]{1,0:T(8,128)}, f32[32,4096]{1,0:...) custom-call(bf16[2,64,1024]{2,1,0:T(8,128)(2,1)} %refs_0_.1, bf16[2,64,1024]{2,1,0:T(8,128)(2,1)} %refs_1_.1, s32[2]{0:T(128)} %refs_2_.1, ...), custom_call_target="tpu_custom_call" | custom-call | tf_op jit(solution)/shard_map/slot/pallas_call | solution.py:1057
  120.0 8.2 %adam.1 = (bf16[2,64,1024]{2,1,0:T(8,128)(2,1)}, bf16[2,64,1024]{2,1,0:T(8,128)(2,1)}, f32[1,393600]{1,0:T(1,128)}, f32[1,393600]{1,0:T(1,128)}, f32[1,393600]{1,0:T(1,128)}, /*index=5*/f32[1,393600]{1,0:T(1,128)}) custom-call(f32[32,3072]{1,0:T(8,128)} %get-tuple-element.13.refs_0_, f32[32,1024]{1,0:T(8,128)} %get-tuple-element.14.refs_1_, ...), custom_call_target="tpu_custom_call" | custom-call | tf_op jit(solution)/shard_map/adam/pallas_call | solution.py:1128

commit v5 on v4

--- a/solution.py
+++ b/solution.py
@@ -365,6 +365,17 @@
             device_id_type=MESH,
         )
 
+    def forward(self, source, target, device, earlier):
+        self.used += 1
+        return pltpu.make_async_remote_copy(
+            src_ref=source,
+            dst_ref=target,
+            send_sem=self.sends.at[self.used - 1],
+            recv_sem=self.recvs.at[earlier],
+            device_id=device,
+            device_id_type=MESH,
+        )
+
     def send(self, source, target, device):
         made = self.copy(source, target, device)
         made.start()
@@ -431,7 +442,7 @@
         wqkv, wo, w_up, w_down,
         x_all, n_all, g_all, b_all, j_all, j_send, g_rows, lens_peer,
         qkv, mixed, part, part_a, part_b, part_c, part_d, summed, grad_two, grad_one,
-        pre_s, hid, hid_all, gp_all, packed, right, left, packed_two, right_two, left_two,
+        pre_s, hid, hid_all, gp_all, packed, plane_got, up_mine, down_mine, packed_two, right_two, left_two,
         trade_in, got_in, trade_qkv, got_qkv, vec_s, vec_by, sums, dqkv, out_half, out_got, tg_half, tg_got, lens,
         local_sems, sends, recvs,
     ) = refs
@@ -538,6 +549,35 @@
             made.append(net.send(spot, spot, peer))
         return made
 
+    class Column:
+        def __init__(self, target):
+            self.target = target
+            self.parts, self.numbers = {}, {}
+            for place in (2, 1, 3):
+                far = lax.rem(slot + depth - place, depth)
+                made = net.copy(target.at[mine_at], self.spot(place), (me, far))
+                self.parts[place], self.numbers[place] = made, net.used - 1
+                goes = {1: slot != 0, 2: slot >= 0, 3: slot != depth - 1}[place]
+                net.open.append((made, goes))
+                pl.when(goes)(made.start)
+            self.passes = {}
+
+        def spot(self, place):
+            return self.target.at[at_rows(place * rows + core * half, half)]
+
+        def relay(self):
+            self.parts[2].wait_recv()
+            up = net.forward(self.spot(2), self.spot(1), (me, depth - 1), self.numbers[1])
+            down = net.forward(self.spot(2), self.spot(3), (me, 0), self.numbers[3])
+            for made, here in ((up, slot == 2), (down, slot == 1)):
+                pl.when(here)(made.start)
+                net.open.append((made, here))
+            self.passes[2] = net.send(self.spot(2), self.spot(2), peer)
+
+        def hand_over(self, place):
+            self.parts[place].wait_recv()
+            self.passes[place] = net.send(self.spot(place), self.spot(place), peer)
+
     x_plane = plane_start(x_all)
     for made in loads[:n_qkv]:
         made.wait()
@@ -595,11 +635,18 @@
 
     first[0].wait_recv()
     norm_one(core * half)
-    n_plane = plane_start(n_all)
+    n_column = Column(n_all)
     first[1].wait_recv()
     norm_one((1 - core) * half)
     for made in loads[n_out:]:
         made.wait()
+
+    for number in range(chips):
+        fine_cols = wide // depth
+        begin = flip_traced(chip, number, chips) * wide + slot * fine_cols
+        at = pl.ds(pl.multiple_of(begin, fine_cols), fine_cols)
+        up_mine[:, number * fine_cols : (number + 1) * fine_cols] = w_up[:, at]
+        down_mine[number * fine_cols : (number + 1) * fine_cols, :] = w_down[at, :]
 
     def bias_of(mask):
         spot = flip_traced(chip, mask, chips)
@@ -664,11 +711,10 @@
 
     second[0].wait_recv()
     norm_two(core * half, True)
-    g_plane = plane_start(g_all)
+    g_column = Column(g_all)
     second[1].wait_recv()
     norm_two((1 - core) * half, False)
-    out_waits = go_back(out_half, out_got)
-    n_pass = plane_pass(n_plane, n_all)
+    n_column.relay()
     x_pass = plane_pass(x_plane, x_all)
 
     def slope_of(value, cdf):
@@ -703,42 +749,8 @@
     b_plane = plane_start(b_all)
     third[1].wait_recv()
     norm_one_back((1 - core) * half, False)
-    g_pass = plane_pass(g_plane, g_all)
-
-    bias_mine = bias_of(0)
-
-    def feed_rows(mask):
-        at = slice(mask * rows, (mask + 1) * rows)
-        value = dot(n_all[at, :], w_up[:, 0:wide]) + bias_mine
-        cdf = normal_cdf(value)
-        hid_all[at, :] = (value * cdf).astype(BF16)
-        low = (through(g_all[at, :], w_down[0:wide, :]) * slope_of(value, cdf)).astype(BF16)
-        gp_all[at, :] = low
-        return jnp.sum(low.astype(F32), axis=0, keepdims=True)
-
-    bias_sum = feed_rows(0)
-    for mask in range(1, chips):
-        n_pass[mask - 1].wait_recv()
-        g_pass[mask - 1].wait_recv()
-        bias_sum = bias_sum + feed_rows(mask)
-    lanes = pl.ds(pl.multiple_of(core * wide, wide), wide)
-    for row in range(chips):
-        vec_s[3 + row : 4 + row, lanes] = jnp.where(chip == row, bias_sum, jnp.zeros_like(bias_sum))
-    down_rows = wide // depth
-    packs = D // wide
-    per_pack = devices // packs
-    span = lines * depth
-    down = inner(hid_all[...], g_all[...]).astype(BF16)
-    for number in range(depth):
-        packed[number, 0:down_rows, :] = down[number * down_rows : (number + 1) * down_rows, :]
-    for group in range(devices):
-        up = inner(n_all[:, group * span : (group + 1) * span], gp_all[...]).astype(BF16)
-        row = down_rows + (group % per_pack) * lines
-        col = (group // per_pack) * wide
-        for number in range(depth):
-            packed[number, row : row + lines, col : col + wide] = up[
-                number * lines : (number + 1) * lines, :
-            ]
+    n_column.hand_over(1)
+    n_column.hand_over(3)
 
     class Line:
         def __init__(self, chunks, from_left, from_right):
@@ -783,9 +795,6 @@
                             self.from_right[order].astype(F32) + self.chunks[low].astype(F32)
                         ).astype(BF16)
                         self.down[order].start()
-
-    feed_line = Line(packed, right, left)
-    feed_line.first()
 
     grad_parts = range(1, chips)
 
@@ -841,8 +850,52 @@
     part[half:rows, :] = grad_one[mine_at, :] + through(dqkv[mine_at, :], wqkv[...])
     tg_copy.wait_recv()
     tg_half[...] = (part[half:rows, :] + part_d[...]).astype(BF16)
-    feed_line.stage(1)
+
+    fine = wide // depth
+    span = lines * depth
+    features_at = pl.ds(pl.multiple_of((depth * core + slot) * fine, fine), fine)
+    bias_mine = jnp.concatenate([vec[3 + number : 4 + number, features_at] for number in range(chips)], axis=1)
+
+    def feed_rows(place):
+        at = slice(place * rows, (place + 1) * rows)
+        value = dot(n_all[at, :], up_mine[...]) + bias_mine
+        cdf = normal_cdf(value)
+        hid_all[at, :] = (value * cdf).astype(BF16)
+        low = (through(g_all[at, :], down_mine[...]) * slope_of(value, cdf)).astype(BF16)
+        gp_all[at, :] = low
+        return jnp.sum(low.astype(F32), axis=0, keepdims=True)
+
+    bias_sum = feed_rows(0)
+    g_column.relay()
+    g_column.hand_over(1)
+    g_column.hand_over(3)
+    out_waits = go_back(out_half, out_got)
     tg_waits = go_back(tg_half, tg_got)
+    for place in (2, 1, 3):
+        n_column.passes[place].wait_recv()
+        g_column.passes[place].wait_recv()
+        bias_sum = bias_sum + feed_rows(place)
+    for number in range(chips):
+        vec_s[3 + number : 4 + number, features_at] = bias_sum[:, number * fine : (number + 1) * fine]
+    depth_rows = D // chips
+    for number in range(chips):
+        block_up = inner(n_all[:, number * depth_rows : (number + 1) * depth_rows], gp_all[...]).astype(BF16)
+        packed[number, fine : 2 * fine, 0:wide] = block_up[0:fine, :]
+        packed[number, fine : 2 * fine, wide : 2 * wide] = block_up[fine : 2 * fine, :]
+
+    def scatter_plane(lines_at):
+        return [
+            net.send(
+                packed.at[flip_traced(chip, mask, chips), lines_at],
+                plane_got.at[mask - 1, lines_at],
+                (flip(me, 2 * mask), slot),
+            )
+            for mask in range(1, chips)
+        ]
+
+    up_copies = scatter_plane(slice(fine, 2 * fine))
+    packed[:, 0:fine, :] = inner(hid_all[...], g_all[...]).astype(BF16).reshape(chips, fine, D)
+    down_copies = scatter_plane(slice(0, fine))
 
     tiles = vec.shape[0] * D // 128
     share = tiles // (devices * depth)
@@ -883,15 +936,13 @@
         def _():
             target[...] += line.from_right[slot, rows_at, :].astype(F32)
 
-    for time in range(2, depth):
-        feed_line.stage(time)
-    finish(feed_line, g_fc2, slice(0, down_rows))
-    low_part = part_d.at[0:down_rows]
-    finish(feed_line, low_part, slice(down_rows, 2 * down_rows))
-    for group in range(devices):
-        row = (group % per_pack) * lines
-        col = (group // per_pack) * wide
-        trade_in[group] = low_part[row : row + lines, col : col + wide].astype(BF16)
+    def plane_sum(copies, lines_at):
+        for made in copies:
+            made.wait_recv()
+        value = packed[chip, lines_at, :].astype(F32)
+        for number in range(chips - 1):
+            value = value + plane_got[number, lines_at, :].astype(F32)
+        return value
 
     def trade(source, target):
         return [
@@ -899,13 +950,19 @@
             for mask in range(1, devices)
         ]
 
-    in_copies = trade(trade_in, got_in)
     input_line.stage(1)
-    for made in in_copies:
-        made.wait_recv()
-    got_in[me] = trade_in[me]
-    for group in range(devices):
-        g_in[:, group * wide : (group + 1) * wide] = got_in[group].astype(F32)
+    low_sum = plane_sum(up_copies, slice(fine, 2 * fine)).astype(BF16)
+    for upper in range(2):
+        for number in range(depth):
+            trade_in[upper * depth + number] = low_sum[
+                number * lines : (number + 1) * lines, upper * wide : (upper + 1) * wide
+            ]
+    here = core * depth + slot
+    in_copies = []
+    for shift in range(1, 2 * depth):
+        far = lax.rem(slot + shift % depth, depth)
+        upper = core if shift < depth else 1 - core
+        in_copies.append(net.send(trade_in.at[upper * depth + far], got_in.at[here], (base + upper, far)))
     for time in range(2, depth):
         input_line.stage(time)
     tg_copy.wait_send()
@@ -920,6 +977,14 @@
             group * lines : (group + 1) * lines, 3 * block : 4 * block
         ]
     qkv_copies = trade(trade_qkv, got_qkv)
+    for made in in_copies:
+        made.wait_recv()
+    got_in[here] = trade_in[here]
+    for group in range(2 * depth):
+        for number in range(chips):
+            start = number * 2 * wide + group * fine
+            g_in[:, start : start + fine] = got_in[group, :, number * fine : (number + 1) * fine].astype(F32)
+    g_fc2[...] = plane_sum(down_copies, slice(0, fine))
     for wait in out_waits + tg_waits:
         wait()
     out_ref[...] = out_got[...]
@@ -1094,9 +1159,10 @@
             low(rows, features // 2),
             low(total, wide),
             low(total, wide),
-            low(depth, 2 * wide // depth, D),
-            low(depth - 1, 2 * wide // depth, D),
-            low(depth - 1, 2 * wide // depth, D),
+            low(chips, 2 * wide // depth, D),
+            low(chips - 1, 2 * wide // depth, D),
+            low(D, wide),
+            low(wide, D),
             low(depth, devices * lines + 16, 4 * block),
             low(depth - 1, devices * lines + 16, 4 * block),
             low(depth - 1, devices * lines + 16, 4 * block),
@@ -1159,7 +1225,7 @@
 def layer(tokens, *rest):
     slots, piece, width = tokens.shape
     devices, depth = lax.axis_size("dp"), lax.axis_size("ctx")
-    fits = slots == 2 and depth == 2 * slots and devices % 2 == 0
+    fits = slots == 2 and depth == 2 * slots and devices == 2 * depth and FF == (devices // 2) * D
     if fits and (H * HD // devices) % 128 == 0 and (FF // devices) % 128 == 0:
         return slot_body(tokens, *rest)
     return body(tokens, *rest)

time: 131 us -> 118 us (0.901)
  the two profiles are of different devices: /device:TPU:0 before, /device:TPU:17 now
where the time goes in v5:
time: 118 us
  Pallas kernels  117 us (99%)
    pallas_call x1, Pallas kernels, slot_body(): pl.pallas_call(partial(slot_kernel, devices, depth, features), out_shape=...  109 us
    pallas_call x1, Pallas kernels, slot_body(): pl.pallas_call(partial(adam_kernel, count), out_shape=(jax.ShapeDtypeStru...  8.17 us

profile of v5, /device:TPU:17, one launch (start us, length us, event | category | flops | bytes accessed | tf_op | source)
XLA Modules:
  0.0 117.9 jit_solution(14307037517543038929)
XLA Ops:
  0.6 108.9 %slot.1 = (bf16[2,64,1024]{2,1,0:T(8,128)(2,1)}, bf16[2,64,1024]{2,1,0:T(8,128)(2,1)}, f32[32,3072]{1,0:T(8,128)}, f32[32,1024]{1,0:T(8,128)}, f32[32,4096]{1,0:...) custom-call(bf16[2,64,1024]{2,1,0:T(8,128)(2,1)} %refs_0_.1, bf16[2,64,1024]{2,1,0:T(8,128)(2,1)} %refs_1_.1, s32[2]{0:T(128)} %refs_2_.1, ...), custom_call_target="tpu_custom_call" | custom-call | tf_op jit(solution)/shard_map/slot/pallas_call | solution.py:1122
  109.5 8.2 %adam.1 = (bf16[2,64,1024]{2,1,0:T(8,128)(2,1)}, bf16[2,64,1024]{2,1,0:T(8,128)(2,1)}, f32[1,393600]{1,0:T(1,128)}, f32[1,393600]{1,0:T(1,128)}, f32[1,393600]{1,0:T(1,128)}, /*index=5*/f32[1,393600]{1,0:T(1,128)}) custom-call(f32[32,3072]{1,0:T(8,128)} %get-tuple-element.13.refs_0_, f32[32,1024]{1,0:T(8,128)} %get-tuple-element.14.refs_1_, ...), custom_call_target="tpu_custom_call" | custom-call | tf_op jit(solution)/shard_map/adam/pallas_call | solution.py:1194

commit v6 on v5

--- a/solution.py
+++ b/solution.py
@@ -440,10 +440,10 @@
         tokens, out_grad, lengths, vec, w_qkv, w_out, w_in, w_fc2,
         out_ref, tgrad_ref, g_qkv, g_out, g_in, g_fc2, g_vec,
         wqkv, wo, w_up, w_down,
-        x_all, n_all, g_all, b_all, j_all, j_send, g_rows, lens_peer,
-        qkv, mixed, part, part_a, part_b, part_c, part_d, summed, grad_two, grad_one,
+        x_all, n_all, g_all, m_all, b_all, j_all, j_send, g_rows, lens_peer,
+        qkv, part, part_a, part_b, part_c, part_d, summed, grad_two, grad_one,
         pre_s, hid, hid_all, gp_all, packed, plane_got, up_mine, down_mine, packed_two, right_two, left_two,
-        trade_in, got_in, trade_qkv, got_qkv, vec_s, vec_by, sums, dqkv, out_half, out_got, tg_half, tg_got, lens,
+        trade_in, got_in, trade_qkv, got_qkv, vec_s, vec_by, vec_got, sums, dqkv, out_half, out_got, tg_half, tg_got, lens,
         local_sems, sends, recvs,
     ) = refs
     chips = devices // 2
@@ -481,9 +481,9 @@
                 wqkv.at[:, (3 * mask + kind) * block : (3 * mask + kind + 1) * block],
             )
     n_qkv = len(loads)
-    for mask in range(chips):
-        start = pl.multiple_of(where[mask] * block, block)
-        load(w_out.at[pl.ds(start, block), :], wo.at[mask * block : (mask + 1) * block, :])
+    for number in range(chips):
+        start = pl.multiple_of((2 * number + core) * block, block)
+        load(w_out.at[pl.ds(start, block), :], wo.at[number * block : (number + 1) * block, :])
     n_out = len(loads)
     for mask in range(chips):
         start = pl.multiple_of(where[mask] * wide, wide)
@@ -606,7 +606,8 @@
         qkv[:, pl.ds(start, block)] = queries
         qkv[:, pl.ds(pl.multiple_of(start + block, block), block)] = keys
         qkv[:, pl.ds(pl.multiple_of(start + 2 * block, block), block)] = values
-        mixed[:, pl.ds(pl.multiple_of(mask * block, block), block)] = total.astype(BF16)
+        lanes = pl.ds(pl.multiple_of(core * chips * block + lax.div(spot, 2) * block, block), block)
+        m_all[0:rows, lanes] = total.astype(BF16)
 
     for made in loads[n_qkv:n_out]:
         made.wait()
@@ -621,7 +622,14 @@
             made[-1].start()
         return made
 
-    first = exchange(lambda at: dot(mixed[at, :], wo[...]), part_a, None)
+    my_lanes = pl.ds(pl.multiple_of(core * chips * block, chips * block), chips * block)
+    first = exchange(lambda at: dot(m_all[at, my_lanes], wo[...]), part_a, None)
+    own_mixed = m_all.at[0:rows, my_lanes]
+    m_passes = [net.send(own_mixed, own_mixed, peer)]
+    m_plane = [
+        net.send(own_mixed, m_all.at[mask * rows : (mask + 1) * rows, my_lanes], (flip(me, 2 * mask), slot))
+        for mask in range(1, chips)
+    ]
     grad_passes = pass_on(grad_waits, g_rows)
 
     def norm_one(start):
@@ -714,8 +722,12 @@
     g_column = Column(g_all)
     second[1].wait_recv()
     norm_two((1 - core) * half, False)
-    n_column.relay()
-    x_pass = plane_pass(x_plane, x_all)
+    def mixed_pass():
+        for mask, made in enumerate(m_plane, 1):
+            made.wait_recv()
+            spot = m_all.at[mask * rows : (mask + 1) * rows, my_lanes]
+            m_passes.append(net.send(spot, spot, peer))
+
 
     def slope_of(value, cdf):
         return cdf + value * (jnp.exp(-0.5 * value * value) * 0.3989422804014327)
@@ -744,9 +756,11 @@
                 vec_s[8:9, :] += jnp.sum(error * (center * scale), axis=0, keepdims=True)
                 vec_s[9:10, :] += jnp.sum(error, axis=0, keepdims=True)
 
+    n_column.relay()
+    x_pass = plane_pass(x_plane, x_all)
+
     third[0].wait_recv()
     norm_one_back(core * half, True)
-    b_plane = plane_start(b_all)
     third[1].wait_recv()
     norm_one_back((1 - core) * half, False)
     n_column.hand_over(1)
@@ -803,7 +817,8 @@
         queries = qkv[:, start : start + block]
         keys = qkv[:, start + block : start + 2 * block]
         values = qkv[:, start + 2 * block : start + 3 * block]
-        grad_mixed = through(b_all[0:rows, :], wo[mask * block : (mask + 1) * block, :]).astype(BF16)
+        turn = pl.ds(pl.multiple_of(lax.div(where[mask], 2) * block, block), block)
+        grad_mixed = through(b_all[0:rows, :], wo[turn, :]).astype(BF16)
         grad_q = jnp.zeros((rows, block), F32)
         grad_k = grad_q
         grad_v = grad_q
@@ -832,7 +847,7 @@
         joint[:, 0:block] = grad_q
         joint[:, block : 2 * block] = grad_k
         joint[:, 2 * block : 3 * block] = grad_v
-        joint[:, 3 * block : 4 * block] = mixed[:, mask * block : (mask + 1) * block]
+        joint[:, 3 * block : 4 * block] = b_all[0:rows, spot]
         if mask:
             return net.send(
                 joint, j_all.at[mask * rows : (mask + 1) * rows], (flip(me, 2 * mask), slot)
@@ -841,7 +856,7 @@
 
     j_copies = [attention_back(mask) for mask in grad_parts]
     attention_back(0)
-    b_pass = plane_pass(b_plane, b_all)
+    mixed_pass()
     for made in third:
         made.wait_send()
     part[0:half, :] = through(dqkv[other_at, :], wqkv[...])
@@ -867,10 +882,23 @@
 
     bias_sum = feed_rows(0)
     g_column.relay()
+    for made in m_passes + x_pass + j_copies:
+        made.wait_recv()
+    for group in range(devices):
+        at = slice(group * span, (group + 1) * span)
+        begin = (group % 2) * chips * block + (group // 2) * block
+        both = inner(x_all[:, at], j_all[:, 0 : 3 * block]).astype(BF16)
+        across = inner(m_all[:, begin : begin + block], j_all[:, 3 * block : 4 * block]).astype(BF16)
+        row = group * lines
+        for number in range(depth):
+            at = slice(number * lines, (number + 1) * lines)
+            packed_two[number, row : row + lines, 0 : 3 * block] = both[at, :]
+            packed_two[number, row : row + lines, 3 * block : 4 * block] = across[at, :]
+    input_line = Line(packed_two, right_two, left_two)
+    input_line.first()
+
     g_column.hand_over(1)
     g_column.hand_over(3)
-    out_waits = go_back(out_half, out_got)
-    tg_waits = go_back(tg_half, tg_got)
     for place in (2, 1, 3):
         n_column.passes[place].wait_recv()
         g_column.passes[place].wait_recv()
@@ -903,27 +931,15 @@
     for tile in range(tiles):
         owner, lane_group = tile // share, tile % share
         row, col = tile // (D // 128), (tile % (D // 128)) * 128
-        spot = (owner % depth) * 16 + owner // depth
+        spot = (owner % depth) * devices + owner // depth
         vec_by[spot : spot + 1, lane_group * 128 : (lane_group + 1) * 128] = vec_s[
             row : row + 1, col : col + 128
         ]
-    for number in range(depth):
-        packed_two[number, rows : rows + 16, :] = vec_by[number * 16 : (number + 1) * 16, :].astype(BF16)
-
-    for made in b_pass + x_pass + j_copies:
-        made.wait_recv()
-    across = inner(j_all[:, 3 * block : 4 * block], b_all[...]).astype(BF16)
-    for group in range(devices):
-        both = inner(x_all[:, group * span : (group + 1) * span], j_all[:, 0 : 3 * block]).astype(BF16)
-        row = group * lines
-        for number in range(depth):
-            at = slice(number * lines, (number + 1) * lines)
-            packed_two[number, row : row + lines, 0 : 3 * block] = both[at, :]
-            packed_two[number, row : row + lines, 3 * block : 4 * block] = across[
-                at, group * block : (group + 1) * block
-            ]
-    input_line = Line(packed_two, right_two, left_two)
-    input_line.first()
+    vec_copies = []
+    for shift in range(1, depth):
+        far = lax.rem(slot + shift, depth)
+        spot = vec_by.at[pl.ds(pl.multiple_of(far * devices, devices), devices)]
+        vec_copies.append(net.send(spot, vec_got.at[shift - 1], (me, far)))
 
     def finish(line, target, rows_at):
         target[...] = line.chunks[slot, rows_at, :].astype(F32)
@@ -950,7 +966,8 @@
             for mask in range(1, devices)
         ]
 
-    input_line.stage(1)
+    for time in range(1, depth - 1):
+        input_line.stage(time)
     low_sum = plane_sum(up_copies, slice(fine, 2 * fine)).astype(BF16)
     for upper in range(2):
         for number in range(depth):
@@ -963,19 +980,21 @@
         far = lax.rem(slot + shift % depth, depth)
         upper = core if shift < depth else 1 - core
         in_copies.append(net.send(trade_in.at[upper * depth + far], got_in.at[here], (base + upper, far)))
-    for time in range(2, depth):
-        input_line.stage(time)
+    out_waits = go_back(out_half, out_got)
+    tg_waits = go_back(tg_half, tg_got)
+    input_line.stage(depth - 1)
     tg_copy.wait_send()
-    finish(input_line, sums, slice(0, rows + 16))
-    first_row = lax.broadcasted_iota(jnp.int32, (16, 3 * block), 0) == 0
+    finish(input_line, sums, slice(0, rows))
+    vec_sum = vec_by[pl.ds(pl.multiple_of(slot * devices, devices), devices), :]
+    for number, made in enumerate(vec_copies):
+        made.wait_recv()
+        vec_sum = vec_sum + vec_got[number]
+    first_row = lax.broadcasted_iota(jnp.int32, (16, 4 * block), 0) == 0
     for group in range(devices):
-        trade_qkv[group, 0:lines, :] = sums[group * lines : (group + 1) * lines, 0 : 3 * block].astype(BF16)
+        trade_qkv[group, 0:lines, :] = sums[group * lines : (group + 1) * lines, :].astype(BF16)
         trade_qkv[group, lines : lines + 16, :] = jnp.where(
-            first_row, sums[rows + group : rows + group + 1, 0 : 3 * block], 0.0
+            first_row, vec_sum[group : group + 1, :], 0.0
         ).astype(BF16)
-        g_out[:, group * block : (group + 1) * block] = sums[
-            group * lines : (group + 1) * lines, 3 * block : 4 * block
-        ]
     qkv_copies = trade(trade_qkv, got_qkv)
     for made in in_copies:
         made.wait_recv()
@@ -994,11 +1013,13 @@
     got_qkv[me] = trade_qkv[me]
     vec_sum = jnp.zeros((16, 3 * block), F32)
     for group in range(devices):
-        vec_sum = vec_sum + got_qkv[group, lines : lines + 16, :].astype(F32)
+        vec_sum = vec_sum + got_qkv[group, lines : lines + 16, 0 : 3 * block].astype(F32)
+        got = got_qkv[group, 0:lines, :].astype(F32)
         for kind in range(3):
-            g_qkv[:, kind * D + group * block : kind * D + (group + 1) * block] = got_qkv[
-                group, 0:lines, kind * block : (kind + 1) * block
-            ].astype(F32)
+            g_qkv[:, kind * D + group * block : kind * D + (group + 1) * block] = got[
+                :, kind * block : (kind + 1) * block
+            ]
+        g_out[:, group * block : (group + 1) * block] = got[:, 3 * block : 4 * block]
     g_vec[...] = vec_sum[0:8, :]
     net.close()
 
@@ -1141,12 +1162,12 @@
             low(total, D),
             low(total, D),
             low(total, D),
+            low(rows, D),
             low(total, 4 * block),
             low(chips - 1, rows, 4 * block),
             low(rows, D),
             pltpu.VMEM((slots, 128), jnp.int32),
             low(rows, 3 * D // 2),
-            low(rows, D // 2),
             wide_f32(rows, D),
             wide_f32(rows, D),
             wide_f32(rows, D),
@@ -1163,16 +1184,17 @@
             low(chips - 1, 2 * wide // depth, D),
             low(D, wide),
             low(wide, D),
-            low(depth, devices * lines + 16, 4 * block),
-            low(depth - 1, devices * lines + 16, 4 * block),
-            low(depth - 1, devices * lines + 16, 4 * block),
+            low(depth, devices * lines, 4 * block),
+            low(depth - 1, devices * lines, 4 * block),
+            low(depth - 1, devices * lines, 4 * block),
             low(devices, lines, wide),
             low(devices, lines, wide),
-            low(devices, lines + 16, 3 * block),
-            low(devices, lines + 16, 3 * block),
+            low(devices, lines + 16, 4 * block),
+            low(devices, lines + 16, 4 * block),
             wide_f32(16, D),
-            wide_f32(16 * depth, 4 * block),
-            wide_f32(rows + 16, 4 * block),
+            wide_f32(devices * depth, 4 * block),
+            wide_f32(depth - 1, devices, 4 * block),
+            wide_f32(rows, 4 * block),
             low(rows, 3 * D // 2),
             low(half, D),
             low(*tokens.shape),

time: 118 us -> 116 us (0.983)
  the two profiles are of different devices: /device:TPU:17 before, /device:TPU:11 now
where the time goes in v6:
time: 116 us
  Pallas kernels  115 us (99%)
    pallas_call x1, Pallas kernels, slot_body(): pl.pallas_call(partial(slot_kernel, devices, depth, features), out_shape=...  107 us
    pallas_call x1, Pallas kernels, slot_body(): pl.pallas_call(partial(adam_kernel, count), out_shape=(jax.ShapeDtypeStru...  8.17 us

profile of v6, /device:TPU:11, one launch (start us, length us, event | category | flops | bytes accessed | tf_op | source)
XLA Modules:
  0.0 116.2 jit_solution(991912954689119614)
XLA Ops:
  0.6 107.2 %slot.1 = (bf16[2,64,1024]{2,1,0:T(8,128)(2,1)}, bf16[2,64,1024]{2,1,0:T(8,128)(2,1)}, f32[32,3072]{1,0:T(8,128)}, f32[32,1024]{1,0:T(8,128)}, f32[32,4096]{1,0:...) custom-call(bf16[2,64,1024]{2,1,0:T(8,128)(2,1)} %refs_0_.1, bf16[2,64,1024]{2,1,0:T(8,128)(2,1)} %refs_1_.1, s32[2]{0:T(128)} %refs_2_.1, ...), custom_call_target="tpu_custom_call" | custom-call | tf_op jit(solution)/shard_map/slot/pallas_call | solution.py:1143
  107.9 8.2 %adam.1 = (bf16[2,64,1024]{2,1,0:T(8,128)(2,1)}, bf16[2,64,1024]{2,1,0:T(8,128)(2,1)}, f32[1,393600]{1,0:T(1,128)}, f32[1,393600]{1,0:T(1,128)}, f32[1,393600]{1,0:T(1,128)}, /*index=5*/f32[1,393600]{1,0:T(1,128)}) custom-call(f32[32,3072]{1,0:T(8,128)} %get-tuple-element.13.refs_0_, f32[32,1024]{1,0:T(8,128)} %get-tuple-element.14.refs_1_, ...), custom_call_target="tpu_custom_call" | custom-call | tf_op jit(solution)/shard_map/adam/pallas_call | solution.py:1216

commit v7 on v6

--- a/solution.py
+++ b/solution.py
@@ -756,16 +756,12 @@
                 vec_s[8:9, :] += jnp.sum(error * (center * scale), axis=0, keepdims=True)
                 vec_s[9:10, :] += jnp.sum(error, axis=0, keepdims=True)
 
-    n_column.relay()
     x_pass = plane_pass(x_plane, x_all)
 
     third[0].wait_recv()
     norm_one_back(core * half, True)
     third[1].wait_recv()
     norm_one_back((1 - core) * half, False)
-    n_column.hand_over(1)
-    n_column.hand_over(3)
-
     class Line:
         def __init__(self, chunks, from_left, from_right):
             self.chunks, self.from_left, self.from_right = chunks, from_left, from_right
@@ -855,8 +851,11 @@
         return None
 
     j_copies = [attention_back(mask) for mask in grad_parts]
+    n_column.relay()
     attention_back(0)
     mixed_pass()
+    n_column.hand_over(1)
+    n_column.hand_over(3)
     for made in third:
         made.wait_send()
     part[0:half, :] = through(dqkv[other_at, :], wqkv[...])
@@ -896,6 +895,7 @@
             packed_two[number, row : row + lines, 3 * block : 4 * block] = across[at, :]
     input_line = Line(packed_two, right_two, left_two)
     input_line.first()
+    out_waits = go_back(out_half, out_got)
 
     g_column.hand_over(1)
     g_column.hand_over(3)
@@ -966,6 +966,7 @@
             for mask in range(1, devices)
         ]
 
+    tg_waits = go_back(tg_half, tg_got)
     for time in range(1, depth - 1):
         input_line.stage(time)
     low_sum = plane_sum(up_copies, slice(fine, 2 * fine)).astype(BF16)
@@ -980,8 +981,6 @@
         far = lax.rem(slot + shift % depth, depth)
         upper = core if shift < depth else 1 - core
         in_copies.append(net.send(trade_in.at[upper * depth + far], got_in.at[here], (base + upper, far)))
-    out_waits = go_back(out_half, out_got)
-    tg_waits = go_back(tg_half, tg_got)
     input_line.stage(depth - 1)
     tg_copy.wait_send()
     finish(input_line, sums, slice(0, rows))

time: 116 us -> 111 us (0.957)
  the two profiles are of different devices: /device:TPU:11 before, /device:TPU:0 now
where the time goes in v7:
time: 111 us; the launch traced here: 109 us
  Pallas kernels  108 us (97%)
    pallas_call x1, Pallas kernels, slot_body(): pl.pallas_call(partial(slot_kernel, devices, depth, features), out_shape=...  100 us
    pallas_call x1, Pallas kernels, slot_body(): pl.pallas_call(partial(adam_kernel, count), out_shape=(jax.ShapeDtypeStru...  8.17 us

profile of v7, /device:TPU:0, one launch (start us, length us, event | category | flops | bytes accessed | tf_op | source)
XLA Modules:
  0.0 109.0 jit_solution(1399693436950283323)
XLA Ops:
  0.6 100.0 %slot.1 = (bf16[2,64,1024]{2,1,0:T(8,128)(2,1)}, bf16[2,64,1024]{2,1,0:T(8,128)(2,1)}, f32[32,3072]{1,0:T(8,128)}, f32[32,1024]{1,0:T(8,128)}, f32[32,4096]{1,0:...) custom-call(bf16[2,64,1024]{2,1,0:T(8,128)(2,1)} %refs_0_.1, bf16[2,64,1024]{2,1,0:T(8,128)(2,1)} %refs_1_.1, s32[2]{0:T(128)} %refs_2_.1, ...), custom_call_target="tpu_custom_call" | custom-call | tf_op jit(solution)/shard_map/slot/pallas_call | solution.py:1142
  100.6 8.2 %adam.1 = (bf16[2,64,1024]{2,1,0:T(8,128)(2,1)}, bf16[2,64,1024]{2,1,0:T(8,128)(2,1)}, f32[1,393600]{1,0:T(1,128)}, f32[1,393600]{1,0:T(1,128)}, f32[1,393600]{1,0:T(1,128)}, /*index=5*/f32[1,393600]{1,0:T(1,128)}) custom-call(f32[32,3072]{1,0:T(8,128)} %get-tuple-element.13.refs_0_, f32[32,1024]{1,0:T(8,128)} %get-tuple-element.14.refs_1_, ...), custom_call_target="tpu_custom_call" | custom-call | tf_op jit(solution)/shard_map/adam/pallas_call | solution.py:1215

commit v8 on v7

--- a/solution.py
+++ b/solution.py
@@ -441,7 +441,7 @@
         out_ref, tgrad_ref, g_qkv, g_out, g_in, g_fc2, g_vec,
         wqkv, wo, w_up, w_down,
         x_all, n_all, g_all, m_all, b_all, j_all, j_send, g_rows, lens_peer,
-        qkv, part, part_a, part_b, part_c, part_d, summed, grad_two, grad_one,
+        qkv, part, part_low, part_a, part_b, part_c, part_d, summed, grad_two, grad_one,
         pre_s, hid, hid_all, gp_all, packed, plane_got, up_mine, down_mine, packed_two, right_two, left_two,
         trade_in, got_in, trade_qkv, got_qkv, vec_s, vec_by, vec_got, sums, dqkv, out_half, out_got, tg_half, tg_got, lens,
         local_sems, sends, recvs,
@@ -617,8 +617,10 @@
         for number, at in enumerate((other_at, mine_at)):
             if before is not None:
                 before[number].wait_send()
-            part[at, :] = compute(at)
-            made.append(net.copy(part.at[at], target.at[at], peer))
+            value = compute(at)
+            part[at, :] = value
+            part_low[at, :] = value.astype(BF16)
+            made.append(net.copy(part_low.at[at], target.at[at], peer))
             made[-1].start()
         return made
 
@@ -636,7 +638,7 @@
         @pl.loop(0, half // chunk)
         def _(step):
             at = pl.ds(pl.multiple_of(start + step * chunk, chunk), chunk)
-            total = x_all[at, :].astype(F32) + (part[at, :] + part_a[at, :]) + vec[2:3, :]
+            total = x_all[at, :].astype(F32) + (part[at, :] + part_a[at, :].astype(F32)) + vec[2:3, :]
             center, scale = layer_norm_stats(total)
             summed[at, :] = total
             n_all[at, :] = (center * scale * vec[8:9, :] + vec[9:10, :]).astype(BF16)
@@ -682,7 +684,7 @@
             at = pl.ds(begin, chunk)
             center, scale = layer_norm_stats(summed[at, :])
             normed = center * scale * vec[8:9, :] + vec[9:10, :]
-            center, scale = layer_norm_stats(normed + (part[at, :] + part_b[at, :]) + vec[7:8, :])
+            center, scale = layer_norm_stats(normed + (part[at, :] + part_b[at, :].astype(F32)) + vec[7:8, :])
             place = begin + lax.broadcasted_iota(jnp.int32, (chunk, 1), 0)
             piece_of = lax.div(place, piece)
             spot = 2 * lax.div(piece_of, 2) + lax.rem(slot + lax.rem(piece_of, 2), 2)
@@ -722,12 +724,13 @@
     g_column = Column(g_all)
     second[1].wait_recv()
     norm_two((1 - core) * half, False)
+    out_waits = go_back(out_half, out_got)
+
     def mixed_pass():
         for mask, made in enumerate(m_plane, 1):
             made.wait_recv()
             spot = m_all.at[mask * rows : (mask + 1) * rows, my_lanes]
             m_passes.append(net.send(spot, spot, peer))
-
 
     def slope_of(value, cdf):
         return cdf + value * (jnp.exp(-0.5 * value * value) * 0.3989422804014327)
@@ -746,7 +749,7 @@
         def _(step):
             at = pl.ds(pl.multiple_of(start + step * chunk, chunk), chunk)
             center, scale = layer_norm_stats(summed[at, :])
-            error = grad_two[at, :] + (part[at, :] + part_c[at, :])
+            error = grad_two[at, :] + (part[at, :] + part_c[at, :].astype(F32))
             grad = layer_norm_back(center, scale, vec[8:9, :], error)
             low = grad.astype(BF16)
             b_all[at, :] = low
@@ -850,8 +853,8 @@
             )
         return None
 
+    n_column.relay()
     j_copies = [attention_back(mask) for mask in grad_parts]
-    n_column.relay()
     attention_back(0)
     mixed_pass()
     n_column.hand_over(1)
@@ -895,7 +898,6 @@
             packed_two[number, row : row + lines, 3 * block : 4 * block] = across[at, :]
     input_line = Line(packed_two, right_two, left_two)
     input_line.first()
-    out_waits = go_back(out_half, out_got)
 
     g_column.hand_over(1)
     g_column.hand_over(3)
@@ -1168,9 +1170,10 @@
             pltpu.VMEM((slots, 128), jnp.int32),
             low(rows, 3 * D // 2),
             wide_f32(rows, D),
-            wide_f32(rows, D),
-            wide_f32(rows, D),
-            wide_f32(rows, D),
+            low(rows, D),
+            low(rows, D),
+            low(rows, D),
+            low(rows, D),
             wide_f32(half, D),
             wide_f32(rows, D),
             wide_f32(rows, D),

time: 111 us -> 108 us (0.973); the launches traced: 109 us -> 108 us
    pallas_call x1, Pallas kernels: 100 us -> 98.8 us  [slot_body(): pl.pallas_call(partial(slot_kernel, devices, depth, features), out_shape=...]
where the time goes in v8:
time: 108 us
  Pallas kernels  107 us (99%)
    pallas_call x1, Pallas kernels, slot_body(): pl.pallas_call(partial(slot_kernel, devices, depth, features), out_shape=...  98.8 us
    pallas_call x1, Pallas kernels, slot_body(): pl.pallas_call(partial(adam_kernel, count), out_shape=(jax.ShapeDtypeStru...  8.17 us

profile of v8, /device:TPU:0, one launch (start us, length us, event | category | flops | bytes accessed | tf_op | source)
XLA Modules:
  0.0 107.8 jit_solution(1290984644587811858)
XLA Ops:
  0.6 98.8 %slot.1 = (bf16[2,64,1024]{2,1,0:T(8,128)(2,1)}, bf16[2,64,1024]{2,1,0:T(8,128)(2,1)}, f32[32,3072]{1,0:T(8,128)}, f32[32,1024]{1,0:T(8,128)}, f32[32,4096]{1,0:...) custom-call(bf16[2,64,1024]{2,1,0:T(8,128)(2,1)} %refs_0_.1, bf16[2,64,1024]{2,1,0:T(8,128)(2,1)} %refs_1_.1, s32[2]{0:T(128)} %refs_2_.1, ...), custom_call_target="tpu_custom_call" | custom-call | tf_op jit(solution)/shard_map/slot/pallas_call | solution.py:1144
  99.4 8.2 %adam.1 = (bf16[2,64,1024]{2,1,0:T(8,128)(2,1)}, bf16[2,64,1024]{2,1,0:T(8,128)(2,1)}, f32[1,393600]{1,0:T(1,128)}, f32[1,393600]{1,0:T(1,128)}, f32[1,393600]{1,0:T(1,128)}, /*index=5*/f32[1,393600]{1,0:T(1,128)}) custom-call(f32[32,3072]{1,0:T(8,128)} %get-tuple-element.13.refs_0_, f32[32,1024]{1,0:T(8,128)} %get-tuple-element.14.refs_1_, ...), custom_call_target="tpu_custom_call" | custom-call | tf_op jit(solution)/shard_map/adam/pallas_call | solution.py:1218

commit v9 on v8

--- a/solution.py
+++ b/solution.py
@@ -1029,38 +1029,48 @@
     (
         g_qkv, g_out, g_in, g_fc2, g_vec, vec, out_in, tgrad_in, w_qkv, w_out, w_in, w_fc2, m_one, m_two,
         out_ref, tgrad_ref, rows_out, params_out, one_out, two_out,
-        grads, params, one, two, b_qkv, b_out, b_in, b_fc2, vec_flat, in_sems, w_sems, out_sems,
+        grads, params, one, two, d_qkv, d_out, d_in, d_fc2, b_qkv, b_out, b_in, b_fc2, out_by, tgrad_by, vec_flat,
+        in_sems, g_sems, w_sems, out_sems, pass_sems,
     ) = refs
     index = lax.axis_index("dp") * lax.axis_size("ctx") + lax.axis_index("ctx")
     size = m_one.shape[1] // 128
-    parts = in_sems.shape[1]
-    step = grads.shape[0] // parts
-    spans = [(number * step, min((number + 1) * step, size) - number * step) for number in range(parts)]
-    loads = []
-    for number, (start, length) in enumerate(spans):
-        pair = []
-        for kind, (source, target) in enumerate(((m_one, one), (m_two, two))):
-            pair.append(
-                pltpu.make_async_copy(
-                    source.reshape(size, 128).at[start : start + length],
-                    target.at[start : start + length],
-                    in_sems.at[kind, number],
-                )
+    kinds = (
+        (g_qkv, d_qkv, w_qkv, b_qkv),
+        (g_out, d_out, w_out, b_out),
+        (g_in, d_in, w_in, b_in),
+        (g_fc2, d_fc2, w_fc2, b_fc2),
+    )
+    lengths = [kind[1].shape[0] * kind[1].shape[1] // 128 for kind in kinds]
+    starts = [sum(lengths[:number]) for number in range(len(kinds))]
+    tail = sum(lengths)
+    order = (3, 2, 0, 1, 4)
+    spans = [(start, length) for start, length in zip(starts, lengths)] + [(tail, size - tail)]
+
+    def load(source, target, sem):
+        made = pltpu.make_async_copy(source, target, sem)
+        made.start()
+        return made
+
+    blocks, loads = {}, {}
+    for number in order:
+        start, length = spans[number]
+        if number < len(kinds):
+            grad, grad_by, weight, weight_by = kinds[number]
+            lines = weight_by.shape[0]
+            mine = pl.ds(pl.multiple_of(index * lines, lines), lines)
+            blocks[number] = [
+                load(grad, grad_by, g_sems.at[number]),
+                load(weight.at[mine, :], weight_by, w_sems.at[number]),
+            ]
+        loads[number] = [
+            load(
+                source.reshape(size, 128).at[start : start + length],
+                target.at[start : start + length],
+                in_sems.at[kind, number],
             )
-            pair[-1].start()
-        loads.append(pair)
-    weights = []
-    for number, (source, target) in enumerate(
-        ((w_qkv, b_qkv), (w_out, b_out), (w_in, b_in), (w_fc2, b_fc2))
-    ):
-        lines = target.shape[0]
-        start = pl.multiple_of(index * lines, lines)
-        weights.append(
-            pltpu.make_async_copy(source.at[pl.ds(start, lines), :], target, w_sems.at[number])
-        )
-        weights[-1].start()
-    out_ref[...] = out_in[...]
-    tgrad_ref[...] = tgrad_in[...]
+            for kind, (source, target) in enumerate(((m_one, one), (m_two, two)))
+        ]
+    passes = [load(out_in, out_by, pass_sems.at[0]), load(tgrad_in, tgrad_by, pass_sems.at[1])]
 
     def flatten(source, target, base):
         lines, groups = source.shape[0], source.shape[1] // 128
@@ -1069,57 +1079,70 @@
             for row in range(0, lines, 8):
                 target[pl.ds(base + row * groups + col, 8, stride=groups), :] = value[row : row + 8, :]
 
-    base = 0
-    for grad in (g_qkv, g_out, g_in, g_fc2):
-        flatten(grad, grads, base)
-        base += grad.shape[0] * grad.shape[1] // 128
-    share = g_vec.shape[1] // 128
-    groups = vec.shape[1] // 128
-    for col in range(groups):
-        lanes = slice(col * 128, (col + 1) * 128)
-        vec_flat[pl.ds(col, 8, stride=groups), :] = vec[0:8, lanes]
-        for row in range(8, vec.shape[0]):
-            vec_flat[row * groups + col : row * groups + col + 1, :] = vec[row : row + 1, lanes]
-    place = lax.broadcasted_iota(jnp.int32, vec_flat.shape, 0)
-    for number in range(share):
-        grads[base + number : base + number + 1, :] = g_vec[0:1, number * 128 : (number + 1) * 128]
-        params[base + number : base + number + 1, :] = jnp.sum(
-            jnp.where(place == index * share + number, vec_flat[...], 0.0), axis=0, keepdims=True
-        )
-    base = 0
-    for made, weight in zip(weights, (b_qkv, b_out, b_in, b_fc2)):
-        made.wait()
-        flatten(weight, params, base)
-        base += weight.shape[0] * weight.shape[1] // 128
+    def vector_rows():
+        share = g_vec.shape[1] // 128
+        groups = vec.shape[1] // 128
+        for col in range(groups):
+            lanes = slice(col * 128, (col + 1) * 128)
+            vec_flat[pl.ds(col, 8, stride=groups), :] = vec[0:8, lanes]
+            for row in range(8, vec.shape[0]):
+                vec_flat[row * groups + col : row * groups + col + 1, :] = vec[row : row + 1, lanes]
+        place = lax.broadcasted_iota(jnp.int32, vec_flat.shape, 0)
+        for number in range(share):
+            spot = slice(tail + number, tail + number + 1)
+            grads[spot, :] = g_vec[0:1, number * 128 : (number + 1) * 128]
+            params[spot, :] = jnp.sum(
+                jnp.where(place == index * share + number, vec_flat[...], 0.0), axis=0, keepdims=True
+            )
+
     fix_one = 1.0 / (1.0 - beta_one**step_count)
     fix_two = 1.0 / (1.0 - beta_two**step_count)
+
+    def update(at):
+        grad, param = grads[at, :], params[at, :]
+        new_one = beta_one * one[at, :] + (1.0 - beta_one) * grad
+        new_two = beta_two * two[at, :] + (1.0 - beta_two) * grad * grad
+        one[at, :] = new_one
+        two[at, :] = new_two
+        change = new_one * fix_one / (jnp.sqrt(new_two * fix_two) + adam_eps)
+        params[at, :] = param - learn_rate * (change + decay_rate * param)
+
+    vector_rows()
     copies = []
-    for number, (start, length) in enumerate(spans):
+    for number in order:
+        start, length = spans[number]
+        if number < len(kinds):
+            grad, grad_by, weight, weight_by = kinds[number]
+            for made in blocks[number]:
+                made.wait()
+            flatten(grad_by, grads, start)
+            flatten(weight_by, params, start)
         for made in loads[number]:
             made.wait()
-
-        @pl.loop(0, step // 56)
-        def _(chunk, start=start):
-            at = pl.ds(pl.multiple_of(start + chunk * 56, 8), 56)
-            grad, param = grads[at, :], params[at, :]
-            new_one = beta_one * one[at, :] + (1.0 - beta_one) * grad
-            new_two = beta_two * two[at, :] + (1.0 - beta_two) * grad * grad
-            one[at, :] = new_one
-            two[at, :] = new_two
-            change = new_one * fix_one / (jnp.sqrt(new_two * fix_two) + adam_eps)
-            params[at, :] = param - learn_rate * (change + decay_rate * param)
-
+        if number < len(kinds):
+
+            @pl.loop(0, length // 64)
+            def _(chunk, start=start):
+                update(pl.ds(pl.multiple_of(start + chunk * 64, 64), 64))
+
+        else:
+            update(slice(start, start + 8))
         for kind, (source, target) in enumerate(
             ((grads, rows_out), (params, params_out), (one, one_out), (two, two_out))
         ):
             copies.append(
-                pltpu.make_async_copy(
+                load(
                     source.at[start : start + length],
                     target.reshape(size, 128).at[start : start + length],
                     out_sems.at[kind, number],
                 )
             )
-            copies[-1].start()
+        if number == order[0]:
+            for made, source, target, sem in zip(
+                passes, (out_by, tgrad_by), (out_ref, tgrad_ref), (pass_sems.at[2], pass_sems.at[3])
+            ):
+                made.wait()
+                copies.append(load(source, target, sem))
     for made in copies:
         made.wait()
 
@@ -1213,7 +1236,7 @@
         name="slot",
     )(tokens, out_grad, lengths, vectors, w_qkv, w_out, w_in, w_fc2)
     size = moment_one.shape[1] // 128
-    padded = (size + 279) // 280 * 280
+    padded = (size + 7) // 8 * 8
     flat = jax.ShapeDtypeStruct(moment_one.shape, F32)
     return pl.pallas_call(
         partial(adam_kernel, count),
@@ -1225,18 +1248,26 @@
             flat,
             flat,
         ),
-        in_specs=[inside] * 8 + [anywhere] * 6,
-        out_specs=(inside, inside) + (anywhere,) * 4,
+        in_specs=[anywhere] * 4 + [inside] * 2 + [anywhere] * 8,
+        out_specs=(anywhere,) * 6,
         scratch_shapes=[wide_f32(padded, 128)] * 4
         + [
+            wide_f32(lines, 3 * D),
+            wide_f32(lines, D),
+            wide_f32(lines, features),
+            wide_f32(features // count, D),
             low(lines, 3 * D),
             low(lines, D),
             low(lines, features),
             low(features // count, D),
+            low(*tokens.shape),
+            low(*tokens.shape),
             wide_f32(vectors.shape[0] * D // 128, 128),
             pltpu.SemaphoreType.DMA((2, 5)),
             pltpu.SemaphoreType.DMA((4,)),
+            pltpu.SemaphoreType.DMA((4,)),
             pltpu.SemaphoreType.DMA((4, 5)),
+            pltpu.SemaphoreType.DMA((4,)),
         ],
         compiler_params=pltpu.CompilerParams(vmem_limit_bytes=64 * 1024 * 1024 - 64 * 1024),
         name="adam",

time: 108 us -> 107 us (level)
  no operation moved by 1% of the time
where the time goes in v9:
time: 107 us
  Pallas kernels  106 us (99%)
    pallas_call x1, Pallas kernels, slot_body(): pl.pallas_call(partial(slot_kernel, devices, depth, features), out_shape=...  98.8 us
    pallas_call x1, Pallas kernels, slot_body(): pl.pallas_call(partial(adam_kernel, count), out_shape=(jax.ShapeDtypeStru...  7.6 us

profile of v9, /device:TPU:0, one launch (start us, length us, event | category | flops | bytes accessed | tf_op | source)
XLA Modules:
  0.0 107.2 jit_solution(9505901522756581690)
XLA Ops:
  0.6 98.8 %slot.1 = (bf16[2,64,1024]{2,1,0:T(8,128)(2,1)}, bf16[2,64,1024]{2,1,0:T(8,128)(2,1)}, f32[32,3072]{1,0:T(8,128)}, f32[32,1024]{1,0:T(8,128)}, f32[32,4096]{1,0:...) custom-call(bf16[2,64,1024]{2,1,0:T(8,128)(2,1)} %refs_0_.1, bf16[2,64,1024]{2,1,0:T(8,128)(2,1)} %refs_1_.1, s32[2]{0:T(128)} %refs_2_.1, ...), custom_call_target="tpu_custom_call" | custom-call | tf_op jit(solution)/shard_map/slot/pallas_call | solution.py:1167
  99.4 7.6 %adam.1 = (bf16[2,64,1024]{2,1,0:T(8,128)(2,1)}, bf16[2,64,1024]{2,1,0:T(8,128)(2,1)}, f32[1,393600]{1,0:T(1,128)}, f32[1,393600]{1,0:T(1,128)}, f32[1,393600]{1,0:T(1,128)}, /*index=5*/f32[1,393600]{1,0:T(1,128)}) custom-call(f32[32,3072]{1,0:T(8,128)} %get-tuple-element.13.refs_0_, f32[32,1024]{1,0:T(8,128)} %get-tuple-element.14.refs_1_, ...), custom_call_target="tpu_custom_call" | custom-call | tf_op jit(solution)/shard_map/adam/pallas_call | solution.py:1241

commit v10 on v9

--- a/solution.py
+++ b/solution.py
@@ -884,6 +884,10 @@
 
     bias_sum = feed_rows(0)
     g_column.relay()
+    tg_waits = go_back(tg_half, tg_got)
+    for column in (n_column, g_column):
+        column.passes[2].wait_recv()
+    bias_sum = bias_sum + feed_rows(2)
     for made in m_passes + x_pass + j_copies:
         made.wait_recv()
     for group in range(devices):
@@ -901,7 +905,7 @@
 
     g_column.hand_over(1)
     g_column.hand_over(3)
-    for place in (2, 1, 3):
+    for place in (1, 3):
         n_column.passes[place].wait_recv()
         g_column.passes[place].wait_recv()
         bias_sum = bias_sum + feed_rows(place)
@@ -968,7 +972,6 @@
             for mask in range(1, devices)
         ]
 
-    tg_waits = go_back(tg_half, tg_got)
     for time in range(1, depth - 1):
         input_line.stage(time)
     low_sum = plane_sum(up_copies, slice(fine, 2 * fine)).astype(BF16)

time: 107 us -> 109 us (1.019)
  Pallas kernels: 106 us -> 108 us
    pallas_call x1, Pallas kernels: 98.8 us -> 101 us  [slot_body(): pl.pallas_call(partial(slot_kernel, devices, depth, features), out_shape=...]
where the time goes in v10:
time: 109 us
  Pallas kernels  108 us (99%)
    pallas_call x1, Pallas kernels, slot_body(): pl.pallas_call(partial(slot_kernel, devices, depth, features), out_shape=...  101 us
    pallas_call x1, Pallas kernels, slot_body(): pl.pallas_call(partial(adam_kernel, count), out_shape=(jax.ShapeDtypeStru...  7.6 us

profile of v10, /device:TPU:0, one launch (start us, length us, event | category | flops | bytes accessed | tf_op | source)
XLA Modules:
  0.0 109.0 jit_solution(18292768470104232599)
XLA Ops:
  0.6 100.6 %slot.1 = (bf16[2,64,1024]{2,1,0:T(8,128)(2,1)}, bf16[2,64,1024]{2,1,0:T(8,128)(2,1)}, f32[32,3072]{1,0:T(8,128)}, f32[32,1024]{1,0:T(8,128)}, f32[32,4096]{1,0:...) custom-call(bf16[2,64,1024]{2,1,0:T(8,128)(2,1)} %refs_0_.1, bf16[2,64,1024]{2,1,0:T(8,128)(2,1)} %refs_1_.1, s32[2]{0:T(128)} %refs_2_.1, ...), custom_call_target="tpu_custom_call" | custom-call | tf_op jit(solution)/shard_map/slot/pallas_call | solution.py:1170
  101.2 7.6 %adam.1 = (bf16[2,64,1024]{2,1,0:T(8,128)(2,1)}, bf16[2,64,1024]{2,1,0:T(8,128)(2,1)}, f32[1,393600]{1,0:T(1,128)}, f32[1,393600]{1,0:T(1,128)}, f32[1,393600]{1,0:T(1,128)}, /*index=5*/f32[1,393600]{1,0:T(1,128)}) custom-call(f32[32,3072]{1,0:T(8,128)} %get-tuple-element.13.refs_0_, f32[32,1024]{1,0:T(8,128)} %get-tuple-element.14.refs_1_, ...), custom_call_target="tpu_custom_call" | custom-call | tf_op jit(solution)/shard_map/adam/pallas_call | solution.py:1244

commit v11 on v10

--- a/solution.py
+++ b/solution.py
@@ -884,7 +884,6 @@
 
     bias_sum = feed_rows(0)
     g_column.relay()
-    tg_waits = go_back(tg_half, tg_got)
     for column in (n_column, g_column):
         column.passes[2].wait_recv()
     bias_sum = bias_sum + feed_rows(2)
@@ -972,6 +971,7 @@
             for mask in range(1, devices)
         ]
 
+    tg_waits = go_back(tg_half, tg_got)
     for time in range(1, depth - 1):
         input_line.stage(time)
     low_sum = plane_sum(up_copies, slice(fine, 2 * fine)).astype(BF16)

time: 109 us -> 109 us (level)
  no operation moved by 1% of the time
where the time goes in v11:
time: 109 us
  Pallas kernels  108 us (99%)
    pallas_call x1, Pallas kernels, slot_body(): pl.pallas_call(partial(slot_kernel, devices, depth, features), out_shape=...  101 us
    pallas_call x1, Pallas kernels, slot_body(): pl.pallas_call(partial(adam_kernel, count), out_shape=(jax.ShapeDtypeStru...  7.6 us

profile of v11, /device:TPU:0, one launch (start us, length us, event | category | flops | bytes accessed | tf_op | source)
XLA Modules:
  0.0 109.0 jit_solution(13973798685784285968)
XLA Ops:
  0.6 100.6 %slot.1 = (bf16[2,64,1024]{2,1,0:T(8,128)(2,1)}, bf16[2,64,1024]{2,1,0:T(8,128)(2,1)}, f32[32,3072]{1,0:T(8,128)}, f32[32,1024]{1,0:T(8,128)}, f32[32,4096]{1,0:...) custom-call(bf16[2,64,1024]{2,1,0:T(8,128)(2,1)} %refs_0_.1, bf16[2,64,1024]{2,1,0:T(8,128)(2,1)} %refs_1_.1, s32[2]{0:T(128)} %refs_2_.1, ...), custom_call_target="tpu_custom_call" | custom-call | tf_op jit(solution)/shard_map/slot/pallas_call | solution.py:1170
  101.2 7.6 %adam.1 = (bf16[2,64,1024]{2,1,0:T(8,128)(2,1)}, bf16[2,64,1024]{2,1,0:T(8,128)(2,1)}, f32[1,393600]{1,0:T(1,128)}, f32[1,393600]{1,0:T(1,128)}, f32[1,393600]{1,0:T(1,128)}, /*index=5*/f32[1,393600]{1,0:T(1,128)}) custom-call(f32[32,3072]{1,0:T(8,128)} %get-tuple-element.13.refs_0_, f32[32,1024]{1,0:T(8,128)} %get-tuple-element.14.refs_1_, ...), custom_call_target="tpu_custom_call" | custom-call | tf_op jit(solution)/shard_map/adam/pallas_call | solution.py:1244

commit v12 on v9

--- a/solution.py
+++ b/solution.py
@@ -566,13 +566,22 @@
             return self.target.at[at_rows(place * rows + core * half, half)]
 
         def relay(self):
-            self.parts[2].wait_recv()
+            self.inner = jnp.logical_or(slot == 1, slot == 2)
+            self.passes[2] = net.copy(self.spot(2), self.spot(2), peer)
+            net.open.append((self.passes[2], None))
+            pl.when(self.inner)(self.parts[2].wait_recv)
             up = net.forward(self.spot(2), self.spot(1), (me, depth - 1), self.numbers[1])
             down = net.forward(self.spot(2), self.spot(3), (me, 0), self.numbers[3])
             for made, here in ((up, slot == 2), (down, slot == 1)):
                 pl.when(here)(made.start)
                 net.open.append((made, here))
-            self.passes[2] = net.send(self.spot(2), self.spot(2), peer)
+            pl.when(self.inner)(self.passes[2].start)
+
+        def late(self):
+            @pl.when(jnp.logical_not(self.inner))
+            def _():
+                self.parts[2].wait_recv()
+                self.passes[2].start()
 
         def hand_over(self, place):
             self.parts[place].wait_recv()
@@ -857,6 +866,7 @@
     j_copies = [attention_back(mask) for mask in grad_parts]
     attention_back(0)
     mixed_pass()
+    n_column.late()
     n_column.hand_over(1)
     n_column.hand_over(3)
     for made in third:
@@ -899,6 +909,7 @@
     input_line = Line(packed_two, right_two, left_two)
     input_line.first()
 
+    g_column.late()
     g_column.hand_over(1)
     g_column.hand_over(3)
     for place in (2, 1, 3):

time: 107 us -> 107 us (level)
  no operation moved by 1% of the time
where the time goes in v12:
time: 107 us
  Pallas kernels  106 us (99%)
    pallas_call x1, Pallas kernels, slot_body(): pl.pallas_call(partial(slot_kernel, devices, depth, features), out_shape=...  98.8 us
    pallas_call x1, Pallas kernels, slot_body(): pl.pallas_call(partial(adam_kernel, count), out_shape=(jax.ShapeDtypeStru...  7.6 us

profile of v12, /device:TPU:0, one launch (start us, length us, event | category | flops | bytes accessed | tf_op | source)
XLA Modules:
  0.0 107.2 jit_solution(2504965179906240748)
XLA Ops:
  0.6 98.8 %slot.1 = (bf16[2,64,1024]{2,1,0:T(8,128)(2,1)}, bf16[2,64,1024]{2,1,0:T(8,128)(2,1)}, f32[32,3072]{1,0:T(8,128)}, f32[32,1024]{1,0:T(8,128)}, f32[32,4096]{1,0:...) custom-call(bf16[2,64,1024]{2,1,0:T(8,128)(2,1)} %refs_0_.1, bf16[2,64,1024]{2,1,0:T(8,128)(2,1)} %refs_1_.1, s32[2]{0:T(128)} %refs_2_.1, ...), custom_call_target="tpu_custom_call" | custom-call | tf_op jit(solution)/shard_map/slot/pallas_call | solution.py:1178
  99.4 7.6 %adam.1 = (bf16[2,64,1024]{2,1,0:T(8,128)(2,1)}, bf16[2,64,1024]{2,1,0:T(8,128)(2,1)}, f32[1,393600]{1,0:T(1,128)}, f32[1,393600]{1,0:T(1,128)}, f32[1,393600]{1,0:T(1,128)}, /*index=5*/f32[1,393600]{1,0:T(1,128)}) custom-call(f32[32,3072]{1,0:T(8,128)} %get-tuple-element.13.refs_0_, f32[32,1024]{1,0:T(8,128)} %get-tuple-element.14.refs_1_, ...), custom_call_target="tpu_custom_call" | custom-call | tf_op jit(solution)/shard_map/adam/pallas_call | solution.py:1252
